TPU v7x, 32 devices: a whole 2x2x4 slice. The times are simulated.
32 devices in a mesh: group: 2 (over y), mx: 4 (over x, core), my: 4 (over z).
Axes of the slice: x: 2, y: 2, z: 4, core: 2. Of those that a mesh axis runs over, the one named last changes fastest.
Arguments:
- teacher_feats: bfloat16 [256, 64, 6144], P(None, ('group', 'my'), 'mx'), parts along dimension 1, may hold values from -6 to 6
- t_gain: bfloat16 [6144], P('mx'), may hold values from 0.25 to 1.75
- t_bias: bfloat16 [6144], P('mx'), may hold values from -3 to 3
- projection: bfloat16 [6144, 1408], P('mx'), may hold values from -0.078125 to 0.078125
- student_in: bfloat16 [256, 64, 1408], P('mx', ('group', 'my')), parts along dimension 1, may hold values from -6 to 6
- s_gain: float32 [1408], replicated, may hold values from 0.25 to 1.75
- w_in: bfloat16 [1408, 6144], P('mx', 'my'), may hold values from -0.15625 to 0.15625
- w_out: bfloat16 [6144, 1408], P('my', 'mx'), may hold values from -0.078125 to 0.078125
Outputs:
- mse_loss: float32 [2], P('group'), parts along dimension 0
- grad_in: float32 [2816, 6144], P(('group', 'mx'), 'my'), parts along dimension 0
- grad_out: float32 [12288, 1408], P(('group', 'my'), 'mx'), parts along dimension 0
There are 2 independent parts, one for each index of `group`. A program takes and returns all parts, laid end to end along the dimension named above; an argument that names none is the same for every part. Nothing has to cross between parts.
All inputs are finite; a program needn't handle non-finite values.
Results may differ from a plain program's by a relative error of at most 0.011.
Values may be sent and summed in bfloat16 or wider, within the bound.
No kernel may reach another device: no remote copies, remote signals or barrier semaphores. Data moves between devices by JAX's collectives and lax.ppermute only.
A program may use at most 192 MiB of HBM per device.

v0:
```python
import jax
import jax.numpy as jnp
from jax import lax
from jax.sharding import PartitionSpec as P

DT = 6144
DS = 1408
PATCHES = 256


epsilon = 1e-06


def gelu_value(value):
    return 0.5 * value * (1.0 + lax.erf(value * 0.7071067811865476))


def gelu_slope(value):
    return (
        0.5 * (1.0 + lax.erf(value * 0.7071067811865476))
        + value * jnp.exp(-0.5 * value * value) * 0.3989422804014327
    )


def shards(teacher_feats, t_gain, t_bias, projection, student_in, s_gain, w_in, w_out):
    patch_all, image_loc, feat_loc = teacher_feats.shape
    mx_count = lax.axis_size("mx")
    my_count = lax.axis_size("my")
    patch_loc = patch_all // mx_count
    features = teacher_feats.astype(jnp.float32)
    feature_sum, squares = lax.psum(
        (jnp.sum(features, axis=2), jnp.sum(features * features, axis=2)), "mx"
    )
    row_mean = feature_sum / DT
    variance = squares / DT - row_mean * row_mean
    normed_teacher = (
        (features - row_mean[..., None])
        * lax.rsqrt(variance + epsilon)[..., None]
        * t_gain.astype(jnp.float32)
        + t_bias.astype(jnp.float32)
    ).astype(jnp.bfloat16)
    flattened = normed_teacher.reshape(patch_loc * lax.axis_size("mx") * image_loc, feat_loc)
    target = lax.psum_scatter(
        jnp.dot(flattened, projection, preferred_element_type=jnp.float32)
        .reshape(patch_loc * lax.axis_size("mx"), image_loc, DS)
        .astype(jnp.bfloat16),
        "mx",
        scatter_dimension=0,
        tiled=True,
    ).astype(jnp.float32)
    student_f32 = student_in.astype(jnp.float32)
    student_mean = jnp.sum(student_f32, axis=2, keepdims=True) / DS
    student_square = jnp.sum(student_f32 * student_f32, axis=2, keepdims=True) / DS
    normed = (
        (student_f32 - student_mean)
        * lax.rsqrt(student_square - student_mean * student_mean + epsilon)
        * s_gain
    ).astype(jnp.bfloat16)
    gathered = lax.all_gather(normed, "my", axis=1, tiled=True)
    rows_all = patch_loc * image_loc * my_count
    normed_flat = gathered.reshape(rows_all, DS)
    preact = jnp.dot(
        normed_flat,
        lax.all_gather(w_in, "mx", axis=0, tiled=True),
        preferred_element_type=jnp.float32,
    )
    activation = gelu_value(preact).astype(jnp.bfloat16)
    w_out_full = lax.all_gather(w_out, "mx", axis=1, tiled=True)
    branch_part = jnp.dot(activation, w_out_full, preferred_element_type=jnp.float32).reshape(
        patch_loc, image_loc * my_count, DS
    )
    branch = lax.psum_scatter(
        branch_part.astype(jnp.bfloat16), "my", scatter_dimension=1, tiled=True
    ).astype(jnp.float32)
    residue = student_f32 + branch - target
    tokens = PATCHES * image_loc * my_count
    squared_sum = lax.psum(jnp.sum(residue * residue), ("mx", "my"))
    mse_loss = jnp.reshape(squared_sum / (tokens * DS), (1,))
    grad_output = (residue / jnp.sqrt(jnp.float32(tokens))).astype(jnp.bfloat16)
    grad_rows = lax.all_gather(grad_output, "my", axis=1, tiled=True).reshape(rows_all, DS)
    grad_act = lax.dot_general(
        grad_rows, w_out_full, (((1,), (1,)), ((), ())), preferred_element_type=jnp.float32
    )
    grad_pre = (grad_act * gelu_slope(preact)).astype(jnp.bfloat16)
    part_in = lax.dot_general(
        normed_flat, grad_pre, (((0,), (0,)), ((), ())), preferred_element_type=jnp.float32
    )
    part_out = lax.dot_general(
        activation, grad_rows, (((0,), (0,)), ((), ())), preferred_element_type=jnp.float32
    )
    grad_in = lax.psum_scatter(
        part_in.astype(jnp.bfloat16), "mx", scatter_dimension=0, tiled=True
    ).astype(jnp.float32)
    grad_out = lax.psum_scatter(
        part_out.astype(jnp.bfloat16), "mx", scatter_dimension=1, tiled=True
    ).astype(jnp.float32)
    return (mse_loss, grad_in, grad_out)


def solution(mesh):
    in_specs = (
        P(None, ("group", "my"), "mx"),
        P("mx"),
        P("mx"),
        P("mx", None),
        P("mx", ("group", "my"), None),
        P(),
        P("mx", "my"),
        P("my", "mx"),
    )
    out_specs = (P("group"), P(("group", "mx"), "my"), P(("group", "my"), "mx"))
    return jax.shard_map(shards, mesh=mesh, in_specs=in_specs, out_specs=out_specs, check_vma=False)
```

profile of v0, /device:TPU:0, one launch (start us, length us, event | category | flops | bytes accessed | tf_op | source)
XLA Modules:
  0.0 622.6 jit_solution(18077358764981232624)
XLA Ops:
  7.2 1.9 convert_reduce_fusion.1
  9.2 3.0 fusion.24
  12.2 0.7 all-gather.7.cloned.1.call-update
  13.0 0.7 all-gather.9.cloned.1.call-update
  13.8 4.8 convert_reduce_fusion
  18.6 0.1 copy.34
  18.7 0.1 copy.36
  18.7 13.4 %all-reduce = (f32[256,8]{0,1:T(8,128)S(1)}, f32[256,8]{0,1:T(8,128)S(1)}) all-reduce(f32[256,8]{0,1:T(8,128)S(1)} %copy.36, f32[256,8]{0,1:T(8,128)S(1)} %copy.34), channel_id=1, replica_groups=mesh['group'=2,'mx'=4,'my'=4] {'mx'}, use_global_device_ids=true, to_apply=%region_6.0 | all-reduce | flops 4096 | bytes 32768 | tf_op jit(solution)/shard_map/psum | solution.py:31
  32.2 0.1 copy.35
  32.3 0.1 copy.37
  32.4 5.0 fusion.3
  37.4 18.9 %fusion.18 = bf16[256,8,1408]{2,0,1:T(8,128)(2,1)} fusion(bf16[256,8,1536]{2,1,0:T(8,128)(2,1)S(1)} %fusion.3, bf16[1536,1408]{1,0:T(8,128)(2,1)} %param.11), kind=kOutput, calls=%fused_computation.26 | convolution fusion | flops 8861253632 | bytes 16384000 | tf_op jit(solution)/shard_map/dot_general | solution.py:44
  56.4 0.6 reduce-scatter.5.cloned.1.call-start
  56.9 64.8 %all-gather.5.cloned.1.call-done = bf16[64,32,1408]{2,0,1:T(8,128)(2,1)} async-done(((bf16[64,8,1408]{2,0,1:T(8,128)(2,1)}), bf16[64,32,1408]{2,0,1:T(8,128)(2,1)}) %all-gather.5.cloned.1.call-update) | async-done | bytes 5767184 | tf_op jit(solution)/shard_map/all_gather | solution.py:59
  121.8 8.5 %copy.32 = bf16[64,32,1408]{2,1,0:T(8,128)(2,1)} copy(bf16[64,32,1408]{2,0,1:T(8,128)(2,1)} %all-gather.5.cloned.1.call-done) | data formatting | bytes 11534336 | tf_op jit(solution)/shard_map/all_gather | solution.py:59
  130.3 26.6 %all-gather.7.cloned.1.call-done = bf16[1408,1536]{1,0:T(8,128)(2,1)} async-done(((bf16[352,1536]{1,0:T(8,128)(2,1)}), bf16[1408,1536]{1,0:T(8,128)(2,1)}) %all-gather.7.cloned.1.call-update) | async-done | bytes 4325392 | tf_op jit(solution)/shard_map/all_gather | solution.py:64
  156.9 17.3 %multiply_convert_fusion = (bf16[2048,1536]{1,0:T(8,128)(2,1)}, f32[2048,1536]{1,0:T(8,128)}) fusion(bf16[2048,1408]{1,0:T(8,128)(2,1)} %bitcast.16, bf16[1408,1536]{1,0:T(8,128)(2,1)} %all-gather.7.cloned.1.call-done), kind=kOutput, calls=%fused_computation.15 | convolution fusion | flops 8874098688 | bytes 28966912 | tf_op jit(solution)/shard_map/dot_general | solution.py:62
  174.2 19.5 %all-gather.9.cloned.1.call-done = bf16[1536,1408]{0,1:T(8,128)(2,1)} async-done(((bf16[1536,352]{0,1:T(8,128)(2,1)}), bf16[1536,1408]{0,1:T(8,128)(2,1)}) %all-gather.9.cloned.1.call-update) | async-done | bytes 4325392 | tf_op jit(solution)/shard_map/all_gather | solution.py:68
  193.7 13.3 %convolution_convert_fusion = bf16[2048,1408]{1,0:T(8,128)(2,1)S(1)} fusion(bf16[2048,1536]{1,0:T(8,128)(2,1)} %get-tuple-element.15, bf16[1536,1408]{0,1:T(8,128)(2,1)} %all-gather.9.cloned.1.call-done), kind=kOutput, calls=%fused_computation.18 | convolution fusion | flops 8861253632 | bytes 16384000 | tf_op jit(solution)/shard_map/dot_general | solution.py:69
  207.0 4.4 copy.33
  211.5 0.0 all-gather.11.cloned.1.call-start
  211.5 39.5 %reduce-scatter.7.cloned.1.call-done = bf16[64,8,1408]{2,0,1:T(8,128)(2,1)} async-done(((bf16[256,8,1408]{2,0,1:T(8,128)(2,1)}), bf16[64,8,1408]{2,0,1:T(8,128)(2,1)}) %reduce-scatter.7.cloned.1.call-update) | async-done | bytes 1441808 | tf_op jit(solution)/shard_map/reduce_scatter | solution.py:43
  251.0 104.5 %reduce-scatter.5.cloned.1.call-done = bf16[64,8,1408]{2,0,1:T(8,128)(2,1)} async-done(((bf16[64,32,1408]{2,0,1:T(8,128)(2,1)}), bf16[64,8,1408]{2,0,1:T(8,128)(2,1)}) %reduce-scatter.5.cloned.1.call-update) | async-done | bytes 1441808 | tf_op jit(solution)/shard_map/reduce_scatter | solution.py:72
  355.5 4.2 multiply_convert_fusion.1
  359.8 107.3 %all-gather.11.cloned.1.call-done = bf16[64,32,1408]{2,0,1:T(8,128)(2,1)} async-done(((bf16[64,8,1408]{2,0,1:T(8,128)(2,1)}), bf16[64,32,1408]{2,0,1:T(8,128)(2,1)}) %all-gather.11.cloned.1.call-update) | async-done | bytes 5767184 | tf_op jit(solution)/shard_map/all_gather | solution.py:80
  467.2 8.4 %copy.39 = bf16[64,32,1408]{2,1,0:T(8,128)(2,1)} copy(bf16[64,32,1408]{2,0,1:T(8,128)(2,1)} %all-gather.11.cloned.1.call-done) | data formatting | bytes 11534336 | tf_op jit(solution)/shard_map/all_gather | solution.py:80
  475.6 43.9 %fusion.12 = bf16[1408,1536]{1,0:T(8,128)(2,1)} fusion(bf16[2048,1408]{1,0:T(8,128)(2,1)} %bitcast.17, f32[2048,1536]{1,0:T(8,128)} %get-tuple-element.16, bf16[2048,1408]{1,0:T(8,128)(2,1)} %bitcast.18, bf16[1536,1408]{0,1:T(8,128)(2,1)} %all-gather.9.cloned.1.call-done), kind=kOutput, calls=%fused_computation.20 | convolution fusion | flops 17750360064 | bytes 32768000 | tf_op jit(solution)/shard_map/dot_general | solution.py:85
  519.6 14.4 %convolution_convert_fusion.1 = bf16[1536,1408]{0,1:T(8,128)(2,1)} fusion(bf16[2048,1536]{1,0:T(8,128)(2,1)} %get-tuple-element.15, bf16[2048,1408]{1,0:T(8,128)(2,1)} %bitcast.19), kind=kOutput, calls=%fused_computation.19 | convolution fusion | flops 8860532736 | bytes 16384000 | tf_op jit(solution)/shard_map/dot_general | solution.py:88
  534.1 32.2 %psum.23 = f32[]{:T(128)} all-reduce(f32[]{:T(128)} %get-tuple-element.10), channel_id=1, replica_groups=mesh['group'=2,'mx'=4,'my'=4] {'mx','my'}, use_global_device_ids=true, to_apply=%region_9.0 | all-reduce | flops 1 | bytes 8 | tf_op jit(solution)/shard_map/psum | solution.py:77
  566.9 2.8 convert_element_type.69
  569.8 41.8 %reduce-scatter.11.cloned.1.call-done = bf16[1536,352]{0,1:T(8,128)(2,1)} async-done(((bf16[1536,1408]{0,1:T(8,128)(2,1)}), bf16[1536,352]{0,1:T(8,128)(2,1)}) %reduce-scatter.11.cloned.1.call-update) | async-done | bytes 1081360 | tf_op jit(solution)/shard_map/reduce_scatter | solution.py:94
  611.5 2.8 convert_element_type.71
  (23 shorter events, 0.4 us)
Async XLA Ops:
  7.2 6.6 %copy-start.1 = (bf16[1536]{0:T(1024)(128)(2,1)S(1)}, bf16[1536]{0:T(1024)(128)(2,1)}, u32[]{:S(2)}) copy-start(bf16[1536]{0:T(1024)(128)(2,1)} %param.9) | copy-start | bytes 9220
  7.2 6.6 %copy-start.2 = (bf16[1536]{0:T(1024)(128)(2,1)S(1)}, bf16[1536]{0:T(1024)(128)(2,1)}, u32[]{:S(2)}) copy-start(bf16[1536]{0:T(1024)(128)(2,1)} %param.10) | copy-start | bytes 9220
  7.2 114.6 %all-gather.5.cloned.1.call-start = ((), (), s32[]{:S(2)}) async-start(), calls=%async_computation.4 | async-start | bytes 7208960 | tf_op jit(solution)/shard_map/all_gather | solution.py:59
  12.2 144.7 %all-gather.7.cloned.1.call-start = ((), (), s32[]{:S(2)}) async-start(), calls=%async_computation.5 | async-start | bytes 5406720 | tf_op jit(solution)/shard_map/all_gather | solution.py:64
  13.0 180.8 %all-gather.9.cloned.1.call-start = ((), (), s32[]{:S(2)}) async-start(), calls=%async_computation.6 | async-start | bytes 5406720 | tf_op jit(solution)/shard_map/all_gather | solution.py:68
  13.7 237.3 %reduce-scatter.7.cloned.1.call-start = ((), (), s32[]{:S(2)}) async-start(), calls=%async_computation.8 | async-start | bytes 7208960 | tf_op jit(solution)/shard_map/reduce_scatter | solution.py:43
  56.4 299.2 %reduce-scatter.5.cloned.1.call-start = ((), (), s32[]{:S(2)}) async-start(), calls=%async_computation.7 | async-start | bytes 7208960 | tf_op jit(solution)/shard_map/reduce_scatter | solution.py:72
  211.5 144.1 %copy-start = (bf16[64,8,1408]{2,1,0:T(8,128)(2,1)S(1)}, bf16[64,8,1408]{2,1,0:T(8,128)(2,1)}, u32[]{:S(2)}) copy-start(bf16[64,8,1408]{2,1,0:T(8,128)(2,1)} %param.12) | copy-start | bytes 4325380
  211.5 255.7 %all-gather.11.cloned.1.call-start = ((), (), s32[]{:S(2)}) async-start(), calls=%async_computation.9 | async-start | bytes 7208960 | tf_op jit(solution)/shard_map/all_gather | solution.py:80
  359.8 207.1 %reduce-scatter.9.cloned.1.call-start = ((), (), s32[]{:S(2)}) async-start(), calls=%async_computation.10 | async-start | bytes 5406720 | tf_op jit(solution)/shard_map/reduce_scatter | solution.py:91
  519.5 92.0 %reduce-scatter.11.cloned.1.call-start = ((), (), s32[]{:S(2)}) async-start(), calls=%async_computation.11 | async-start | bytes 5406720 | tf_op jit(solution)/shard_map/reduce_scatter | solution.py:94
Sparse Core Ops, SparseCore 0:
  12.3 109.3 all-gather.4
  123.3 33.5 all-gather.6
  158.4 35.2 all-gather.8
  196.1 54.8 reduce-scatter.6
  253.2 102.2 reduce-scatter.4
  359.9 107.2 all-gather.10
  519.7 43.8 reduce-scatter.8
  566.1 45.3 reduce-scatter.10
where the time goes:
time: 626 us; the launch traced here: 623 us
  waiting for transfers between devices  406 us (65%)
  matrix products  108 us (17%)
  blocking collectives  45.6 us (7%)
  other arithmetic  24.7 us (4%)
  local copies, waits for them, and re-layouts  21.7 us (3%)
  between operations  16.3 us (3%)
    all_gather x1, waiting for transfers between devices, shards(): lax.all_gather(grad_output, 'my', axis=1, tiled=True).reshape(rows_all, DS)  107 us
    reduce_scatter x1, waiting for transfers between devices, shards(): lax.psum_scatter(branch_part.astype(jnp.bfloat16), 'my', scatter_dimensio...  105 us
    all_gather x1, waiting for transfers between devices, shards(): gathered = lax.all_gather(normed, 'my', axis=1, tiled=True)  64.8 us
    dot_general x1, matrix products, shards(): lax.dot_general(normed_flat, grad_pre, (((0,), (0,)), ((), ())), preferre...  43.9 us
    reduce_scatter x1, waiting for transfers between devices, shards(): lax.psum_scatter(part_out.astype(jnp.bfloat16), 'mx', scatter_dimension=1...  41.8 us
    reduce_scatter x1, waiting for transfers between devices, shards(): lax.psum_scatter(jnp.dot(flattened, projection, preferred_element_type=jn...  39.5 us
    psum x1, blocking collectives, shards(): squared_sum = lax.psum(jnp.sum(residue * residue), ('mx', 'my'))  32.2 us
    all_gather x1, waiting for transfers between devices, shards(): lax.all_gather(w_in, 'mx', axis=0, tiled=True)  26.6 us
  transfers between devices with their start and end apart: 8, of which 7 were waited for; matrix products, arithmetic and copies ran while one was open for 14% of the time, Pallas kernels for 0%

commit v1 on v0

--- a/solution.py
+++ b/solution.py
@@ -1,12 +1,15 @@
 import jax
 import jax.numpy as jnp
 from jax import lax
+from jax.experimental import pallas as pl
+from jax.experimental.pallas import tpu as pltpu
 from jax.sharding import PartitionSpec as P
 
 DT = 6144
 DS = 1408
 PATCHES = 256
-
+F32 = jnp.float32
+BF16 = jnp.bfloat16
 
 epsilon = 1e-06
 
@@ -20,6 +23,167 @@
         0.5 * (1.0 + lax.erf(value * 0.7071067811865476))
         + value * jnp.exp(-0.5 * value * value) * 0.3989422804014327
     )
+
+
+def swap(value, axis, bit):
+    count = lax.axis_size(axis)
+    return lax.ppermute(value, axis, [(i, i ^ bit) for i in range(count)])
+
+
+def assemble_body(offs_ref, *refs):
+    pieces, out, sems = refs[:-2], refs[-2], refs[-1]
+    copies = []
+    for i, piece in enumerate(pieces):
+        off = pl.multiple_of(offs_ref[i], 16)
+        copies.append(
+            pltpu.make_async_copy(piece, out.at[pl.ds(off, piece.shape[0]), :], sems.at[i])
+        )
+    for copy in copies:
+        copy.start()
+    for copy in copies:
+        copy.wait()
+
+
+def assemble(pieces, offsets):
+    cols = pieces[0].shape[1]
+    rows = sum(p.shape[0] for p in pieces)
+    offs = jnp.stack([jnp.asarray(o, jnp.int32) for o in offsets])
+    return pl.pallas_call(
+        assemble_body,
+        out_shape=jax.ShapeDtypeStruct((rows, cols), pieces[0].dtype),
+        in_specs=[pl.BlockSpec(memory_space=pltpu.SMEM)]
+        + [pl.BlockSpec(memory_space=pl.ANY)] * len(pieces),
+        out_specs=pl.BlockSpec(memory_space=pltpu.VMEM),
+        scratch_shapes=[pltpu.SemaphoreType.DMA((len(pieces),))],
+        cost_estimate=pl.CostEstimate(flops=0, transcendentals=0, bytes_accessed=4 * rows * cols),
+    )(offs, *pieces)
+
+
+def fetch_weight(piece, mx, g):
+    rows, cols = piece.shape
+    half = rows // 2
+    mine, other = g * half, (1 - g) * half
+    own_half = lax.dynamic_slice(piece, (mine, 0), (half, cols))
+    x_g = swap(own_half, "mx", 2)
+    z_g = swap(own_half, "my", 2)
+    x_o = swap(x_g, "group", 1)
+    z_o = swap(z_g, "group", 1)
+    d_g = swap(z_g, "mx", 2)
+    d_o = swap(d_g, "group", 1)
+    c_own = swap(piece, "mx", 1)
+    near = [(piece, mx * rows), (c_own, (mx ^ 1) * rows)]
+    far = []
+    for part, block, off, to in (
+        (x_g, 2, mine, near),
+        (x_o, 2, other, near),
+        (z_g, 0, mine, far),
+        (z_o, 0, other, far),
+        (d_g, 2, mine, far),
+        (d_o, 2, other, far),
+    ):
+        to.append((part, (mx ^ block) * rows + off))
+        to.append((swap(part, "mx", 1), (mx ^ block ^ 1) * rows + off))
+    return tuple(assemble([p for p, _ in grp], [o for _, o in grp]) for grp in (near, far))
+
+
+def pair_shards(teacher_feats, t_gain, t_bias, projection, student_in, s_gain, w_in, w_out):
+    mx = lax.axis_index("mx")
+    g = lax.axis_index("group")
+    patch_all, image_loc, feat_loc = teacher_feats.shape
+    patch_loc = patch_all // 4
+    toks = patch_loc * image_loc
+    tokens = PATCHES * image_loc * 4
+
+    student_f32 = student_in.reshape(toks, DS).astype(F32)
+    student_mean = jnp.sum(student_f32, axis=1, keepdims=True) / DS
+    student_square = jnp.sum(student_f32 * student_f32, axis=1, keepdims=True) / DS
+    normed_own = (
+        (student_f32 - student_mean)
+        * lax.rsqrt(student_square - student_mean * student_mean + epsilon)
+        * s_gain
+    ).astype(BF16)
+    normed = jnp.concatenate([normed_own, swap(normed_own, "my", 1)], axis=0)
+
+    in_near, in_far = fetch_weight(w_in, mx, g)
+    out_near, out_far = fetch_weight(w_out.T, mx, g)
+
+    features = teacher_feats.astype(F32)
+    stats = jnp.stack([jnp.sum(features, axis=2), jnp.sum(features * features, axis=2)])
+    stats = stats + swap(stats, "mx", 1)
+    stats = stats + swap(stats, "mx", 2)
+    row_mean = stats[0] / DT
+    rstd = lax.rsqrt(stats[1] / DT - row_mean * row_mean + epsilon)
+
+    def target_part(block):
+        start = (mx ^ block) * patch_loc
+        feats = lax.dynamic_slice_in_dim(teacher_feats, start, patch_loc, 0).astype(F32)
+        mean = lax.dynamic_slice_in_dim(row_mean, start, patch_loc, 0)
+        scale = lax.dynamic_slice_in_dim(rstd, start, patch_loc, 0)
+        tnorm = (
+            (feats - mean[..., None]) * scale[..., None] * t_gain.astype(F32) + t_bias.astype(F32)
+        ).astype(BF16)
+        return jnp.dot(
+            tnorm.reshape(toks, feat_loc), projection, preferred_element_type=F32
+        ).astype(BF16)
+
+    q3 = target_part(3)
+    q1 = target_part(1)
+    q2 = target_part(2)
+    q0 = target_part(0)
+    t2 = (q2.astype(F32) + swap(q3, "mx", 1).astype(F32)).astype(BF16)
+    t0 = q0.astype(F32) + swap(q1, "mx", 1).astype(F32)
+    target = t0 + swap(t2, "mx", 2).astype(F32)
+
+    def forward(weight):
+        preact = jnp.dot(normed, weight, preferred_element_type=F32)
+        return gelu_value(preact).astype(BF16), gelu_slope(preact)
+
+    act_near, slope_near = forward(in_near)
+    act_far, slope_far = forward(in_far)
+
+    def nt(left, right):
+        return lax.dot_general(left, right, (((1,), (1,)), ((), ())), preferred_element_type=F32)
+
+    branch_pair = (nt(act_near[toks:], out_near) + nt(act_far[toks:], out_far)).astype(BF16)
+    branch_recv = swap(branch_pair, "my", 1)
+    branch_own = (nt(act_near[:toks], out_near) + nt(act_far[:toks], out_far)).astype(BF16)
+
+    residue = student_f32 + (branch_own.astype(F32) + branch_recv.astype(F32)) - target
+    grad_own = (residue / jnp.sqrt(jnp.float32(tokens))).astype(BF16)
+    grad = jnp.concatenate([grad_own, swap(grad_own, "my", 1)], axis=0)
+    loss = jnp.broadcast_to(jnp.sum(residue * residue), (8, 128))
+    for axis, bit in (("my", 1), ("my", 2), ("mx", 1), ("mx", 2)):
+        loss = loss + swap(loss, axis, bit)
+    mse_loss = loss[0, :1] / (tokens * DS)
+
+    def tn(left, right):
+        return lax.dot_general(
+            left, right, (((0,), (0,)), ((), ())), preferred_element_type=F32
+        ).astype(BF16)
+
+    def reduce_mx(part):
+        rows = part.shape[0] // 4
+        blocks = [
+            lax.dynamic_slice_in_dim(part, (mx ^ k) * rows, rows, 0) for k in range(4)
+        ]
+        s2 = (blocks[2].astype(F32) + swap(blocks[3], "mx", 1).astype(F32)).astype(BF16)
+        s0 = blocks[0].astype(F32) + swap(blocks[1], "mx", 1).astype(F32)
+        return s0 + swap(s2, "mx", 2).astype(F32)
+
+    def backward(weight_out, slope, act):
+        part_out = tn(grad, act)
+        grad_act = jnp.dot(grad, weight_out, preferred_element_type=F32)
+        grad_pre = (grad_act * slope).astype(BF16)
+        part_in = tn(normed, grad_pre)
+        return reduce_mx(part_out), reduce_mx(part_in)
+
+    far_out, far_in = backward(out_far, slope_far, act_far)
+    far_out = swap(far_out.astype(BF16), "my", 2)
+    far_in = swap(far_in.astype(BF16), "my", 2)
+    near_out, near_in = backward(out_near, slope_near, act_near)
+    grad_in = near_in + far_in.astype(F32)
+    grad_out = (near_out + far_out.astype(F32)).T
+    return (mse_loss, grad_in, grad_out)
 
 
 def shards(teacher_feats, t_gain, t_bias, projection, student_in, s_gain, w_in, w_out):
@@ -109,4 +273,6 @@
         P("my", "mx"),
     )
     out_specs = (P("group"), P(("group", "mx"), "my"), P(("group", "my"), "mx"))
-    return jax.shard_map(shards, mesh=mesh, in_specs=in_specs, out_specs=out_specs, check_vma=False)
+    pairs = mesh.shape["group"] == 2 and mesh.shape["mx"] == 4 and mesh.shape["my"] == 4
+    body = pair_shards if pairs else shards
+    return jax.shard_map(body, mesh=mesh, in_specs=in_specs, out_specs=out_specs, check_vma=False)

time: 626 us -> 450 us (0.72)
  waiting for transfers between devices: 406 us -> 220 us
  blocking collectives: 45.6 us -> 0 us
  starting transfers between devices: 0.85 us -> 40.3 us
  Pallas kernels: 0 us -> 19.9 us
  between operations: 16.3 us -> 3.47 us
    ppermute x0 -> x52, waiting for transfers between devices: none -> 220 us  [swap(): return lax.ppermute(value, axis, [(i, i ^ bit) for i in range(count)])]
    all_gather x4 -> x0, waiting for transfers between devices: 218 us -> none  [the longest x1 107 us: shards(): lax.all_gather(grad_output, 'my', axis=1, tiled=True).reshape(rows_all, DS)]
    reduce_scatter x4 -> x0, waiting for transfers between devices: 186 us -> none  [the longest x1 105 us: shards(): lax.psum_scatter(branch_part.astype(jnp.bfloat16), 'my', scatter_dimensio...]
    psum x2 -> x0, blocking collectives: 45.6 us -> none  [the longest x1 32.2 us: shards(): squared_sum = lax.psum(jnp.sum(residue * residue), ('mx', 'my'))]
    ppermute x0 -> x52, starting transfers between devices: none -> 40.3 us  [swap(): return lax.ppermute(value, axis, [(i, i ^ bit) for i in range(count)])]
    pallas_call x0 -> x4, Pallas kernels: none -> 19.9 us  [assemble(): pl.pallas_call(assemble_body, out_shape=jax.ShapeDtypeStruct((rows, cols)...]
    all_gather x2 -> x0, local copies, waits for them, and re-layouts: 16.9 us -> none  [the longest x1 8.51 us: shards(): gathered = lax.all_gather(normed, 'my', axis=1, tiled=True)]
    dynamic_slice x0 -> x15, local copies, waits for them, and re-layouts: none -> 12 us  [the longest x4 7.45 us: reduce_mx(): lax.dynamic_slice_in_dim(part, (mx ^ k) * rows, rows, 0)]
  transfers between devices with their start and end apart: 8 -> 52, of which waited for: 7 -> 18; matrix products, arithmetic and copies ran while one was open for 14% -> 30% of each run, Pallas kernels for 0% -> 5%
where the time goes in v1:
time: 450 us; the launch traced here: 441 us
  waiting for transfers between devices  220 us (49%)
  matrix products  114 us (25%)
  starting transfers between devices  40.3 us (9%)
  local copies, waits for them, and re-layouts  21.8 us (5%)
  other arithmetic  21.3 us (5%)
  Pallas kernels  19.9 us (4%)
    ppermute x52, waiting for transfers between devices, swap(): return lax.ppermute(value, axis, [(i, i ^ bit) for i in range(count)])  220 us
    dot_general x4, matrix products, tn(): lax.dot_general(left, right, (((0,), (0,)), ((), ())), preferred_element_...  49.3 us
    ppermute x52, starting transfers between devices, swap(): return lax.ppermute(value, axis, [(i, i ^ bit) for i in range(count)])  40.3 us
    dot_general x4, matrix products, target_part(): jnp.dot(tnorm.reshape(toks, feat_loc), projection, preferred_element_type...  25.4 us
    dot_general x2, matrix products, forward(): preact = jnp.dot(normed, weight, preferred_element_type=F32)  20.5 us
    pallas_call x4, Pallas kernels, assemble(): pl.pallas_call(assemble_body, out_shape=jax.ShapeDtypeStruct((rows, cols)...  19.9 us
    dot_general x4, matrix products, nt(): lax.dot_general(left, right, (((1,), (1,)), ((), ())), preferred_element_...  19.1 us
  transfers between devices with their start and end apart: 52, of which 18 were waited for; matrix products, arithmetic and copies ran while one was open for 30% of the time, Pallas kernels for 5%

profile of v1, /device:TPU:0, one launch (start us, length us, event | category | flops | bytes accessed | tf_op | source)
XLA Modules:
  0.0 441.5 jit_solution(657805863390147055)
XLA Ops:
  2.5 4.0 collective-permute-start.11
  10.5 4.8 %convert_reduce_fusion = (f32[256,8]{1,0:T(8,128)S(1)}, f32[256,8]{1,0:T(8,128)S(1)}) fusion(bf16[256,8,1536]{2,1,0:T(8,128)(2,1)} %param.8), kind=kLoop, calls=%fused_computation.1 | loop fusion | flops 12578816 | bytes 6307840 | tf_op jit(solution)/shard_map/reduce_sum | solution.py:111
  18.7 13.7 %collective-permute-done.29 = f32[2,256,8]{1,2,0:T(8,128)S(1)} collective-permute-done((f32[2,256,8]{1,2,0:T(8,128)S(1)}, f32[2,256,8]{1,2,0:T(8,128)S(1)}, u32[]{:S(2)}, u32[]{:S(2)}) %collective-permute-start.29) | collective-permute-done | bytes 16416 | tf_op jit(solution)/shard_map/ppermute | solution.py:30
  32.7 6.6 %convolution_convert_fusion.4 = bf16[512,1408]{1,0:T(8,128)(2,1)} fusion(bf16[1536,1408]{1,0:T(8,128)(2,1)} %param.11, f32[64,8]{1,0:T(8,128)S(1)} %copy.28, f32[64,8]{1,0:T(8,128)S(1)} %copy.27, bf16[256,8,1536]{2,1,0:T(8,128)(2,1)} %param.8, s32[]{:T(128)S(6)} %select_n.22, f32[1536]{0:T(1024)S(1)} %convert_element_type.218, ...), kind=kOutput, calls=%fused_computation.41 | convolution fusion | flops 2220032000 | bytes 7356420 | tf_op jit(solution)/shard_map/dot_general | solution.py:125
  45.2 8.5 %collective-permute-done.19.refs_0_ = bf16[176,1536]{1,0:T(8,128)(2,1)S(1)} collective-permute-done((bf16[176,1536]{1,0:T(8,128)(2,1)}, bf16[176,1536]{1,0:T(8,128)(2,1)S(1)}, u32[]{:S(2)}, u32[]{:S(2)}) %collective-permute-start.19) | collective-permute-done | bytes 540704 | tf_op jit(solution)/shard_map/ppermute | solution.py:30
  57.0 12.9 %collective-permute-done.4.refs_4_ = bf16[176,1536]{1,0:T(8,128)(2,1)} collective-permute-done((bf16[176,1536]{1,0:T(8,128)(2,1)}, bf16[176,1536]{1,0:T(8,128)(2,1)}, u32[]{:S(2)}, u32[]{:S(2)}) %collective-permute-start.4) | collective-permute-done | bytes 540704 | tf_op jit(solution)/shard_map/ppermute | solution.py:30
  71.9 6.5 %convolution_convert_fusion.6 = bf16[512,1408]{1,0:T(8,128)(2,1)} fusion(bf16[1536,1408]{1,0:T(8,128)(2,1)} %param.11, f32[64,8]{1,0:T(8,128)S(1)} %copy.24, f32[64,8]{1,0:T(8,128)S(1)} %copy.23, bf16[256,8,1536]{2,1,0:T(8,128)(2,1)} %param.8, s32[]{:T(128)S(6)} %select_n.20, f32[1536]{0:T(1024)S(1)} %convert_element_type.218, ...), kind=kOutput, calls=%fused_computation.44 | convolution fusion | flops 2220032000 | bytes 7356420 | tf_op jit(solution)/shard_map/dot_general | solution.py:125
  80.6 6.9 %add_convert_fusion.4 = bf16[512,1408]{1,0:T(8,128)(2,1)} fusion(bf16[512,1408]{1,0:T(8,128)(2,1)} %collective-permute-done.31, bf16[1536,1408]{1,0:T(8,128)(2,1)} %param.11, f32[64,8]{1,0:T(8,128)S(1)} %copy.26, f32[64,8]{1,0:T(8,128)S(1)} %copy.25, bf16[256,8,1536]{2,1,0:T(8,128)(2,1)} %param.8, s32[]{:T(128)S(6)} %select_n.21, ...), kind=kOutput, calls=%fused_computation.55 | convolution fusion | flops 2222915584 | bytes 8798212 | tf_op jit(solution)/shard_map/dot_general | solution.py:125
  87.5 4.9 %shard_map.104 = bf16[1408,1536]{1,0:T(8,128)(2,1)} custom-call(s32[6]{0:T(128)} %stack.71.offs_ref, bf16[352,1536]{1,0:T(8,128)(2,1)} %bitcast.84, bf16[352,1536]{1,0:T(8,128)(2,1)} %collective-permute-done.6.refs_1_, bf16[176,1536]{1,0:T(8,128)(2,1)} %collective-permute-done.7.refs_2_, bf16[176,1536]{1,0:T(8,128)(2,1)} %collective-permute-done.8.refs_3_, ...), custom_call_target="tpu_custom_call" | custom-call | bytes 8650752 | tf_op jit(solution)/shard_map/pallas_call | solution.py:51
  94.6 5.1 %shard_map.103 = bf16[1408,1536]{1,0:T(8,128)(2,1)} custom-call(s32[6]{0:T(128)} %stack.71.offs_ref, bf16[352,1536]{1,0:T(8,128)(2,1)} %refs_0_.1, bf16[352,1536]{1,0:T(8,128)(2,1)} %collective-permute-done.1.refs_1_, bf16[176,1536]{1,0:T(8,128)(2,1)} %collective-permute-done.2.refs_2_, bf16[176,1536]{1,0:T(8,128)(2,1)} %collective-permute-done.3.refs_3_, ...), custom_call_target="tpu_custom_call" | custom-call | bytes 8650752 | tf_op jit(solution)/shard_map/pallas_call | solution.py:51
  105.1 10.2 %multiply_convert_fusion.1 = (bf16[1024,1536]{1,0:T(8,128)(2,1)S(1)}, f32[1024,1536]{1,0:T(8,128)}) fusion(bf16[1408,1536]{1,0:T(8,128)(2,1)} %shard_map.103, bf16[512,1408]{1,0:T(8,128)(2,1)} %collective-permute-done, bf16[512,1408]{1,0:T(8,128)(2,1)} %fusion.24), kind=kOutput, calls=%fused_computation.23 | convolution fusion | flops 4442816512 | bytes 16646144 | tf_op jit(solution)/shard_map/dot_general | solution.py:138
  116.3 14.7 %collective-permute-done.17.refs_6_ = bf16[176,1536]{1,0:T(8,128)(2,1)S(1)} collective-permute-done((bf16[176,1536]{1,0:T(8,128)(2,1)S(1)}, bf16[176,1536]{1,0:T(8,128)(2,1)S(1)}, u32[]{:S(2)}, u32[]{:S(2)}) %collective-permute-start.17) | collective-permute-done | bytes 540704 | tf_op jit(solution)/shard_map/ppermute | solution.py:30
  131.0 4.2 fusion.37
  136.4 5.7 %collective-permute-done.25.refs_6_ = bf16[176,1536]{1,0:T(8,128)(2,1)} collective-permute-done((bf16[176,1536]{1,0:T(8,128)(2,1)}, bf16[176,1536]{1,0:T(8,128)(2,1)}, u32[]{:S(2)}, u32[]{:S(2)}) %collective-permute-start.25) | collective-permute-done | bytes 540704 | tf_op jit(solution)/shard_map/ppermute | solution.py:30
  143.4 5.0 %shard_map.105 = bf16[1408,1536]{1,0:T(8,128)(2,1)} custom-call(s32[8]{0:T(128)} %stack.76.offs_ref, bf16[176,1536]{1,0:T(8,128)(2,1)} %collective-permute-done.11.refs_0_, bf16[176,1536]{1,0:T(8,128)(2,1)} %collective-permute-done.12.refs_1_, bf16[176,1536]{1,0:T(8,128)(2,1)} %collective-permute-done.13.refs_2_, bf16[176,1536]{1,0:T(8,128)(2,1)} %copy-done.11, ...), custom_call_target="tpu_custom_call" | custom-call | bytes 8650752 | tf_op jit(solution)/shard_map/pallas_call | solution.py:51
  148.4 10.3 %multiply_convert_fusion = (bf16[1024,1536]{1,0:T(8,128)(2,1)}, f32[1024,1536]{1,0:T(8,128)}) fusion(bf16[1408,1536]{1,0:T(8,128)(2,1)} %shard_map.105, bf16[512,1408]{1,0:T(8,128)(2,1)} %collective-permute-done, bf16[512,1408]{1,0:T(8,128)(2,1)} %fusion.24), kind=kOutput, calls=%fused_computation.21 | convolution fusion | flops 4442816512 | bytes 16646144 | tf_op jit(solution)/shard_map/dot_general | solution.py:138
  159.9 5.0 %shard_map.106 = bf16[1408,1536]{1,0:T(8,128)(2,1)} custom-call(s32[8]{0:T(128)} %stack.76.offs_ref, bf16[176,1536]{1,0:T(8,128)(2,1)} %copy-done.7, bf16[176,1536]{1,0:T(8,128)(2,1)} %copy-done.12, bf16[176,1536]{1,0:T(8,128)(2,1)} %collective-permute-done.21.refs_2_, bf16[176,1536]{1,0:T(8,128)(2,1)} %collective-permute-done.22.refs_3_, ...), custom_call_target="tpu_custom_call" | custom-call | bytes 8650752 | tf_op jit(solution)/shard_map/pallas_call | solution.py:51
  164.9 6.3 %fusion.19 = bf16[512,1408]{1,0:T(8,128)(2,1)S(1)} fusion(f32[512,1408]{1,0:T(8,128)} %fusion.37, bf16[1408,1536]{1,0:T(8,128)(2,1)} %shard_map.106, bf16[1024,1536]{1,0:T(8,128)(2,1)} %get-tuple-element.29), kind=kOutput, calls=%fused_computation.40 | convolution fusion | flops 2216034304 | bytes 10223616 | tf_op jit(solution)/shard_map/dot_general | solution.py:145
  173.4 5.5 %fusion.21 = f32[512,1408]{1,0:T(8,128)S(1)} fusion(bf16[1536,1408]{1,0:T(8,128)(2,1)} %param.11, f32[1536]{0:T(1024)S(1)} %convert_element_type.218, f32[1536]{0:T(1024)S(1)} %convert_element_type.217, f32[64,8]{1,0:T(8,128)S(1)} %copy.22, f32[64,8]{1,0:T(8,128)S(1)} %copy.21, bf16[256,8,1536]{2,1,0:T(8,128)(2,1)} %param.8, s32[]{:T(128)S(6)} %select_n.19), kind=kOutput, calls=%fused_computation.46 | convolution fusion | flops 2220752896 | bytes 8798212 | tf_op jit(solution)/shard_map/dot_general | solution.py:125
  181.6 10.9 %collective-permute-done.32 = bf16[512,1408]{1,0:T(8,128)(2,1)} collective-permute-done((bf16[512,1408]{1,0:T(8,128)(2,1)}, bf16[512,1408]{1,0:T(8,128)(2,1)}, u32[]{:S(2)}, u32[]{:S(2)}) %collective-permute-start.32) | collective-permute-done | bytes 1441824 | tf_op jit(solution)/shard_map/ppermute | solution.py:30
  192.6 12.3 %collective-permute-done.27 = bf16[512,1408]{1,0:T(8,128)(2,1)} collective-permute-done((bf16[512,1408]{1,0:T(8,128)(2,1)S(1)}, bf16[512,1408]{1,0:T(8,128)(2,1)}, u32[]{:S(2)}, u32[]{:S(2)}) %collective-permute-start.27) | collective-permute-done | bytes 1441824 | tf_op jit(solution)/shard_map/ppermute | solution.py:30
  204.9 6.0 %multiply_convert_fusion.2 = (bf16[512,1408]{1,0:T(8,128)(2,1)S(1)}, f32[]{:T(128)}) fusion(bf16[512,1408]{1,0:T(8,128)(2,1)} %collective-permute-done.32, f32[512,1408]{1,0:T(8,128)S(1)} %fusion.21, bf16[512,1408]{1,0:T(8,128)(2,1)} %collective-permute-done.30, bf16[512,1408]{1,0:T(8,128)(2,1)} %collective-permute-done.27, f32[512,1408]{1,0:T(8,128)S(1)} %fusion.40, ...), kind=kOutput, calls=%fused_computation.53 | convolution fusion | flops 2226126848 | bytes 18874372 | tf_op jit(solution)/shard_map/dot_general | solution.py:145
  213.7 30.1 %collective-permute-done.33 = f32[8,128]{1,0:T(8,128)S(1)} collective-permute-done((f32[8,128]{1,0:T(8,128)S(1)}, f32[8,128]{1,0:T(8,128)S(1)}, u32[]{:S(2)}, u32[]{:S(2)}) %collective-permute-start.33) | collective-permute-done | bytes 4128 | tf_op jit(solution)/shard_map/ppermute | solution.py:30
  250.9 7.0 %convolution_convert_fusion = bf16[1408,1536]{1,0:T(8,128)(2,1)S(1)} fusion(bf16[1024,1536]{1,0:T(8,128)(2,1)} %get-tuple-element.29, bf16[512,1408]{1,0:T(8,128)(2,1)} %collective-permute-done.37, bf16[512,1408]{1,0:T(8,128)(2,1)S(1)} %get-tuple-element.15), kind=kOutput, calls=%fused_computation.5 | convolution fusion | flops 4437114880 | bytes 10354688 | tf_op jit(solution)/shard_map/dot_general | solution.py:160
  262.1 6.6 %convolution_convert_fusion.1 = bf16[1408,1536]{1,0:T(8,128)(2,1)S(1)} fusion(bf16[1024,1536]{1,0:T(8,128)(2,1)S(1)} %copy-done.22, bf16[512,1408]{1,0:T(8,128)(2,1)} %collective-permute-done.37, bf16[512,1408]{1,0:T(8,128)(2,1)S(1)} %get-tuple-element.15), kind=kOutput, calls=%fused_computation.6 | convolution fusion | flops 4437114880 | bytes 10354688 | tf_op jit(solution)/shard_map/dot_general | solution.py:160
  272.0 17.8 %convolution_convert_fusion.2 = bf16[1408,1536]{1,0:T(8,128)(2,1)} fusion(f32[1024,1536]{1,0:T(8,128)} %get-tuple-element.30, bf16[1408,1536]{1,0:T(8,128)(2,1)} %shard_map.106, bf16[512,1408]{1,0:T(8,128)(2,1)} %collective-permute-done.37, bf16[512,1408]{1,0:T(8,128)(2,1)} %copy-done.18, bf16[512,1408]{1,0:T(8,128)(2,1)} %collective-permute-done, ...), kind=kOutput, calls=%fused_computation.7 | convolution fusion | flops 8887795712 | bytes 20709376 | tf_op jit(solution)/shard_map/dot_general | solution.py:160
  293.3 18.0 %convolution_convert_fusion.3 = bf16[1408,1536]{1,0:T(8,128)(2,1)} fusion(f32[1024,1536]{1,0:T(8,128)} %get-tuple-element.28, bf16[1408,1536]{1,0:T(8,128)(2,1)} %shard_map.104, bf16[512,1408]{1,0:T(8,128)(2,1)} %collective-permute-done.37, bf16[512,1408]{1,0:T(8,128)(2,1)} %copy-done.18, bf16[512,1408]{1,0:T(8,128)(2,1)} %collective-permute-done, ...), kind=kOutput, calls=%fused_computation.8 | convolution fusion | flops 8887795712 | bytes 20709376 | tf_op jit(solution)/shard_map/dot_general | solution.py:160
  322.1 17.8 %collective-permute-done.50 = bf16[352,1536]{1,0:T(8,128)(2,1)S(1)} collective-permute-done((bf16[352,1536]{1,0:T(8,128)(2,1)S(1)}, bf16[352,1536]{1,0:T(8,128)(2,1)S(1)}, u32[]{:S(2)}, u32[]{:S(2)}) %collective-permute-start.50) | collective-permute-done | bytes 1081376 | tf_op jit(solution)/shard_map/ppermute | solution.py:30
  346.9 16.3 %collective-permute-done.43 = bf16[352,1536]{1,0:T(8,128)(2,1)S(1)} collective-permute-done((bf16[352,1536]{1,0:T(8,128)(2,1)S(1)}, bf16[352,1536]{1,0:T(8,128)(2,1)S(1)}, u32[]{:S(2)}, u32[]{:S(2)}) %collective-permute-start.43) | collective-permute-done | bytes 1081376 | tf_op jit(solution)/shard_map/ppermute | solution.py:30
  364.8 20.9 %collective-permute-done.36 = f32[8,128]{1,0:T(8,128)S(1)} collective-permute-done((f32[8,128]{1,0:T(8,128)S(1)}, f32[8,128]{1,0:T(8,128)S(1)}, u32[]{:S(2)}, u32[]{:S(2)}) %collective-permute-start.36) | collective-permute-done | bytes 4128 | tf_op jit(solution)/shard_map/ppermute | solution.py:30
  390.8 25.1 %collective-permute-done.51 = bf16[352,1536]{1,0:T(8,128)(2,1)S(1)} collective-permute-done((bf16[352,1536]{1,0:T(8,128)(2,1)S(1)}, bf16[352,1536]{1,0:T(8,128)(2,1)S(1)}, u32[]{:S(2)}, u32[]{:S(2)}) %collective-permute-start.51) | collective-permute-done | bytes 1081376 | tf_op jit(solution)/shard_map/ppermute | solution.py:30
  417.7 20.3 %collective-permute-done.44 = bf16[352,1536]{1,0:T(8,128)(2,1)S(1)} collective-permute-done((bf16[352,1536]{1,0:T(8,128)(2,1)S(1)}, bf16[352,1536]{1,0:T(8,128)(2,1)S(1)}, u32[]{:S(2)}, u32[]{:S(2)}) %collective-permute-start.44) | collective-permute-done | bytes 1081376 | tf_op jit(solution)/shard_map/ppermute | solution.py:30
  (202 shorter events, 88.1 us)
Async XLA Ops:
  2.5 40.6 %collective-permute-start.11 = (bf16[176,1536]{1,0:T(8,128)(2,1)}, bf16[176,1536]{1,0:T(8,128)(2,1)}, u32[]{:S(2)}, u32[]{:S(2)}) collective-permute-start(bf16[176,1536]{1,0:T(8,128)(2,1)} %constant_dynamic-slice_fusion.16), channel_id=1, source_target_pairs={{0,2},{1,3},{2,0},{3,1},{4,6},{5,7},{6,4},{7,5},{8,10},{9,11},{10,... | collective-permute-start | bytes 1622024 | tf_op jit(solution)/shard_map/ppermute | solution.py:30
  6.5 38.5 %collective-permute-start.2 = (bf16[176,1536]{1,0:T(8,128)(2,1)}, bf16[176,1536]{1,0:T(8,128)(2,1)}, u32[]{:S(2)}, u32[]{:S(2)}) collective-permute-start(bf16[176,1536]{1,0:T(8,128)(2,1)} %constant_dynamic-slice_fusion.16), channel_id=1, source_target_pairs={{0,8},{4,12},{8,0},{12,4},{1,9},{5,13},{9,1},{13,5},{2,10},{6,14},... | collective-permute-start | bytes 1622024 | tf_op jit(solution)/shard_map/ppermute | solution.py:30
  9.9 43.9 %collective-permute-start.19 = (bf16[176,1536]{1,0:T(8,128)(2,1)}, bf16[176,1536]{1,0:T(8,128)(2,1)S(1)}, u32[]{:S(2)}, u32[]{:S(2)}) collective-permute-start(bf16[176,1536]{1,0:T(8,128)(2,1)} %dynamic-slice_bitcast_fusion), channel_id=1, source_target_pairs={{0,2},{1,3},{2,0},{3,1},{4,6},{5,7},{6,4},{7,5},{8,10},{9,11},{10,... | collective-permute-start | bytes 1622024 | tf_op jit(solution)/shard_map/ppermute | solution.py:30
  10.3 32.9 %collective-permute-start.7 = (bf16[176,1536]{1,0:T(8,128)(2,1)}, bf16[176,1536]{1,0:T(8,128)(2,1)}, u32[]{:S(2)}, u32[]{:S(2)}) collective-permute-start(bf16[176,1536]{1,0:T(8,128)(2,1)} %dynamic-slice_bitcast_fusion), channel_id=1, source_target_pairs={{0,8},{4,12},{8,0},{12,4},{1,9},{5,13},{9,1},{13,5},{2,10},{6,14},... | collective-permute-start | bytes 1622024 | tf_op jit(solution)/shard_map/ppermute | solution.py:30
  39.3 39.5 %collective-permute-start.31 = (bf16[512,1408]{1,0:T(8,128)(2,1)}, bf16[512,1408]{1,0:T(8,128)(2,1)}, u32[]{:S(2)}, u32[]{:S(2)}) collective-permute-start(bf16[512,1408]{1,0:T(8,128)(2,1)} %convolution_convert_fusion.4), channel_id=1, source_target_pairs={{0,4},{4,0},{8,12},{12,8},{1,5},{5,1},{9,13},{13,9},{2,6},{6,2},{1... | collective-permute-start | bytes 4325384 | tf_op jit(solution)/shard_map/ppermute | solution.py:30
  43.1 35.4 %collective-permute-start.6 = (bf16[352,1536]{1,0:T(8,128)(2,1)S(1)}, bf16[352,1536]{1,0:T(8,128)(2,1)}, u32[]{:S(2)}, u32[]{:S(2)}) collective-permute-start(bf16[352,1536]{1,0:T(8,128)(2,1)S(1)} %bitcast.85), channel_id=1, source_target_pairs={{0,4},{4,0},{8,12},{12,8},{1,5},{5,1},{9,13},{13,9},{2,6},{6,2},{1... | collective-permute-start | bytes 3244040 | tf_op jit(solution)/shard_map/ppermute | solution.py:30
  43.1 28.2 %collective-permute-start.9 = (bf16[176,1536]{1,0:T(8,128)(2,1)}, bf16[176,1536]{1,0:T(8,128)(2,1)}, u32[]{:S(2)}, u32[]{:S(2)}) collective-permute-start(bf16[176,1536]{1,0:T(8,128)(2,1)} %collective-permute-done.7.refs_2_), channel_id=1, source_target_pairs={{0,16},{16,0},{1,17},{17,1},{2,18},{18,2},{3,19},{19,3},{4,20},{20... | collective-permute-start | bytes 1622024 | tf_op jit(solution)/shard_map/ppermute | solution.py:30
  45.1 26.4 %collective-permute-start.8 = (bf16[176,1536]{1,0:T(8,128)(2,1)}, bf16[176,1536]{1,0:T(8,128)(2,1)}, u32[]{:S(2)}, u32[]{:S(2)}) collective-permute-start(bf16[176,1536]{1,0:T(8,128)(2,1)} %collective-permute-done.7.refs_2_), channel_id=1, source_target_pairs={{0,4},{4,0},{8,12},{12,8},{1,5},{5,1},{9,13},{13,9},{2,6},{6,2},{1... | collective-permute-start | bytes 1622024 | tf_op jit(solution)/shard_map/ppermute | solution.py:30
  69.9 33.6 %collective-permute-start = (bf16[512,1408]{1,0:T(8,128)(2,1)}, bf16[512,1408]{1,0:T(8,128)(2,1)}, u32[]{:S(2)}, u32[]{:S(2)}) collective-permute-start(bf16[512,1408]{1,0:T(8,128)(2,1)} %fusion.24), channel_id=1, source_target_pairs={{0,1},{1,0},{2,3},{3,2},{4,5},{5,4},{6,7},{7,6},{8,9},{9,8},{10,11... | collective-permute-start | bytes 4325384 | tf_op jit(solution)/shard_map/ppermute | solution.py:30
  99.8 35.4 %collective-permute-start.21 = (bf16[176,1536]{1,0:T(8,128)(2,1)S(1)}, bf16[176,1536]{1,0:T(8,128)(2,1)}, u32[]{:S(2)}, u32[]{:S(2)}) collective-permute-start(bf16[176,1536]{1,0:T(8,128)(2,1)S(1)} %collective-permute-done.19.refs_0_), channel_id=1, source_target_pairs={{0,16},{16,0},{1,17},{17,1},{2,18},{18,2},{3,19},{19,3},{4,20},{20... | collective-permute-start | bytes 1622024 | tf_op jit(solution)/shard_map/ppermute | solution.py:30
  103.5 27.5 %collective-permute-start.17 = (bf16[176,1536]{1,0:T(8,128)(2,1)S(1)}, bf16[176,1536]{1,0:T(8,128)(2,1)S(1)}, u32[]{:S(2)}, u32[]{:S(2)}) collective-permute-start(bf16[176,1536]{1,0:T(8,128)(2,1)S(1)} %collective-permute-done.15.refs_4_), channel_id=1, source_target_pairs={{0,16},{16,0},{1,17},{17,1},{2,18},{18,2},{3,19},{19,3},{4,20},{20... | collective-permute-start | bytes 1622024 | tf_op jit(solution)/shard_map/ppermute | solution.py:30
  115.9 26.2 %collective-permute-start.25 = (bf16[176,1536]{1,0:T(8,128)(2,1)}, bf16[176,1536]{1,0:T(8,128)(2,1)}, u32[]{:S(2)}, u32[]{:S(2)}) collective-permute-start(bf16[176,1536]{1,0:T(8,128)(2,1)} %collective-permute-done.23.refs_4_), channel_id=1, source_target_pairs={{0,16},{16,0},{1,17},{17,1},{2,18},{18,2},{3,19},{19,3},{4,20},{20... | collective-permute-start | bytes 1622024 | tf_op jit(solution)/shard_map/ppermute | solution.py:30
  135.2 46.4 %collective-permute-start.30 = (bf16[512,1408]{1,0:T(8,128)(2,1)}, bf16[512,1408]{1,0:T(8,128)(2,1)}, u32[]{:S(2)}, u32[]{:S(2)}) collective-permute-start(bf16[512,1408]{1,0:T(8,128)(2,1)} %convolution_convert_fusion.6), channel_id=1, source_target_pairs={{0,4},{4,0},{8,12},{12,8},{1,5},{5,1},{9,13},{13,9},{2,6},{6,2},{1... | collective-permute-start | bytes 4325384 | tf_op jit(solution)/shard_map/ppermute | solution.py:30
  158.7 33.9 %collective-permute-start.32 = (bf16[512,1408]{1,0:T(8,128)(2,1)}, bf16[512,1408]{1,0:T(8,128)(2,1)}, u32[]{:S(2)}, u32[]{:S(2)}) collective-permute-start(bf16[512,1408]{1,0:T(8,128)(2,1)} %add_convert_fusion.4), channel_id=1, source_target_pairs={{0,8},{4,12},{8,0},{12,4},{1,9},{5,13},{9,1},{13,5},{2,10},{6,14},... | collective-permute-start | bytes 4325384 | tf_op jit(solution)/shard_map/ppermute | solution.py:30
  171.2 33.8 %collective-permute-start.27 = (bf16[512,1408]{1,0:T(8,128)(2,1)S(1)}, bf16[512,1408]{1,0:T(8,128)(2,1)}, u32[]{:S(2)}, u32[]{:S(2)}) collective-permute-start(bf16[512,1408]{1,0:T(8,128)(2,1)S(1)} %fusion.19), channel_id=1, source_target_pairs={{0,1},{1,0},{2,3},{3,2},{4,5},{5,4},{6,7},{7,6},{8,9},{9,8},{10,11... | collective-permute-start | bytes 4325384 | tf_op jit(solution)/shard_map/ppermute | solution.py:30
  210.9 40.0 %collective-permute-start.37 = (bf16[512,1408]{1,0:T(8,128)(2,1)S(1)}, bf16[512,1408]{1,0:T(8,128)(2,1)}, u32[]{:S(2)}, u32[]{:S(2)}) collective-permute-start(bf16[512,1408]{1,0:T(8,128)(2,1)S(1)} %get-tuple-element.15), channel_id=1, source_target_pairs={{0,1},{1,0},{2,3},{3,2},{4,5},{5,4},{6,7},{7,6},{8,9},{9,8},{10,11... | collective-permute-start | bytes 4325384 | tf_op jit(solution)/shard_map/ppermute | solution.py:30
  213.3 30.5 %collective-permute-start.33 = (f32[8,128]{1,0:T(8,128)S(1)}, f32[8,128]{1,0:T(8,128)S(1)}, u32[]{:S(2)}, u32[]{:S(2)}) collective-permute-start(f32[8,128]{1,0:T(8,128)S(1)} %broadcast_in_dim.2), channel_id=1, source_target_pairs={{0,1},{1,0},{2,3},{3,2},{4,5},{5,4},{6,7},{7,6},{8,9},{9,8},{10,11... | collective-permute-start | bytes 12296 | tf_op jit(solution)/shard_map/ppermute | solution.py:30
  259.5 61.7 %collective-permute-start.48 = (bf16[352,1536]{1,0:T(8,128)(2,1)}, bf16[352,1536]{1,0:T(8,128)(2,1)S(1)}, u32[]{:S(2)}, u32[]{:S(2)}) collective-permute-start(bf16[352,1536]{1,0:T(8,128)(2,1)} %get-tuple-element.9), channel_id=1, source_target_pairs={{0,4},{4,0},{8,12},{12,8},{1,5},{5,1},{9,13},{13,9},{2,6},{6,2},{1... | collective-permute-start | bytes 3244040 | tf_op jit(solution)/shard_map/ppermute | solution.py:30
  261.2 50.1 %collective-permute-start.49 = (bf16[352,1536]{1,0:T(8,128)(2,1)}, bf16[352,1536]{1,0:T(8,128)(2,1)}, u32[]{:S(2)}, u32[]{:S(2)}) collective-permute-start(bf16[352,1536]{1,0:T(8,128)(2,1)} %get-tuple-element.10), channel_id=1, source_target_pairs={{0,4},{4,0},{8,12},{12,8},{1,5},{5,1},{9,13},{13,9},{2,6},{6,2},{1... | collective-permute-start | bytes 3244040 | tf_op jit(solution)/shard_map/ppermute | solution.py:30
  271.8 47.3 %collective-permute-start.46 = (bf16[352,1536]{1,0:T(8,128)(2,1)}, bf16[352,1536]{1,0:T(8,128)(2,1)}, u32[]{:S(2)}, u32[]{:S(2)}) collective-permute-start(bf16[352,1536]{1,0:T(8,128)(2,1)} %get-tuple-element.8), channel_id=1, source_target_pairs={{0,4},{4,0},{8,12},{12,8},{1,5},{5,1},{9,13},{13,9},{2,6},{6,2},{1... | collective-permute-start | bytes 3244040 | tf_op jit(solution)/shard_map/ppermute | solution.py:30
  292.9 23.7 %collective-permute-start.42 = (bf16[352,1536]{1,0:T(8,128)(2,1)}, bf16[352,1536]{1,0:T(8,128)(2,1)}, u32[]{:S(2)}, u32[]{:S(2)}) collective-permute-start(bf16[352,1536]{1,0:T(8,128)(2,1)} %get-tuple-element.14), channel_id=1, source_target_pairs={{0,4},{4,0},{8,12},{12,8},{1,5},{5,1},{9,13},{13,9},{2,6},{6,2},{1... | collective-permute-start | bytes 3244040 | tf_op jit(solution)/shard_map/ppermute | solution.py:30
  313.2 26.8 %collective-permute-start.50 = (bf16[352,1536]{1,0:T(8,128)(2,1)S(1)}, bf16[352,1536]{1,0:T(8,128)(2,1)S(1)}, u32[]{:S(2)}, u32[]{:S(2)}) collective-permute-start(bf16[352,1536]{1,0:T(8,128)(2,1)S(1)} %add_convert_fusion.6), channel_id=1, source_target_pairs={{0,8},{4,12},{8,0},{12,4},{1,9},{5,13},{9,1},{13,5},{2,10},{6,14},... | collective-permute-start | bytes 3244040 | tf_op jit(solution)/shard_map/ppermute | solution.py:30
  316.5 27.0 %collective-permute-start.39 = (bf16[352,1536]{1,0:T(8,128)(2,1)S(1)}, bf16[352,1536]{1,0:T(8,128)(2,1)S(1)}, u32[]{:S(2)}, u32[]{:S(2)}) collective-permute-start(bf16[352,1536]{1,0:T(8,128)(2,1)S(1)} %get-tuple-element.12), channel_id=1, source_target_pairs={{0,4},{4,0},{8,12},{12,8},{1,5},{5,1},{9,13},{13,9},{2,6},{6,2},{1... | collective-permute-start | bytes 3244040 | tf_op jit(solution)/shard_map/ppermute | solution.py:30
  316.6 29.6 %collective-permute-start.41 = (bf16[352,1536]{1,0:T(8,128)(2,1)S(1)}, bf16[352,1536]{1,0:T(8,128)(2,1)S(1)}, u32[]{:S(2)}, u32[]{:S(2)}) collective-permute-start(bf16[352,1536]{1,0:T(8,128)(2,1)S(1)} %copy-done.6), channel_id=1, source_target_pairs={{0,4},{4,0},{8,12},{12,8},{1,5},{5,1},{9,13},{13,9},{2,6},{6,2},{1... | collective-permute-start | bytes 3244040 | tf_op jit(solution)/shard_map/ppermute | solution.py:30
  319.1 44.1 %collective-permute-start.43 = (bf16[352,1536]{1,0:T(8,128)(2,1)S(1)}, bf16[352,1536]{1,0:T(8,128)(2,1)S(1)}, u32[]{:S(2)}, u32[]{:S(2)}) collective-permute-start(bf16[352,1536]{1,0:T(8,128)(2,1)S(1)} %add_convert_fusion.9), channel_id=1, source_target_pairs={{0,8},{4,12},{8,0},{12,4},{1,9},{5,13},{9,1},{13,5},{2,10},{6,14},... | collective-permute-start | bytes 3244040 | tf_op jit(solution)/shard_map/ppermute | solution.py:30
  322.1 65.0 %collective-permute-start.45 = (bf16[352,1536]{1,0:T(8,128)(2,1)S(1)}, bf16[352,1536]{1,0:T(8,128)(2,1)S(1)}, u32[]{:S(2)}, u32[]{:S(2)}) collective-permute-start(bf16[352,1536]{1,0:T(8,128)(2,1)S(1)} %get-tuple-element.7), channel_id=1, source_target_pairs={{0,4},{4,0},{8,12},{12,8},{1,5},{5,1},{9,13},{13,9},{2,6},{6,2},{1... | collective-permute-start | bytes 3244040 | tf_op jit(solution)/shard_map/ppermute | solution.py:30
  340.0 50.8 %collective-permute-start.47 = (bf16[352,1536]{1,0:T(8,128)(2,1)S(1)}, bf16[352,1536]{1,0:T(8,128)(2,1)S(1)}, u32[]{:S(2)}, u32[]{:S(2)}) collective-permute-start(bf16[352,1536]{1,0:T(8,128)(2,1)S(1)} %add_convert_fusion.7), channel_id=1, source_target_pairs={{0,8},{4,12},{8,0},{12,4},{1,9},{5,13},{9,1},{13,5},{2,10},{6,14},... | collective-permute-start | bytes 3244040 | tf_op jit(solution)/shard_map/ppermute | solution.py:30
  343.5 72.4 %collective-permute-start.51 = (bf16[352,1536]{1,0:T(8,128)(2,1)S(1)}, bf16[352,1536]{1,0:T(8,128)(2,1)S(1)}, u32[]{:S(2)}, u32[]{:S(2)}) collective-permute-start(bf16[352,1536]{1,0:T(8,128)(2,1)S(1)} %add_convert_fusion.5), channel_id=1, source_target_pairs={{0,2},{1,3},{2,0},{3,1},{4,6},{5,7},{6,4},{7,5},{8,10},{9,11},{10,... | collective-permute-start | bytes 3244040 | tf_op jit(solution)/shard_map/ppermute | solution.py:30
  346.3 39.4 %collective-permute-start.36 = (f32[8,128]{1,0:T(8,128)S(1)}, f32[8,128]{1,0:T(8,128)S(1)}, u32[]{:S(2)}, u32[]{:S(2)}) collective-permute-start(f32[8,128]{1,0:T(8,128)S(1)} %add.265), channel_id=1, source_target_pairs={{0,8},{4,12},{8,0},{12,4},{1,9},{5,13},{9,1},{13,5},{2,10},{6,14},... | collective-permute-start | bytes 12296 | tf_op jit(solution)/shard_map/ppermute | solution.py:30
  363.2 54.6 %collective-permute-start.38 = (bf16[352,1536]{1,0:T(8,128)(2,1)S(1)}, bf16[352,1536]{1,0:T(8,128)(2,1)S(1)}, u32[]{:S(2)}, u32[]{:S(2)}) collective-permute-start(bf16[352,1536]{1,0:T(8,128)(2,1)S(1)} %get-tuple-element.11), channel_id=1, source_target_pairs={{0,4},{4,0},{8,12},{12,8},{1,5},{5,1},{9,13},{13,9},{2,6},{6,2},{1... | collective-permute-start | bytes 3244040 | tf_op jit(solution)/shard_map/ppermute | solution.py:30
  385.7 32.1 %collective-permute-start.40 = (bf16[352,1536]{1,0:T(8,128)(2,1)S(1)}, bf16[352,1536]{1,0:T(8,128)(2,1)S(1)}, u32[]{:S(2)}, u32[]{:S(2)}) collective-permute-start(bf16[352,1536]{1,0:T(8,128)(2,1)S(1)} %add_convert_fusion.10), channel_id=1, source_target_pairs={{0,8},{4,12},{8,0},{12,4},{1,9},{5,13},{9,1},{13,5},{2,10},{6,14},... | collective-permute-start | bytes 3244040 | tf_op jit(solution)/shard_map/ppermute | solution.py:30
  387.2 50.8 %collective-permute-start.44 = (bf16[352,1536]{1,0:T(8,128)(2,1)S(1)}, bf16[352,1536]{1,0:T(8,128)(2,1)S(1)}, u32[]{:S(2)}, u32[]{:S(2)}) collective-permute-start(bf16[352,1536]{1,0:T(8,128)(2,1)S(1)} %add_convert_fusion.8), channel_id=1, source_target_pairs={{0,2},{1,3},{2,0},{3,1},{4,6},{5,7},{6,4},{7,5},{8,10},{9,11},{10,... | collective-permute-start | bytes 3244040 | tf_op jit(solution)/shard_map/ppermute | solution.py:30
  (51 other events, 788.4 us)

commit v2 on v0

--- a/solution.py
+++ b/solution.py
@@ -1,14 +1,22 @@
 import jax
 import jax.numpy as jnp
 from jax import lax
+from jax.experimental import pallas as pl
+from jax.experimental.pallas import tpu as pltpu
 from jax.sharding import PartitionSpec as P
 
 DT = 6144
 DS = 1408
 PATCHES = 256
-
+F32 = jnp.float32
+BF16 = jnp.bfloat16
 
 epsilon = 1e-06
+
+FC = 256
+TINY = pl.CostEstimate(flops=1000, transcendentals=0, bytes_accessed=1000)
+PARAMS = pltpu.CompilerParams(vmem_limit_bytes=58 * 2**20)
+LIGHT = pltpu.CompilerParams(vmem_limit_bytes=24 * 2**20)
 
 
 def gelu_value(value):
@@ -20,6 +28,461 @@
         0.5 * (1.0 + lax.erf(value * 0.7071067811865476))
         + value * jnp.exp(-0.5 * value * value) * 0.3989422804014327
     )
+
+
+def swap(value, axis, bit):
+    count = lax.axis_size(axis)
+    return lax.ppermute(value, axis, [(i, i ^ bit) for i in range(count)])
+
+
+def assemble(pieces, rows):
+    arrays = [p[0] for p in pieces]
+    cols = arrays[0].shape[1]
+    offs = jnp.stack([jnp.asarray(p[3], jnp.int32) for p in pieces])
+
+    def body(offs_ref, *refs):
+        parts, out, sems = refs[:-2], refs[-2], refs[-1]
+        copies = []
+        for i, part in enumerate(parts):
+            first, count = pieces[i][1:3]
+            off = pl.multiple_of(offs_ref[i], 16)
+            copies.append(
+                pltpu.make_async_copy(
+                    part.at[first : first + count, :], out.at[pl.ds(off, count), :], sems.at[i]
+                )
+            )
+        for copy in copies:
+            copy.start()
+        for copy in copies:
+            copy.wait()
+
+    return pl.pallas_call(
+        body,
+        out_shape=jax.ShapeDtypeStruct((rows, cols), arrays[0].dtype),
+        in_specs=[pl.BlockSpec(memory_space=pltpu.SMEM)]
+        + [pl.BlockSpec(memory_space=pl.ANY)] * len(pieces),
+        out_specs=pl.BlockSpec(memory_space=pltpu.VMEM),
+        scratch_shapes=[pltpu.SemaphoreType.DMA((len(pieces),))],
+        cost_estimate=TINY,
+        compiler_params=PARAMS,
+        name="assemble",
+    )(offs, *arrays)
+
+
+def whole(shape):
+    return pl.BlockSpec(shape, lambda j: (0,) * len(shape))
+
+
+def turned(value):
+    part = value[:, :128]
+    for at in range(128, value.shape[1], 128):
+        part = part + value[:, at : at + 128]
+    return jnp.sum(part.T, axis=0, keepdims=True)
+
+
+def teacher_sums(feats):
+    count, width = feats.shape
+    step = 512
+
+    def body(x_ref, out):
+        x = x_ref[...].astype(F32)
+        out[0:1, :] = turned(x)
+        out[1:2, :] = turned(x * x)
+        out[2:, :] = jnp.zeros((6, step), F32)
+
+    return pl.pallas_call(
+        body,
+        grid=(count // step,),
+        in_specs=[pl.BlockSpec((step, width), lambda j: (j, 0))],
+        out_specs=pl.BlockSpec((8, step), lambda j: (0, j)),
+        out_shape=jax.ShapeDtypeStruct((8, count), F32),
+        compiler_params=PARAMS,
+        cost_estimate=TINY,
+        name="teacher_sums",
+    )(feats)
+
+
+def target_parts(mx, ks, feats, sums, gain, bias, projection):
+    count, width = feats.shape
+    step = 256
+    toks = count // 4
+    per = toks // step
+
+    def body(mx_ref, x_ref, s_ref, g_ref, b_ref, w_ref, *outs):
+        j = pl.program_id(0)
+        sums_t = jnp.concatenate([s_ref[...], jnp.zeros((6, step), F32)], axis=0).T
+        mean = sums_t[:, 0:1] / DT
+        rstd = lax.rsqrt(sums_t[:, 1:2] / DT - mean * mean + epsilon)
+        tnorm = (x_ref[...].astype(F32) - mean) * rstd * g_ref[...] + b_ref[...]
+        value = jnp.dot(tnorm.astype(BF16), w_ref[...], preferred_element_type=F32).astype(BF16)
+        for n, out in enumerate(outs):
+
+            @pl.when(j // per == n)
+            def _(out=out):
+                out[...] = value
+
+    def row(j, mx_ref):
+        k = ks[0] - j // per
+        return (mx_ref[0] ^ k) * per + j % per
+
+    return pl.pallas_call(
+        body,
+        grid_spec=pltpu.PrefetchScalarGridSpec(
+            num_scalar_prefetch=1,
+            grid=(len(ks) * per,),
+            in_specs=[
+                pl.BlockSpec((step, width), lambda j, m: (row(j, m), 0)),
+                pl.BlockSpec((2, step), lambda j, m: (0, row(j, m))),
+                pl.BlockSpec((1, width), lambda j, m: (0, 0)),
+                pl.BlockSpec((1, width), lambda j, m: (0, 0)),
+                pl.BlockSpec((width, DS), lambda j, m: (0, 0)),
+            ],
+            out_specs=[
+                pl.BlockSpec(
+                    (step, DS), lambda j, m, n=n: (jnp.clip(j - n * per, 0, per - 1), 0)
+                )
+                for n in range(len(ks))
+            ],
+        ),
+        out_shape=[jax.ShapeDtypeStruct((toks, DS), BF16)] * len(ks),
+        compiler_params=PARAMS,
+        cost_estimate=TINY,
+        name="targets",
+    )(mx, feats, sums, gain, bias, projection)
+
+
+def student_norm(student, gain):
+    count, width = student.shape
+    step = 128
+
+    def body(x_ref, g_ref, out):
+        x = x_ref[...].astype(F32)
+        mean = jnp.sum(x, axis=1, keepdims=True) / DS
+        square = jnp.sum(x * x, axis=1, keepdims=True) / DS
+        out[...] = ((x - mean) * lax.rsqrt(square - mean * mean + epsilon) * g_ref[...]).astype(BF16)
+
+    return pl.pallas_call(
+        body,
+        grid=(count // step,),
+        in_specs=[
+            pl.BlockSpec((step, width), lambda j: (j, 0)),
+            pl.BlockSpec((1, width), lambda j: (0, 0)),
+        ],
+        out_specs=pl.BlockSpec((step, width), lambda j: (j, 0)),
+        out_shape=jax.ShapeDtypeStruct((count, width), BF16),
+        compiler_params=PARAMS,
+        cost_estimate=TINY,
+        name="student_norm",
+    )(student, gain)
+
+
+def forward_part(normed_own, normed_pair, weight):
+    toks = normed_own.shape[0]
+    cols = weight.shape[1]
+
+    def body(no, np_, w, pre, act):
+        for part, off in ((no, 0), (np_, toks)):
+            value = jnp.dot(part[...], w[...], preferred_element_type=F32)
+            pre[off : off + toks, :] = value
+            act[off : off + toks, :] = gelu_value(value).astype(BF16)
+
+    chunk = pl.BlockSpec((2 * toks, FC), lambda j: (0, j))
+    return pl.pallas_call(
+        body,
+        grid=(cols // FC,),
+        in_specs=[whole((toks, DS)), whole((toks, DS)), pl.BlockSpec((DS, FC), lambda j: (0, j))],
+        out_specs=[chunk, chunk],
+        out_shape=[
+            jax.ShapeDtypeStruct((2 * toks, cols), F32),
+            jax.ShapeDtypeStruct((2 * toks, cols), BF16),
+        ],
+        compiler_params=PARAMS,
+        cost_estimate=TINY,
+        name="forward",
+    )(normed_own, normed_pair, weight)
+
+
+def branch_part(act_near, act_far, w_near, w_far, which, dtype):
+    toks = act_near.shape[0] // 2
+    cols = act_near.shape[1]
+    step = 2 * FC
+    n = cols // step
+
+    def body(an, af, wn, wf, out, acc):
+        j = pl.program_id(0)
+
+        @pl.when(j == 0)
+        def _():
+            acc[...] = jnp.zeros_like(acc)
+
+        @pl.when(j < n)
+        def _():
+            acc[...] += nt(an[...], wn[...])
+
+        @pl.when(j >= n)
+        def _():
+            acc[...] += nt(af[...], wf[...])
+
+        @pl.when(j == 2 * n - 1)
+        def _():
+            out[...] = acc[...].astype(out.dtype)
+
+    near = lambda j: jnp.minimum(j, n - 1)
+    far = lambda j: jnp.maximum(j - n, 0)
+    return pl.pallas_call(
+        body,
+        grid=(2 * n,),
+        in_specs=[
+            pl.BlockSpec((toks, step), lambda j: (which, near(j))),
+            pl.BlockSpec((toks, step), lambda j: (which, far(j))),
+            pl.BlockSpec((DS, step), lambda j: (0, near(j))),
+            pl.BlockSpec((DS, step), lambda j: (0, far(j))),
+        ],
+        out_specs=whole((toks, DS)),
+        out_shape=jax.ShapeDtypeStruct((toks, DS), dtype),
+        scratch_shapes=[pltpu.VMEM((toks, DS), F32)],
+        compiler_params=PARAMS,
+        cost_estimate=TINY,
+        name="branch",
+    )(act_near, act_far, w_near, w_far)
+
+
+def store_blocks(mx, acc, scratch, outs):
+    if len(outs) == 1:
+        outs[0][...] = acc.astype(BF16)
+        return
+    rows = DS // 4
+    scratch[...] = acc.astype(BF16)
+    for k, out in enumerate(outs):
+        off = pl.multiple_of((mx ^ k) * rows, 32)
+        out[...] = scratch[pl.ds(off, rows), :]
+
+
+def block_outs(split, cols):
+    count, rows = (4, DS // 4) if split else (1, DS)
+    specs = [pl.BlockSpec((rows, FC), lambda j: (0, j))] * count
+    shapes = [jax.ShapeDtypeStruct((rows, cols), BF16)] * count
+    return specs, shapes
+
+
+def grad_out_part(mx, grad_own, grad_pair, act, split):
+    toks = grad_own.shape[0]
+    cols = act.shape[1]
+    specs, shapes = block_outs(split, cols)
+
+    def body(mx_ref, go, gp, a, *rest):
+        outs, (gt, scratch) = rest[:-2], rest[-2:]
+
+        @pl.when(pl.program_id(0) == 0)
+        def _():
+            gt[:, :toks] = go[...].T
+            gt[:, toks:] = gp[...].T
+
+        acc = jnp.dot(gt[...], a[...], preferred_element_type=F32)
+        store_blocks(mx_ref[0], acc, scratch, outs)
+
+    return pl.pallas_call(
+        body,
+        grid=(cols // FC,),
+        in_specs=[
+            pl.BlockSpec(memory_space=pltpu.SMEM),
+            whole((toks, DS)),
+            whole((toks, DS)),
+            pl.BlockSpec((2 * toks, FC), lambda j: (0, j)),
+        ],
+        out_specs=specs,
+        out_shape=shapes,
+        scratch_shapes=[pltpu.VMEM((DS, 2 * toks), BF16), pltpu.VMEM((DS, FC), BF16)],
+        compiler_params=LIGHT,
+        cost_estimate=TINY,
+        name="grad_out",
+    )(mx, grad_own, grad_pair, act)
+
+
+def grad_in_part(mx, grad_own, grad_pair, w_out, slope, normed_t, split):
+    toks = grad_own.shape[0]
+    cols = w_out.shape[1]
+    specs, shapes = block_outs(split, cols)
+
+    def body(mx_ref, go, gp, w, sl, nrm, *rest):
+        outs, (pre, scratch) = rest[:-2], rest[-2:]
+        for part, off in ((go, 0), (gp, toks)):
+            act_grad = jnp.dot(part[...], w[...], preferred_element_type=F32)
+            pre[off : off + toks, :] = (act_grad * sl[off : off + toks, :]).astype(BF16)
+        acc = jnp.dot(nrm[...], pre[...], preferred_element_type=F32)
+        store_blocks(mx_ref[0], acc, scratch, outs)
+
+    return pl.pallas_call(
+        body,
+        grid=(cols // FC,),
+        in_specs=[
+            pl.BlockSpec(memory_space=pltpu.SMEM),
+            whole((toks, DS)),
+            whole((toks, DS)),
+            pl.BlockSpec((DS, FC), lambda j: (0, j)),
+            pl.BlockSpec((2 * toks, FC), lambda j: (0, j)),
+            whole((DS, 2 * toks)),
+        ],
+        out_specs=specs,
+        out_shape=shapes,
+        scratch_shapes=[pltpu.VMEM((2 * toks, FC), BF16), pltpu.VMEM((DS, FC), BF16)],
+        compiler_params=LIGHT,
+        cost_estimate=TINY,
+        name="grad_in",
+    )(mx, grad_own, grad_pair, w_out, slope, normed_t)
+
+
+def after(value, *deps):
+    return lax.optimization_barrier((value,) + deps)[0]
+
+
+def together(*values):
+    return lax.optimization_barrier(values)
+
+
+def nt(left, right):
+    return lax.dot_general(left, right, (((1,), (1,)), ((), ())), preferred_element_type=F32)
+
+
+def tn(left, right):
+    return lax.dot_general(
+        left, right, (((0,), (0,)), ((), ())), preferred_element_type=F32
+    ).astype(BF16)
+
+
+def pair_shards(teacher_feats, t_gain, t_bias, projection, student_in, s_gain, w_in, w_out):
+    mx = lax.axis_index("mx")
+    g = lax.axis_index("group")
+    patch_all, image_loc, feat_loc = teacher_feats.shape
+    patch_loc = patch_all // 4
+    toks = patch_loc * image_loc
+    tokens = PATCHES * image_loc * 4
+    w_out = w_out.T
+    rows, cols = w_in.shape
+    half = rows // 2
+    mine, other = g * half, (1 - g) * half
+
+    mx1 = mx.reshape(1).astype(jnp.int32)
+
+    def my_half(w):
+        return lax.dynamic_slice(w, (mine, 0), (half, cols))
+
+    z_send = jnp.concatenate([my_half(w_in), my_half(w_out)], axis=0)
+    z_g = swap(z_send, "my", 2)
+    in_near = lax.all_gather(w_in, "mx", axis=0, tiled=True)
+    out_near = lax.all_gather(w_out, "mx", axis=0, tiled=True)
+
+    feats = teacher_feats.reshape(4 * toks, feat_loc)
+    student = student_in.reshape(toks, DS)
+    normed_own = student_norm(after(student, z_send), s_gain.reshape(1, DS))
+    normed_pair = swap(normed_own, "my", 1)
+    sums = teacher_sums(after(feats, normed_own))
+    sums = lax.psum(sums[:2], "mx")
+    gain = t_gain.astype(F32).reshape(1, feat_loc)
+    bias = t_bias.astype(F32).reshape(1, feat_loc)
+    parts = target_parts(mx1, (3, 2, 1, 0), feats, sums, gain, bias, projection)
+    q3, q2, q1, q0, z_g, normed_pair = together(*parts, z_g, normed_pair)
+
+    d_g = swap(z_g, "mx", 2)
+    z_o = swap(z_g, "group", 1)
+    zgc = swap(z_g, "mx", 1)
+    q3c = swap(q3, "mx", 1)
+    pre_near, act_near = forward_part(normed_own, normed_pair, in_near)
+    pre_near, act_near, d_g, z_o, zgc, q3c = together(pre_near, act_near, d_g, z_o, zgc, q3c)
+    in_do = swap(d_g[:half], "group", 1)
+    out_do = swap(z_o[half:], "mx", 2)
+    zoc, dgc = swap(z_o, "mx", 1), swap(d_g, "mx", 1)
+    in_do, out_do, zoc, dgc = together(in_do, out_do, zoc, dgc)
+    in_doc, out_doc = swap(in_do, "mx", 1), swap(out_do, "mx", 1)
+    t2 = (q2.astype(F32) + q3c.astype(F32)).astype(BF16)
+    in_doc, out_doc, t2 = together(in_doc, out_doc, t2)
+
+    def far_rows(first, d_o, d_oc):
+        out = []
+        for part, part_c, block, off, at in (
+            (z_g, zgc, 0, mine, first),
+            (z_o, zoc, 0, other, first),
+            (d_g, dgc, 2, mine, first),
+            (d_o, d_oc, 2, other, 0),
+        ):
+            out.append((part, at, half, (mx ^ block) * rows + off))
+            out.append((part_c, at, half, (mx ^ block ^ 1) * rows + off))
+        return out
+
+    in_far = assemble(far_rows(0, in_do, in_doc), DS)
+    target_x = swap(t2, "mx", 2)
+    q1c = swap(after(q1, in_doc), "mx", 1)
+    pre_far, act_far = forward_part(normed_own, normed_pair, in_far)
+    pre_far, act_far, q1c, out_doc = together(pre_far, act_far, q1c, out_doc)
+    out_far = assemble(far_rows(half, out_do, out_doc), DS)
+    t0 = q0.astype(F32) + q1c.astype(F32)
+
+    branch_pair = branch_part(act_near, act_far, out_near, out_far, 1, BF16)
+    branch_recv = swap(branch_pair, "my", 1)
+    branch_own = branch_part(after(act_near, branch_pair), act_far, out_near, out_far, 0, F32)
+    slope_far = gelu_slope(after(pre_far, branch_own))
+    slope_near = gelu_slope(after(pre_near, slope_far))
+    normed_t = jnp.concatenate([after(normed_own, slope_near).T, normed_pair.T], axis=1)
+    branch_recv = after(branch_recv, normed_t)
+
+    target = t0 + target_x.astype(F32)
+    residue = student.astype(F32) + (branch_own + branch_recv.astype(F32)) - target
+    grad_own = (residue / jnp.sqrt(jnp.float32(tokens))).astype(BF16)
+    loss = jnp.broadcast_to(jnp.sum(residue * residue), (8, 128))
+    grad_own, loss = lax.optimization_barrier((grad_own, loss))
+    grad_pair = swap(grad_own, "my", 1)
+    for bit in (1, 2):
+        loss = loss + swap(loss, "mx", bit)
+    grad_pair = after(grad_pair, loss)
+
+    loss_z = swap(loss, "my", 1)
+    o0, o1, o2, o3 = grad_out_part(mx1, grad_own, grad_pair, act_far, True)
+    o0, o1, o2, o3, loss_z = together(o0, o1, o2, o3, loss_z)
+    loss = loss + loss_z
+    loss_z = swap(loss, "my", 2)
+    got2, got0 = swap(o3, "mx", 1), swap(o1, "mx", 1)
+    h0, h1 = slice(0, half), slice(half, rows)
+    s2_out = [(o2[c].astype(F32) + got2[c].astype(F32)).astype(BF16) for c in (h0, h1)]
+    x_out = [swap(v, "mx", 2) for v in s2_out]
+    i0, i1, i2, i3 = grad_in_part(
+        mx1, after(grad_own, *s2_out), grad_pair, out_far, slope_far, normed_t, True
+    )
+    i0, i1, i2, i3, x_out0, got0, loss_z = together(i0, i1, i2, i3, x_out[0], got0, loss_z)
+    mse_loss = (loss + loss_z)[0, :1] / (tokens * DS)
+
+    def last(keep, got, x):
+        return (keep.astype(F32) + got.astype(F32) + x.astype(F32)).astype(BF16)
+
+    f0 = last(o0[h0], got0[h0], x_out0)
+    f_out0 = swap(f0, "my", 2)
+    gin2, gin0 = swap(after(i3, f0), "mx", 1), swap(after(i1, f0), "mx", 1)
+    s2_in = (i2.astype(F32) + gin2.astype(F32)).astype(BF16)
+    x_in = swap(s2_in, "mx", 2)
+    n0, n1, n2, n3 = grad_out_part(mx1, after(grad_own, s2_in), grad_pair, act_near, True)
+    n0, n1, n2, n3, x_out1, gin0, f_out0 = together(n0, n1, n2, n3, x_out[1], gin0, f_out0)
+    f1 = last(o0[h1], got0[h1], x_out1)
+    f_out1 = swap(f1, "my", 2)
+    gn2, gn0 = swap(after(n3, f1), "mx", 1), swap(after(n1, f1), "mx", 1)
+    gn2, gn0 = together(gn2, gn0)
+    s2_on = (n2.astype(F32) + gn2.astype(F32)).astype(BF16)
+    x_on = swap(s2_on, "mx", 2)
+    m0, m1, m2, m3 = grad_in_part(
+        mx1, after(grad_own, s2_on), grad_pair, out_near, slope_near, normed_t, True
+    )
+    m0, m1, m2, m3, x_in, f_out1 = together(m0, m1, m2, m3, x_in, f_out1)
+    f2 = [last(i0[c], gin0[c], x_in[c]) for c in (h0, h1)]
+    f_in = [swap(v, "my", 2) for v in f2]
+    gm2, gm0 = swap(after(m3, *f2), "mx", 1), swap(after(m1, *f2), "mx", 1)
+    gm2, gm0, x_on, f_in0 = together(gm2, gm0, x_on, f_in[0])
+    s2_mn = (m2.astype(F32) + gm2.astype(F32)).astype(BF16)
+    x_mn = swap(s2_mn, "mx", 2)
+    grad_out_near = n0.astype(F32) + gn0.astype(F32) + x_on.astype(F32)
+    grad_in_near = m0.astype(F32) + gm0.astype(F32) + x_mn.astype(F32)
+    f_out = jnp.concatenate([f_out0, f_out1], axis=0)
+    f_in = jnp.concatenate([f_in0, f_in[1]], axis=0)
+    grad_out = (grad_out_near + f_out.astype(F32)).T
+    grad_in = grad_in_near + f_in.astype(F32)
+    return (mse_loss, grad_in, grad_out)
 
 
 def shards(teacher_feats, t_gain, t_bias, projection, student_in, s_gain, w_in, w_out):
@@ -109,4 +572,6 @@
         P("my", "mx"),
     )
     out_specs = (P("group"), P(("group", "mx"), "my"), P(("group", "my"), "mx"))
-    return jax.shard_map(shards, mesh=mesh, in_specs=in_specs, out_specs=out_specs, check_vma=False)
+    pairs = mesh.shape["group"] == 2 and mesh.shape["mx"] == 4 and mesh.shape["my"] == 4
+    body = pair_shards if pairs else shards
+    return jax.shard_map(body, mesh=mesh, in_specs=in_specs, out_specs=out_specs, check_vma=False)

time: 626 us -> 386 us (0.62)
  waiting for transfers between devices: 406 us -> 157 us
  Pallas kernels: 0 us -> 121 us
  matrix products: 108 us -> 0 us
  blocking collectives: 45.6 us -> 12.1 us
  starting transfers between devices: 0.85 us -> 28.7 us
  other arithmetic: 24.7 us -> 31.2 us
    all_gather x4 -> x2, waiting for transfers between devices: 218 us -> 0.02 us  [the longest x1 0.02 us: pair_shards(): out_near = lax.all_gather(w_out, 'mx', axis=0, tiled=True)]
    reduce_scatter x4 -> x0, waiting for transfers between devices: 186 us -> none  [the longest x1 105 us: shards(): lax.psum_scatter(branch_part.astype(jnp.bfloat16), 'my', scatter_dimensio...]
    ppermute x0 -> x37, waiting for transfers between devices: none -> 156 us  [swap(): return lax.ppermute(value, axis, [(i, i ^ bit) for i in range(count)])]
    pallas_call x0 -> x13, Pallas kernels: none -> 121 us  [the longest x2 24.6 us: grad_in_part(): pl.pallas_call(body, grid=(cols // FC,), in_specs=[pl.BlockSpec(memory_sp...]
    dot_general x5 -> x0, matrix products: 108 us -> none  [the longest x1 43.9 us: shards(): lax.dot_general(normed_flat, grad_pre, (((0,), (0,)), ((), ())), preferre...]
    psum x2 -> x1, blocking collectives: 45.6 us -> 12.1 us  [pair_shards(): sums = lax.psum(sums[:2], 'mx')]
    ppermute x0 -> x37, starting transfers between devices: none -> 28.6 us  [swap(): return lax.ppermute(value, axis, [(i, i ^ bit) for i in range(count)])]
    add x0 -> x7, other arithmetic: none -> 17.2 us  [the longest x2 15.4 us: gelu_slope(): 0.5 * (1.0 + lax.erf(value * 0.7071067811865476))]
  transfers between devices with their start and end apart: 8 -> 39, of which waited for: 7 -> 19; matrix products, arithmetic and copies ran while one was open for 14% -> 9% of each run, Pallas kernels for 0% -> 31%
where the time goes in v2:
time: 386 us; the launch traced here: 385 us
  waiting for transfers between devices  157 us (41%)
  Pallas kernels  121 us (31%)
  other arithmetic  31.2 us (8%)
  starting transfers between devices  28.7 us (7%)
  local copies, waits for them, and re-layouts  18.4 us (5%)
  between operations  16.3 us (4%)
  blocking collectives  12.1 us (3%)
    ppermute x37, waiting for transfers between devices, swap(): return lax.ppermute(value, axis, [(i, i ^ bit) for i in range(count)])  156 us
    ppermute x37, starting transfers between devices, swap(): return lax.ppermute(value, axis, [(i, i ^ bit) for i in range(count)])  28.6 us
    pallas_call x2, Pallas kernels, grad_in_part(): pl.pallas_call(body, grid=(cols // FC,), in_specs=[pl.BlockSpec(memory_sp...  24.6 us
    pallas_call x2, Pallas kernels, branch_part(): pl.pallas_call(body, grid=(2 * n,), in_specs=[pl.BlockSpec((toks, step),...  22.4 us
    pallas_call x2, Pallas kernels, forward_part(): pl.pallas_call(body, grid=(cols // FC,), in_specs=[whole((toks, DS)), who...  21.6 us
    pallas_call x1, Pallas kernels, target_parts(): pl.pallas_call(body, grid_spec=pltpu.PrefetchScalarGridSpec(num_scalar_pr...  18.4 us
    add x2, other arithmetic, gelu_slope(): 0.5 * (1.0 + lax.erf(value * 0.7071067811865476))  15.4 us
    pallas_call x2, Pallas kernels, grad_out_part(): pl.pallas_call(body, grid=(cols // FC,), in_specs=[pl.BlockSpec(memory_sp...  14.6 us
  transfers between devices with their start and end apart: 39, of which 19 were waited for; matrix products, arithmetic and copies ran while one was open for 9% of the time, Pallas kernels for 31%

profile of v2, /device:TPU:0, one launch (start us, length us, event | category | flops | bytes accessed | tf_op | source)
XLA Modules:
  0.0 384.5 jit_solution(3105207947847417082)
XLA Ops:
  10.5 3.9 %student_norm.1.no = bf16[512,1408]{1,0:T(8,128)(2,1)} custom-call(bf16[512,1408]{1,0:T(8,128)(2,1)} %bitcast.29, f32[1,1408]{1,0:T(1,128)} %reshape.31.g_ref), custom_call_target="tpu_custom_call" | custom-call | flops 1000 | bytes 1000 | tf_op jit(solution)/shard_map/student_norm/pallas_call | solution.py:164
  14.4 2.6 copy.11
  17.0 3.0 collective-permute-start.1
  20.0 2.6 collective-permute-start
  22.6 5.2 %teacher_sums.1 = f32[8,2048]{1,0:T(8,128)} custom-call(bf16[2048,1536]{1,0:T(8,128)(2,1)} %bitcast.27), custom_call_target="tpu_custom_call" | custom-call | flops 1000 | bytes 1000 | tf_op jit(solution)/shard_map/teacher_sums/pallas_call | solution.py:93
  29.8 12.1 %psum.7.s_ref = f32[2,2048]{1,0:T(2,128)} all-reduce(f32[2,2048]{1,0:T(2,128)S(1)} %slice.72), channel_id=1, replica_groups=mesh['group'=2,'mx'=4,'my'=4] {'mx'}, use_global_device_ids=true, to_apply=%region_0.0 | all-reduce | flops 4096 | bytes 32768 | tf_op jit(solution)/shard_map/psum | solution.py:380
  42.0 18.4 %targets.1 = (bf16[512,1408]{1,0:T(8,128)(2,1)}, bf16[512,1408]{1,0:T(8,128)(2,1)}, bf16[512,1408]{1,0:T(8,128)(2,1)}, bf16[512,1408]{1,0:T(8,128)(2,1)}) custom-call(s32[1]{0:T(128)} %bitcast.2.mx_ref, bf16[2048,1536]{1,0:T(8,128)(2,1)} %bitcast.28, f32[2,2048]{1,0:T(2,128)} %psum.7.s_ref, f32[1,1536]{1,0:T(1,128)} %reshape.39.g_ref, ...), custom_call_target="tpu_custom_call" | custom-call | flops 1000 | bytes 1000 | tf_op jit(solution)/shard_map/targets/pallas_call | solution.py:128
  60.3 14.0 %collective-permute-done.refs_0_ = bf16[352,1536]{1,0:T(8,128)(2,1)S(1)} collective-permute-done((bf16[352,1536]{1,0:T(8,128)(2,1)}, bf16[352,1536]{1,0:T(8,128)(2,1)S(1)}, u32[]{:S(2)}, u32[]{:S(2)}) %collective-permute-start) | collective-permute-done | bytes 1081376 | tf_op jit(solution)/shard_map/ppermute | solution.py:35
  81.9 10.8 %forward.2 = (f32[1024,1536]{1,0:T(8,128)}, bf16[1024,1536]{1,0:T(8,128)(2,1)}) custom-call(bf16[512,1408]{1,0:T(8,128)(2,1)} %student_norm.1.no, bf16[512,1408]{1,0:T(8,128)(2,1)} %copy.12.np_, bf16[1408,1536]{1,0:T(8,128)(2,1)} %all-gather.3.cloned.1.call-done.w), custom_call_target="tpu_custom_call" | custom-call | flops 1000 | bytes 1000 | tf_op jit(solution)/shard_map/forward/pallas_call | solution.py:190
  92.7 9.8 %collective-permute-done.3.refs_2_ = bf16[352,1536]{1,0:T(8,128)(2,1)S(1)} collective-permute-done((bf16[352,1536]{1,0:T(8,128)(2,1)S(1)}, bf16[352,1536]{1,0:T(8,128)(2,1)S(1)}, u32[]{:S(2)}, u32[]{:S(2)}) %collective-permute-start.3) | collective-permute-done | bytes 1081376 | tf_op jit(solution)/shard_map/ppermute | solution.py:35
  102.4 3.7 collective-permute-done.2.refs_4_
  108.9 12.2 %collective-permute-done.6.refs_6_ = bf16[176,1536]{1,0:T(8,128)(2,1)S(1)} collective-permute-done((bf16[176,1536]{1,0:T(8,128)(2,1)S(1)}, bf16[176,1536]{1,0:T(8,128)(2,1)S(1)}, u32[]{:S(2)}, u32[]{:S(2)}) %collective-permute-start.6) | collective-permute-done | bytes 540704 | tf_op jit(solution)/shard_map/ppermute | solution.py:35
  124.2 2.8 add_convert_fusion
  129.2 4.9 %assemble.2.w = bf16[1408,1536]{1,0:T(8,128)(2,1)} custom-call(s32[8]{0:T(128)} %stack.44.offs_ref, bf16[352,1536]{1,0:T(8,128)(2,1)} %copy-done.10, bf16[352,1536]{1,0:T(8,128)(2,1)} %collective-permute-done.4.refs_1_, bf16[352,1536]{1,0:T(8,128)(2,1)} %copy-done.5, bf16[352,1536]{1,0:T(8,128)(2,1)} %copy-done.11, bf16[352,1536]{1,0:T(8,128)(2,1)} %copy-done.6, ...), custom_call_target="tpu_custom_call" | custom-call | flops 1000 | bytes 1000 | tf_op jit(solution)/shard_map/assemble/pallas_call | solution.py:59
  134.8 10.8 %forward.3 = (f32[1024,1536]{1,0:T(8,128)}, bf16[1024,1536]{1,0:T(8,128)(2,1)}) custom-call(bf16[512,1408]{1,0:T(8,128)(2,1)} %student_norm.1.no, bf16[512,1408]{1,0:T(8,128)(2,1)} %copy.12.np_, bf16[1408,1536]{1,0:T(8,128)(2,1)} %assemble.2.w), custom_call_target="tpu_custom_call" | custom-call | flops 1000 | bytes 1000 | tf_op jit(solution)/shard_map/forward/pallas_call | solution.py:190
  145.6 5.0 %assemble.3.wf.w = bf16[1408,1536]{1,0:T(8,128)(2,1)} custom-call(s32[8]{0:T(128)} %stack.44.offs_ref, bf16[352,1536]{1,0:T(8,128)(2,1)} %copy-done.10, bf16[352,1536]{1,0:T(8,128)(2,1)} %collective-permute-done.4.refs_1_, bf16[352,1536]{1,0:T(8,128)(2,1)} %copy-done.5, bf16[352,1536]{1,0:T(8,128)(2,1)} %copy-done.11, bf16[352,1536]{1,0:T(8,128)(2,1)} %copy-done.6, ...), custom_call_target="tpu_custom_call" | custom-call | flops 1000 | bytes 1000 | tf_op jit(solution)/shard_map/assemble/pallas_call | solution.py:59
  150.6 10.9 %branch.2 = bf16[512,1408]{1,0:T(8,128)(2,1)} custom-call(bf16[1024,1536]{1,0:T(8,128)(2,1)} %get-tuple-element.130.an.a, bf16[1024,1536]{1,0:T(8,128)(2,1)} %get-tuple-element.128.af.a, bf16[1408,1536]{1,0:T(8,128)(2,1)} %all-gather.5.cloned.1.call-done.wn.w, bf16[1408,1536]{1,0:T(8,128)(2,1)} %assemble.3.wf.w), custom_call_target="tpu_custom_call" | custom-call | flops 1000 | bytes 1000 | tf_op jit(solution)/shard_map/branch/pallas_call | solution.py:232
  163.0 11.5 %branch.3 = f32[512,1408]{1,0:T(8,128)} custom-call(bf16[1024,1536]{1,0:T(8,128)(2,1)} %get-tuple-element.130.an.a, bf16[1024,1536]{1,0:T(8,128)(2,1)} %get-tuple-element.128.af.a, bf16[1408,1536]{1,0:T(8,128)(2,1)} %all-gather.5.cloned.1.call-done.wn.w, bf16[1408,1536]{1,0:T(8,128)(2,1)} %assemble.3.wf.w), custom_call_target="tpu_custom_call" | custom-call | flops 1000 | bytes 1000 | tf_op jit(solution)/shard_map/branch/pallas_call | solution.py:232
  174.5 7.6 %fusion.3.sl = f32[1024,1536]{1,0:T(8,128)} fusion(f32[1024,1536]{1,0:T(8,128)} %get-tuple-element.133), kind=kLoop, calls=%fused_computation.5 | loop fusion | flops 12582912 | bytes 12582912 | tf_op jit(solution)/shard_map/add | solution.py:28
  182.2 7.7 %fusion.7.sl = f32[1024,1536]{1,0:T(8,128)} fusion(f32[1024,1536]{1,0:T(8,128)} %get-tuple-element.134), kind=kLoop, calls=%fused_computation.9 | loop fusion | flops 12582912 | bytes 12582912 | tf_op jit(solution)/shard_map/add | solution.py:28
  195.6 4.3 %multiply_reduce_fusion = (f32[]{:T(128)}, f32[512,1408]{1,0:T(8,128)S(1)}) fusion(bf16[512,1408]{1,0:T(8,128)(2,1)} %collective-permute-done.14, bf16[512,1408]{1,0:T(8,128)(2,1)} %copy-done.16, bf16[512,1408]{1,0:T(8,128)(2,1)S(1)} %copy-done.15, f32[512,1408]{1,0:T(8,128)S(1)} %copy-done.4, bf16[512,1408]{1,0:T(8,128)(2,1)} %collective-permute-done.13, ...), kind=kLoop, calls=%fused_computation.11 | loop fusion | flops 8650751 | bytes 12976132 | tf_op jit(solution)/shard_map/reduce_sum | solution.py:431
  207.9 26.1 %collective-permute-done.17.gp = bf16[512,1408]{1,0:T(8,128)(2,1)S(1)} collective-permute-done((bf16[512,1408]{1,0:T(8,128)(2,1)S(1)}, bf16[512,1408]{1,0:T(8,128)(2,1)S(1)}, u32[]{:S(2)}, u32[]{:S(2)}) %collective-permute-start.17) | collective-permute-done | bytes 1441824 | tf_op jit(solution)/shard_map/ppermute | solution.py:35
  234.0 7.3 %grad_out.2 = (bf16[352,1536]{1,0:T(8,128)(2,1)S(1)}, bf16[352,1536]{1,0:T(8,128)(2,1)S(1)}, bf16[352,1536]{1,0:T(8,128)(2,1)S(1)}, bf16[352,1536]{1,0:T(8,128)(2,1)S(1)}) custom-call(s32[1]{0:T(128)} %bitcast.2.mx_ref, bf16[512,1408]{1,0:T(8,128)(2,1)S(1)} %multiply_convert_fusion.go, bf16[512,1408]{1,0:T(8,128)(2,1)S(1)} %collective-permute-done.17.gp, ...), custom_call_target="tpu_custom_call" | custom-call | flops 1000 | bytes 1000 | tf_op jit(solution)/shard_map/grad_out/pallas_call | solution.py:284
  248.3 2.8 copy-done.2
  251.0 12.3 %grad_in.2 = (bf16[352,1536]{1,0:T(8,128)(2,1)S(1)}, bf16[352,1536]{1,0:T(8,128)(2,1)S(1)}, bf16[352,1536]{1,0:T(8,128)(2,1)S(1)}, bf16[352,1536]{1,0:T(8,128)(2,1)S(1)}) custom-call(s32[1]{0:T(128)} %bitcast.2.mx_ref, bf16[512,1408]{1,0:T(8,128)(2,1)S(1)} %multiply_convert_fusion.go, bf16[512,1408]{1,0:T(8,128)(2,1)S(1)} %collective-permute-done.17.gp, ...), custom_call_target="tpu_custom_call" | custom-call | flops 1000 | bytes 1000 | tf_op jit(solution)/shard_map/grad_in/pallas_call | solution.py:315
  266.7 7.3 %grad_out.3 = (bf16[352,1536]{1,0:T(8,128)(2,1)S(1)}, bf16[352,1536]{1,0:T(8,128)(2,1)S(1)}, bf16[352,1536]{1,0:T(8,128)(2,1)S(1)}, bf16[352,1536]{1,0:T(8,128)(2,1)S(1)}) custom-call(s32[1]{0:T(128)} %bitcast.2.mx_ref, bf16[512,1408]{1,0:T(8,128)(2,1)S(1)} %multiply_convert_fusion.go, bf16[512,1408]{1,0:T(8,128)(2,1)S(1)} %collective-permute-done.17.gp, ...), custom_call_target="tpu_custom_call" | custom-call | flops 1000 | bytes 1000 | tf_op jit(solution)/shard_map/grad_out/pallas_call | solution.py:284
  274.0 4.5 %collective-permute-done.24 = bf16[176,1536]{1,0:T(8,128)(2,1)S(1)} collective-permute-done((bf16[176,1536]{1,0:T(8,128)(2,1)S(1)}, bf16[176,1536]{1,0:T(8,128)(2,1)S(1)}, u32[]{:S(2)}, u32[]{:S(2)}) %collective-permute-start.24) | collective-permute-done | bytes 540704 | tf_op jit(solution)/shard_map/ppermute | solution.py:35
  278.4 12.8 %collective-permute-done.26 = bf16[176,1536]{1,0:T(8,128)(2,1)S(1)} collective-permute-done((bf16[176,1536]{1,0:T(8,128)(2,1)S(1)}, bf16[176,1536]{1,0:T(8,128)(2,1)S(1)}, u32[]{:S(2)}, u32[]{:S(2)}) %collective-permute-start.26) | collective-permute-done | bytes 540704 | tf_op jit(solution)/shard_map/ppermute | solution.py:35
  296.0 12.3 %grad_in.3 = (bf16[352,1536]{1,0:T(8,128)(2,1)S(1)}, bf16[352,1536]{1,0:T(8,128)(2,1)S(1)}, bf16[352,1536]{1,0:T(8,128)(2,1)S(1)}, bf16[352,1536]{1,0:T(8,128)(2,1)S(1)}) custom-call(s32[1]{0:T(128)} %bitcast.2.mx_ref, bf16[512,1408]{1,0:T(8,128)(2,1)S(1)} %multiply_convert_fusion.go, bf16[512,1408]{1,0:T(8,128)(2,1)S(1)} %collective-permute-done.17.gp, ...), custom_call_target="tpu_custom_call" | custom-call | flops 1000 | bytes 1000 | tf_op jit(solution)/shard_map/grad_in/pallas_call | solution.py:315
  308.4 10.3 %collective-permute-done.30 = bf16[176,1536]{1,0:T(8,128)(2,1)S(1)} collective-permute-done((bf16[176,1536]{1,0:T(8,128)(2,1)S(1)}, bf16[176,1536]{1,0:T(8,128)(2,1)S(1)}, u32[]{:S(2)}, u32[]{:S(2)}) %collective-permute-start.30) | collective-permute-done | bytes 540704 | tf_op jit(solution)/shard_map/ppermute | solution.py:35
  320.3 26.2 %collective-permute-done.34 = bf16[176,1536]{1,0:T(8,128)(2,1)S(1)} collective-permute-done((bf16[176,1536]{1,0:T(8,128)(2,1)S(1)}, bf16[176,1536]{1,0:T(8,128)(2,1)S(1)}, u32[]{:S(2)}, u32[]{:S(2)}) %collective-permute-start.34) | collective-permute-done | bytes 540704 | tf_op jit(solution)/shard_map/ppermute | solution.py:35
  351.4 23.3 %collective-permute-done.36 = bf16[176,1536]{1,0:T(8,128)(2,1)S(1)} collective-permute-done((bf16[176,1536]{1,0:T(8,128)(2,1)S(1)}, bf16[176,1536]{1,0:T(8,128)(2,1)S(1)}, u32[]{:S(2)}, u32[]{:S(2)}) %collective-permute-start.36) | collective-permute-done | bytes 540704 | tf_op jit(solution)/shard_map/ppermute | solution.py:35
  (161 shorter events, 59.2 us)
Async XLA Ops:
  7.2 74.7 %all-gather.3.cloned.1.call-start = ((), (), s32[]{:S(2)}) async-start(), calls=%async_computation | async-start | bytes 5406720 | tf_op jit(solution)/shard_map/all_gather | solution.py:372
  7.9 142.7 %all-gather.5.cloned.1.call-start = ((), (), s32[]{:S(2)}) async-start(), calls=%async_computation.1 | async-start | bytes 5406720 | tf_op jit(solution)/shard_map/all_gather | solution.py:373
  17.0 58.0 %collective-permute-start.1 = (bf16[512,1408]{0,1:T(8,128)(2,1)}, bf16[512,1408]{0,1:T(8,128)(2,1)S(1)}, u32[]{:S(2)}, u32[]{:S(2)}) collective-permute-start(bf16[512,1408]{0,1:T(8,128)(2,1)} %copy.11), channel_id=1, source_target_pairs={{0,1},{1,0},{2,3},{3,2},{4,5},{5,4},{6,7},{7,6},{8,9},{9,8},{10,11... | collective-permute-start | bytes 4325384 | tf_op jit(solution)/shard_map/ppermute | solution.py:35
  20.0 54.3 %collective-permute-start = (bf16[352,1536]{1,0:T(8,128)(2,1)}, bf16[352,1536]{1,0:T(8,128)(2,1)S(1)}, u32[]{:S(2)}, u32[]{:S(2)}) collective-permute-start(bf16[352,1536]{1,0:T(8,128)(2,1)} %pad_maximum_fusion.1), channel_id=1, source_target_pairs={{0,2},{1,3},{2,0},{3,1},{4,6},{5,7},{6,4},{7,5},{8,10},{9,11},{10,... | collective-permute-start | bytes 3244040 | tf_op jit(solution)/shard_map/ppermute | solution.py:35
  75.0 31.2 %collective-permute-start.5 = (bf16[512,1408]{1,0:T(8,128)(2,1)}, bf16[512,1408]{1,0:T(8,128)(2,1)}, u32[]{:S(2)}, u32[]{:S(2)}) collective-permute-start(bf16[512,1408]{1,0:T(8,128)(2,1)} %get-tuple-element.111), channel_id=1, source_target_pairs={{0,4},{4,0},{8,12},{12,8},{1,5},{5,1},{9,13},{13,9},{2,6},{6,2},{1... | collective-permute-start | bytes 4325384 | tf_op jit(solution)/shard_map/ppermute | solution.py:35
  76.2 16.5 %collective-permute-start.4 = (bf16[352,1536]{1,0:T(8,128)(2,1)S(1)}, bf16[352,1536]{1,0:T(8,128)(2,1)}, u32[]{:S(2)}, u32[]{:S(2)}) collective-permute-start(bf16[352,1536]{1,0:T(8,128)(2,1)S(1)} %collective-permute-done.refs_0_), channel_id=1, source_target_pairs={{0,4},{4,0},{8,12},{12,8},{1,5},{5,1},{9,13},{13,9},{2,6},{6,2},{1... | collective-permute-start | bytes 3244040 | tf_op jit(solution)/shard_map/ppermute | solution.py:35
  76.2 26.3 %collective-permute-start.3 = (bf16[352,1536]{1,0:T(8,128)(2,1)S(1)}, bf16[352,1536]{1,0:T(8,128)(2,1)S(1)}, u32[]{:S(2)}, u32[]{:S(2)}) collective-permute-start(bf16[352,1536]{1,0:T(8,128)(2,1)S(1)} %collective-permute-done.refs_0_), channel_id=1, source_target_pairs={{0,16},{16,0},{1,17},{17,1},{2,18},{18,2},{3,19},{19,3},{4,20},{20... | collective-permute-start | bytes 3244040 | tf_op jit(solution)/shard_map/ppermute | solution.py:35
  77.9 28.3 %collective-permute-start.2 = (bf16[352,1536]{1,0:T(8,128)(2,1)S(1)}, bf16[352,1536]{1,0:T(8,128)(2,1)S(1)}, u32[]{:S(2)}, u32[]{:S(2)}) collective-permute-start(bf16[352,1536]{1,0:T(8,128)(2,1)S(1)} %collective-permute-done.refs_0_), channel_id=1, source_target_pairs={{0,8},{4,12},{8,0},{12,4},{1,9},{5,13},{9,1},{13,5},{2,10},{6,14},... | collective-permute-start | bytes 3244040 | tf_op jit(solution)/shard_map/ppermute | solution.py:35
  106.2 16.1 %collective-permute-start.8 = (bf16[352,1536]{1,0:T(8,128)(2,1)S(1)}, bf16[352,1536]{1,0:T(8,128)(2,1)S(1)}, u32[]{:S(2)}, u32[]{:S(2)}) collective-permute-start(bf16[352,1536]{1,0:T(8,128)(2,1)S(1)} %collective-permute-done.3.refs_2_), channel_id=1, source_target_pairs={{0,4},{4,0},{8,12},{12,8},{1,5},{5,1},{9,13},{13,9},{2,6},{6,2},{1... | collective-permute-start | bytes 3244040 | tf_op jit(solution)/shard_map/ppermute | solution.py:35
  106.2 16.1 %collective-permute-start.9 = (bf16[352,1536]{1,0:T(8,128)(2,1)S(1)}, bf16[352,1536]{1,0:T(8,128)(2,1)S(1)}, u32[]{:S(2)}, u32[]{:S(2)}) collective-permute-start(bf16[352,1536]{1,0:T(8,128)(2,1)S(1)} %collective-permute-done.2.refs_4_), channel_id=1, source_target_pairs={{0,4},{4,0},{8,12},{12,8},{1,5},{5,1},{9,13},{13,9},{2,6},{6,2},{1... | collective-permute-start | bytes 3244040 | tf_op jit(solution)/shard_map/ppermute | solution.py:35
  106.8 14.3 %collective-permute-start.6 = (bf16[176,1536]{1,0:T(8,128)(2,1)S(1)}, bf16[176,1536]{1,0:T(8,128)(2,1)S(1)}, u32[]{:S(2)}, u32[]{:S(2)}) collective-permute-start(bf16[176,1536]{1,0:T(8,128)(2,1)S(1)} %slice.55), channel_id=1, source_target_pairs={{0,16},{16,0},{1,17},{17,1},{2,18},{18,2},{3,19},{19,3},{4,20},{20... | collective-permute-start | bytes 1622024 | tf_op jit(solution)/shard_map/ppermute | solution.py:35
  108.3 14.0 %collective-permute-start.7 = (bf16[176,1536]{1,0:T(8,128)(2,1)S(1)}, bf16[176,1536]{1,0:T(8,128)(2,1)S(1)}, u32[]{:S(2)}, u32[]{:S(2)}) collective-permute-start(bf16[176,1536]{1,0:T(8,128)(2,1)S(1)} %slice.56), channel_id=1, source_target_pairs={{0,8},{4,12},{8,0},{12,4},{1,9},{5,13},{9,1},{13,5},{2,10},{6,14},... | collective-permute-start | bytes 1622024 | tf_op jit(solution)/shard_map/ppermute | solution.py:35
  128.6 17.0 %collective-permute-start.12 = (bf16[512,1408]{1,0:T(8,128)(2,1)}, bf16[512,1408]{1,0:T(8,128)(2,1)S(1)}, u32[]{:S(2)}, u32[]{:S(2)}) collective-permute-start(bf16[512,1408]{1,0:T(8,128)(2,1)} %get-tuple-element.126), channel_id=1, source_target_pairs={{0,4},{4,0},{8,12},{12,8},{1,5},{5,1},{9,13},{13,9},{2,6},{6,2},{1... | collective-permute-start | bytes 4325384 | tf_op jit(solution)/shard_map/ppermute | solution.py:35
  134.2 61.4 %collective-permute-start.14 = (bf16[512,1408]{1,0:T(8,128)(2,1)}, bf16[512,1408]{1,0:T(8,128)(2,1)}, u32[]{:S(2)}, u32[]{:S(2)}) collective-permute-start(bf16[512,1408]{1,0:T(8,128)(2,1)} %add_convert_fusion), channel_id=1, source_target_pairs={{0,8},{4,12},{8,0},{12,4},{1,9},{5,13},{9,1},{13,5},{2,10},{6,14},... | collective-permute-start | bytes 4325384 | tf_op jit(solution)/shard_map/ppermute | solution.py:35
  161.6 34.0 %collective-permute-start.13 = (bf16[512,1408]{1,0:T(8,128)(2,1)}, bf16[512,1408]{1,0:T(8,128)(2,1)}, u32[]{:S(2)}, u32[]{:S(2)}) collective-permute-start(bf16[512,1408]{1,0:T(8,128)(2,1)} %branch.2), channel_id=1, source_target_pairs={{0,1},{1,0},{2,3},{3,2},{4,5},{5,4},{6,7},{7,6},{8,9},{9,8},{10,11... | collective-permute-start | bytes 4325384 | tf_op jit(solution)/shard_map/ppermute | solution.py:35
  201.0 33.0 %collective-permute-start.17 = (bf16[512,1408]{1,0:T(8,128)(2,1)S(1)}, bf16[512,1408]{1,0:T(8,128)(2,1)S(1)}, u32[]{:S(2)}, u32[]{:S(2)}) collective-permute-start(bf16[512,1408]{1,0:T(8,128)(2,1)S(1)} %multiply_convert_fusion.go), channel_id=1, source_target_pairs={{0,1},{1,0},{2,3},{3,2},{4,5},{5,4},{6,7},{7,6},{8,9},{9,8},{10,11... | collective-permute-start | bytes 4325384 | tf_op jit(solution)/shard_map/ppermute | solution.py:35
  207.3 33.9 %collective-permute-start.18 = (f32[8,128]{1,0:T(8,128)S(1)}, f32[8,128]{1,0:T(8,128)S(1)}, u32[]{:S(2)}, u32[]{:S(2)}) collective-permute-start(f32[8,128]{1,0:T(8,128)S(1)} %add.153), channel_id=1, source_target_pairs={{0,1},{1,0},{2,3},{3,2},{4,5},{5,4},{6,7},{7,6},{8,9},{9,8},{10,11... | collective-permute-start | bytes 12296 | tf_op jit(solution)/shard_map/ppermute | solution.py:35
  241.3 22.0 %collective-permute-start.21 = (bf16[352,1536]{1,0:T(8,128)(2,1)S(1)}, bf16[352,1536]{1,0:T(8,128)(2,1)S(1)}, u32[]{:S(2)}, u32[]{:S(2)}) collective-permute-start(bf16[352,1536]{1,0:T(8,128)(2,1)S(1)} %get-tuple-element.155), channel_id=1, source_target_pairs={{0,4},{4,0},{8,12},{12,8},{1,5},{5,1},{9,13},{13,9},{2,6},{6,2},{1... | collective-permute-start | bytes 3244040 | tf_op jit(solution)/shard_map/ppermute | solution.py:35
  244.3 19.1 %collective-permute-start.20 = (bf16[176,1536]{1,0:T(8,128)(2,1)S(1)}, bf16[176,1536]{1,0:T(8,128)(2,1)S(1)}, u32[]{:S(2)}, u32[]{:S(2)}) collective-permute-start(bf16[176,1536]{1,0:T(8,128)(2,1)S(1)} %get-tuple-element.204), channel_id=1, source_target_pairs={{0,8},{4,12},{8,0},{12,4},{1,9},{5,13},{9,1},{13,5},{2,10},{6,14},... | collective-permute-start | bytes 1622024 | tf_op jit(solution)/shard_map/ppermute | solution.py:35
  245.9 17.5 %collective-permute-start.22 = (f32[8,128]{1,0:T(8,128)S(1)}, f32[8,128]{1,0:T(8,128)S(1)}, u32[]{:S(2)}, u32[]{:S(2)}) collective-permute-start(f32[8,128]{1,0:T(8,128)S(1)} %add.154), channel_id=1, source_target_pairs={{0,2},{1,3},{2,0},{3,1},{4,6},{5,7},{6,4},{7,5},{8,10},{9,11},{10,... | collective-permute-start | bytes 12296 | tf_op jit(solution)/shard_map/ppermute | solution.py:35
  263.7 27.5 %collective-permute-start.25 = (bf16[352,1536]{1,0:T(8,128)(2,1)S(1)}, bf16[352,1536]{1,0:T(8,128)(2,1)S(1)}, u32[]{:S(2)}, u32[]{:S(2)}) collective-permute-start(bf16[352,1536]{1,0:T(8,128)(2,1)S(1)} %get-tuple-element.169), channel_id=1, source_target_pairs={{0,4},{4,0},{8,12},{12,8},{1,5},{5,1},{9,13},{13,9},{2,6},{6,2},{1... | collective-permute-start | bytes 3244040 | tf_op jit(solution)/shard_map/ppermute | solution.py:35
  264.2 14.3 %collective-permute-start.24 = (bf16[176,1536]{1,0:T(8,128)(2,1)S(1)}, bf16[176,1536]{1,0:T(8,128)(2,1)S(1)}, u32[]{:S(2)}, u32[]{:S(2)}) collective-permute-start(bf16[176,1536]{1,0:T(8,128)(2,1)S(1)} %get-tuple-element.203), channel_id=1, source_target_pairs={{0,8},{4,12},{8,0},{12,4},{1,9},{5,13},{9,1},{13,5},{2,10},{6,14},... | collective-permute-start | bytes 1622024 | tf_op jit(solution)/shard_map/ppermute | solution.py:35
  264.7 26.5 %collective-permute-start.26 = (bf16[176,1536]{1,0:T(8,128)(2,1)S(1)}, bf16[176,1536]{1,0:T(8,128)(2,1)S(1)}, u32[]{:S(2)}, u32[]{:S(2)}) collective-permute-start(bf16[176,1536]{1,0:T(8,128)(2,1)S(1)} %add_convert_fusion.7), channel_id=1, source_target_pairs={{0,2},{1,3},{2,0},{3,1},{4,6},{5,7},{6,4},{7,5},{8,10},{9,11},{10,... | collective-permute-start | bytes 1622024 | tf_op jit(solution)/shard_map/ppermute | solution.py:35
  291.5 4.2 %collective-permute-start.27 = (bf16[352,1536]{1,0:T(8,128)(2,1)S(1)}, bf16[352,1536]{1,0:T(8,128)(2,1)S(1)}, u32[]{:S(2)}, u32[]{:S(2)}) collective-permute-start(bf16[352,1536]{1,0:T(8,128)(2,1)S(1)} %get-tuple-element.173), channel_id=1, source_target_pairs={{0,4},{4,0},{8,12},{12,8},{1,5},{5,1},{9,13},{13,9},{2,6},{6,2},{1... | collective-permute-start | bytes 3244040 | tf_op jit(solution)/shard_map/ppermute | solution.py:35
  292.0 26.7 %collective-permute-start.29 = (bf16[352,1536]{1,0:T(8,128)(2,1)S(1)}, bf16[352,1536]{1,0:T(8,128)(2,1)S(1)}, u32[]{:S(2)}, u32[]{:S(2)}) collective-permute-start(bf16[352,1536]{1,0:T(8,128)(2,1)S(1)} %add_convert_fusion.3), channel_id=1, source_target_pairs={{0,8},{4,12},{8,0},{12,4},{1,9},{5,13},{9,1},{13,5},{2,10},{6,14},... | collective-permute-start | bytes 3244040 | tf_op jit(solution)/shard_map/ppermute | solution.py:35
  293.5 25.3 %collective-permute-start.30 = (bf16[176,1536]{1,0:T(8,128)(2,1)S(1)}, bf16[176,1536]{1,0:T(8,128)(2,1)S(1)}, u32[]{:S(2)}, u32[]{:S(2)}) collective-permute-start(bf16[176,1536]{1,0:T(8,128)(2,1)S(1)} %add_convert_fusion.6), channel_id=1, source_target_pairs={{0,2},{1,3},{2,0},{3,1},{4,6},{5,7},{6,4},{7,5},{8,10},{9,11},{10,... | collective-permute-start | bytes 1622024 | tf_op jit(solution)/shard_map/ppermute | solution.py:35
  319.1 27.3 %collective-permute-start.32 = (bf16[352,1536]{1,0:T(8,128)(2,1)S(1)}, bf16[352,1536]{1,0:T(8,128)(2,1)S(1)}, u32[]{:S(2)}, u32[]{:S(2)}) collective-permute-start(bf16[352,1536]{1,0:T(8,128)(2,1)S(1)} %get-tuple-element.189), channel_id=1, source_target_pairs={{0,4},{4,0},{8,12},{12,8},{1,5},{5,1},{9,13},{13,9},{2,6},{6,2},{1... | collective-permute-start | bytes 3244040 | tf_op jit(solution)/shard_map/ppermute | solution.py:35
  319.2 27.3 %collective-permute-start.31 = (bf16[352,1536]{1,0:T(8,128)(2,1)S(1)}, bf16[352,1536]{1,0:T(8,128)(2,1)S(1)}, u32[]{:S(2)}, u32[]{:S(2)}) collective-permute-start(bf16[352,1536]{1,0:T(8,128)(2,1)S(1)} %get-tuple-element.187), channel_id=1, source_target_pairs={{0,4},{4,0},{8,12},{12,8},{1,5},{5,1},{9,13},{13,9},{2,6},{6,2},{1... | collective-permute-start | bytes 3244040 | tf_op jit(solution)/shard_map/ppermute | solution.py:35
  319.7 26.8 %collective-permute-start.33 = (bf16[352,1536]{1,0:T(8,128)(2,1)S(1)}, bf16[352,1536]{1,0:T(8,128)(2,1)S(1)}, u32[]{:S(2)}, u32[]{:S(2)}) collective-permute-start(bf16[352,1536]{1,0:T(8,128)(2,1)S(1)} %add_convert_fusion.2), channel_id=1, source_target_pairs={{0,8},{4,12},{8,0},{12,4},{1,9},{5,13},{9,1},{13,5},{2,10},{6,14},... | collective-permute-start | bytes 3244040 | tf_op jit(solution)/shard_map/ppermute | solution.py:35
  320.3 26.2 %collective-permute-start.34 = (bf16[176,1536]{1,0:T(8,128)(2,1)S(1)}, bf16[176,1536]{1,0:T(8,128)(2,1)S(1)}, u32[]{:S(2)}, u32[]{:S(2)}) collective-permute-start(bf16[176,1536]{1,0:T(8,128)(2,1)S(1)} %get-tuple-element.202), channel_id=1, source_target_pairs={{0,2},{1,3},{2,0},{3,1},{4,6},{5,7},{6,4},{7,5},{8,10},{9,11},{10,... | collective-permute-start | bytes 1622024 | tf_op jit(solution)/shard_map/ppermute | solution.py:35
  346.7 28.0 %collective-permute-start.35 = (bf16[352,1536]{1,0:T(8,128)(2,1)S(1)}, bf16[352,1536]{1,0:T(8,128)(2,1)S(1)}, u32[]{:S(2)}, u32[]{:S(2)}) collective-permute-start(bf16[352,1536]{1,0:T(8,128)(2,1)S(1)} %add_convert_fusion.1), channel_id=1, source_target_pairs={{0,8},{4,12},{8,0},{12,4},{1,9},{5,13},{9,1},{13,5},{2,10},{6,14},... | collective-permute-start | bytes 3244040 | tf_op jit(solution)/shard_map/ppermute | solution.py:35
  349.4 25.3 %collective-permute-start.36 = (bf16[176,1536]{1,0:T(8,128)(2,1)S(1)}, bf16[176,1536]{1,0:T(8,128)(2,1)S(1)}, u32[]{:S(2)}, u32[]{:S(2)}) collective-permute-start(bf16[176,1536]{1,0:T(8,128)(2,1)S(1)} %get-tuple-element.201), channel_id=1, source_target_pairs={{0,2},{1,3},{2,0},{3,1},{4,6},{5,7},{6,4},{7,5},{8,10},{9,11},{10,... | collective-permute-start | bytes 1622024 | tf_op jit(solution)/shard_map/ppermute | solution.py:35
  (38 other events, 455.5 us)
Sparse Core Ops, SparseCore 0:
  9.6 38.1 all-gather.2
  49.4 37.5 all-gather.4

commit v3 on v2

--- a/solution.py
+++ b/solution.py
@@ -35,22 +35,31 @@
     return lax.ppermute(value, axis, [(i, i ^ bit) for i in range(count)])
 
 
+def piece_copies(pieces, offs_ref, parts, out, sems):
+    copies = []
+    for i, part in enumerate(parts):
+        first, count = pieces[i][1:3]
+        off = pl.multiple_of(offs_ref[i], 16)
+        copies.append(
+            pltpu.make_async_copy(
+                part.at[first : first + count, :], out.at[pl.ds(off, count), :], sems.at[i]
+            )
+        )
+    return copies
+
+
+def piece_offsets(pieces):
+    return jnp.stack([jnp.asarray(p[3], jnp.int32) for p in pieces])
+
+
 def assemble(pieces, rows):
     arrays = [p[0] for p in pieces]
     cols = arrays[0].shape[1]
-    offs = jnp.stack([jnp.asarray(p[3], jnp.int32) for p in pieces])
+    offs = piece_offsets(pieces)
 
     def body(offs_ref, *refs):
         parts, out, sems = refs[:-2], refs[-2], refs[-1]
-        copies = []
-        for i, part in enumerate(parts):
-            first, count = pieces[i][1:3]
-            off = pl.multiple_of(offs_ref[i], 16)
-            copies.append(
-                pltpu.make_async_copy(
-                    part.at[first : first + count, :], out.at[pl.ds(off, count), :], sems.at[i]
-                )
-            )
+        copies = piece_copies(pieces, offs_ref, parts, out, sems)
         for copy in copies:
             copy.start()
         for copy in copies:
@@ -170,7 +179,7 @@
         ],
         out_specs=pl.BlockSpec((step, width), lambda j: (j, 0)),
         out_shape=jax.ShapeDtypeStruct((count, width), BF16),
-        compiler_params=PARAMS,
+        compiler_params=LIGHT,
         cost_estimate=TINY,
         name="student_norm",
     )(student, gain)
@@ -202,41 +211,151 @@
     )(normed_own, normed_pair, weight)
 
 
-def branch_part(act_near, act_far, w_near, w_far, which, dtype):
-    toks = act_near.shape[0] // 2
-    cols = act_near.shape[1]
+def forward_pieces(normed_own, normed_pair, pieces):
+    toks = normed_own.shape[0]
+    cols = pieces[0][0].shape[1]
+    count = len(pieces)
+
+    def body(offs_ref, no, np_, *refs):
+        parts, (pre, act, w, sems) = refs[:count], refs[count:]
+        j = pl.program_id(0)
+
+        @pl.when(j == 0)
+        def _():
+            copies = piece_copies(pieces, offs_ref, parts, w, sems)
+            for copy in copies:
+                copy.start()
+            for copy in copies:
+                copy.wait()
+
+        chunk = w[:, pl.ds(pl.multiple_of(j * FC, FC), FC)]
+        for part, off in ((no, 0), (np_, toks)):
+            value = jnp.dot(part[...], chunk, preferred_element_type=F32)
+            pre[off : off + toks, :] = value
+            act[off : off + toks, :] = gelu_value(value).astype(BF16)
+
+    chunk = pl.BlockSpec((2 * toks, FC), lambda j: (0, j))
+    return pl.pallas_call(
+        body,
+        grid=(cols // FC,),
+        in_specs=[pl.BlockSpec(memory_space=pltpu.SMEM), whole((toks, DS)), whole((toks, DS))]
+        + [pl.BlockSpec(memory_space=pl.ANY)] * count,
+        out_specs=[chunk, chunk],
+        out_shape=[
+            jax.ShapeDtypeStruct((2 * toks, cols), F32),
+            jax.ShapeDtypeStruct((2 * toks, cols), BF16),
+        ],
+        scratch_shapes=[pltpu.VMEM((DS, cols), BF16), pltpu.SemaphoreType.DMA((count,))],
+        compiler_params=PARAMS,
+        cost_estimate=TINY,
+        name="forward_far",
+    )(piece_offsets(pieces), normed_own, normed_pair, *[p[0] for p in pieces])
+
+
+def branch_pieces(near, act, pieces, which, dtype):
+    toks = act.shape[0] // 2
+    cols = act.shape[1]
     step = 2 * FC
     n = cols // step
-
-    def body(an, af, wn, wf, out, acc):
+    count = len(pieces)
+
+    def body(offs_ref, nr, a, *refs):
+        parts, (out, acc, w, sems) = refs[:count], refs[count:]
         j = pl.program_id(0)
 
         @pl.when(j == 0)
         def _():
-            acc[...] = jnp.zeros_like(acc)
-
-        @pl.when(j < n)
-        def _():
-            acc[...] += nt(an[...], wn[...])
-
-        @pl.when(j >= n)
-        def _():
-            acc[...] += nt(af[...], wf[...])
-
-        @pl.when(j == 2 * n - 1)
+            copies = piece_copies(pieces, offs_ref, parts, w, sems)
+            for copy in copies:
+                copy.start()
+            acc[...] = nr[...]
+            for copy in copies:
+                copy.wait()
+
+        acc[...] += nt(a[...], w[:, pl.ds(pl.multiple_of(j * step, step), step)])
+
+        @pl.when(j == n - 1)
         def _():
             out[...] = acc[...].astype(out.dtype)
 
-    near = lambda j: jnp.minimum(j, n - 1)
-    far = lambda j: jnp.maximum(j - n, 0)
-    return pl.pallas_call(
-        body,
-        grid=(2 * n,),
+    return pl.pallas_call(
+        body,
+        grid=(n,),
         in_specs=[
-            pl.BlockSpec((toks, step), lambda j: (which, near(j))),
-            pl.BlockSpec((toks, step), lambda j: (which, far(j))),
-            pl.BlockSpec((DS, step), lambda j: (0, near(j))),
-            pl.BlockSpec((DS, step), lambda j: (0, far(j))),
+            pl.BlockSpec(memory_space=pltpu.SMEM),
+            pl.BlockSpec((toks, DS), lambda j: (which, 0)),
+            pl.BlockSpec((toks, step), lambda j: (which, j)),
+        ]
+        + [pl.BlockSpec(memory_space=pl.ANY)] * count,
+        out_specs=whole((toks, DS)),
+        out_shape=jax.ShapeDtypeStruct((toks, DS), dtype),
+        scratch_shapes=[
+            pltpu.VMEM((toks, DS), F32),
+            pltpu.VMEM((DS, cols), BF16),
+            pltpu.SemaphoreType.DMA((count,)),
+        ],
+        compiler_params=PARAMS,
+        cost_estimate=TINY,
+        name="branch_far",
+    )(piece_offsets(pieces), near, act, *[p[0] for p in pieces])
+
+
+def branch_near_part(act, weight):
+    count, cols = act.shape
+    step = 2 * FC
+
+    def body(a, w, out):
+        value = nt(a[...], w[...])
+
+        @pl.when(pl.program_id(0) == 0)
+        def _():
+            out[...] = value
+
+        @pl.when(pl.program_id(0) > 0)
+        def _():
+            out[...] += value
+
+    return pl.pallas_call(
+        body,
+        grid=(cols // step,),
+        in_specs=[
+            pl.BlockSpec((count, step), lambda j: (0, j)),
+            pl.BlockSpec((DS, step), lambda j: (0, j)),
+        ],
+        out_specs=whole((count, DS)),
+        out_shape=jax.ShapeDtypeStruct((count, DS), F32),
+        compiler_params=PARAMS,
+        cost_estimate=TINY,
+        name="branch_near",
+    )(act, weight)
+
+
+def branch_part(near, act, weight, which, dtype):
+    toks = act.shape[0] // 2
+    cols = act.shape[1]
+    step = 2 * FC
+    n = cols // step
+
+    def body(nr, a, w, out, acc):
+        j = pl.program_id(0)
+
+        @pl.when(j == 0)
+        def _():
+            acc[...] = nr[...]
+
+        acc[...] += nt(a[...], w[...])
+
+        @pl.when(j == n - 1)
+        def _():
+            out[...] = acc[...].astype(out.dtype)
+
+    return pl.pallas_call(
+        body,
+        grid=(n,),
+        in_specs=[
+            pl.BlockSpec((toks, DS), lambda j: (which, 0)),
+            pl.BlockSpec((toks, step), lambda j: (which, j)),
+            pl.BlockSpec((DS, step), lambda j: (0, j)),
         ],
         out_specs=whole((toks, DS)),
         out_shape=jax.ShapeDtypeStruct((toks, DS), dtype),
@@ -244,7 +363,7 @@
         compiler_params=PARAMS,
         cost_estimate=TINY,
         name="branch",
-    )(act_near, act_far, w_near, w_far)
+    )(near, act, weight)
 
 
 def store_blocks(mx, acc, scratch, outs):
@@ -392,10 +511,11 @@
     in_do = swap(d_g[:half], "group", 1)
     out_do = swap(z_o[half:], "mx", 2)
     zoc, dgc = swap(z_o, "mx", 1), swap(d_g, "mx", 1)
-    in_do, out_do, zoc, dgc = together(in_do, out_do, zoc, dgc)
+    t2 = (q2.astype(F32) + q3c.astype(F32)).astype(BF16)
+    near_share = branch_near_part(after(act_near, t2), out_near)
+    in_do, out_do, zoc, dgc, near_share = together(in_do, out_do, zoc, dgc, near_share)
     in_doc, out_doc = swap(in_do, "mx", 1), swap(out_do, "mx", 1)
-    t2 = (q2.astype(F32) + q3c.astype(F32)).astype(BF16)
-    in_doc, out_doc, t2 = together(in_doc, out_doc, t2)
+    in_doc, out_doc = together(in_doc, out_doc)
 
     def far_rows(first, d_o, d_oc):
         out = []
@@ -409,21 +529,19 @@
             out.append((part_c, at, half, (mx ^ block ^ 1) * rows + off))
         return out
 
-    in_far = assemble(far_rows(0, in_do, in_doc), DS)
-    target_x = swap(t2, "mx", 2)
+    target_x = swap(after(t2, in_doc), "mx", 2)
     q1c = swap(after(q1, in_doc), "mx", 1)
-    pre_far, act_far = forward_part(normed_own, normed_pair, in_far)
-    pre_far, act_far, q1c, out_doc = together(pre_far, act_far, q1c, out_doc)
-    out_far = assemble(far_rows(half, out_do, out_doc), DS)
+    pre_far, act_far = forward_pieces(normed_own, normed_pair, far_rows(0, in_do, in_doc))
+    pre_far, act_far, q1c = together(pre_far, act_far, q1c)
+    out_rows = far_rows(half, out_do, out_doc)
     t0 = q0.astype(F32) + q1c.astype(F32)
 
-    branch_pair = branch_part(act_near, act_far, out_near, out_far, 1, BF16)
+    branch_pair = branch_pieces(near_share, act_far, out_rows, 1, BF16)
     branch_recv = swap(branch_pair, "my", 1)
-    branch_own = branch_part(after(act_near, branch_pair), act_far, out_near, out_far, 0, F32)
+    out_far = assemble([(p, at, n, after(o, branch_pair)) for p, at, n, o in out_rows], DS)
+    branch_own = branch_part(near_share, act_far, out_far, 0, F32)
     slope_far = gelu_slope(after(pre_far, branch_own))
-    slope_near = gelu_slope(after(pre_near, slope_far))
-    normed_t = jnp.concatenate([after(normed_own, slope_near).T, normed_pair.T], axis=1)
-    branch_recv = after(branch_recv, normed_t)
+    branch_recv = after(branch_recv, slope_far)
 
     target = t0 + target_x.astype(F32)
     residue = student.astype(F32) + (branch_own + branch_recv.astype(F32)) - target
@@ -433,47 +551,51 @@
     grad_pair = swap(grad_own, "my", 1)
     for bit in (1, 2):
         loss = loss + swap(loss, "mx", bit)
-    grad_pair = after(grad_pair, loss)
-
-    loss_z = swap(loss, "my", 1)
+    slope_near = gelu_slope(after(pre_near, grad_own))
+    normed_t = jnp.concatenate([after(normed_own, slope_near).T, normed_pair.T], axis=1)
+    grad_pair, loss, slope_near, normed_t = together(grad_pair, loss, slope_near, normed_t)
+
     o0, o1, o2, o3 = grad_out_part(mx1, grad_own, grad_pair, act_far, True)
-    o0, o1, o2, o3, loss_z = together(o0, o1, o2, o3, loss_z)
-    loss = loss + loss_z
-    loss_z = swap(loss, "my", 2)
     got2, got0 = swap(o3, "mx", 1), swap(o1, "mx", 1)
-    h0, h1 = slice(0, half), slice(half, rows)
+    early = rows // 48 * 16 + 16
+    h0, h1 = slice(0, early), slice(early, rows)
     s2_out = [(o2[c].astype(F32) + got2[c].astype(F32)).astype(BF16) for c in (h0, h1)]
     x_out = [swap(v, "mx", 2) for v in s2_out]
-    i0, i1, i2, i3 = grad_in_part(
-        mx1, after(grad_own, *s2_out), grad_pair, out_far, slope_far, normed_t, True
-    )
-    i0, i1, i2, i3, x_out0, got0, loss_z = together(i0, i1, i2, i3, x_out[0], got0, loss_z)
-    mse_loss = (loss + loss_z)[0, :1] / (tokens * DS)
+    n0, n1, n2, n3 = grad_out_part(mx1, after(grad_own, *s2_out), grad_pair, act_near, True)
+    n0, n1, n2, n3, x_out0, got0 = together(n0, n1, n2, n3, x_out[0], got0)
 
     def last(keep, got, x):
         return (keep.astype(F32) + got.astype(F32) + x.astype(F32)).astype(BF16)
 
     f0 = last(o0[h0], got0[h0], x_out0)
     f_out0 = swap(f0, "my", 2)
-    gin2, gin0 = swap(after(i3, f0), "mx", 1), swap(after(i1, f0), "mx", 1)
+    gn2, gn0 = swap(after(n3, f0), "mx", 1), swap(after(n1, f0), "mx", 1)
+    i0, i1, i2, i3 = grad_in_part(
+        mx1, after(grad_own, f0), grad_pair, out_far, slope_far, normed_t, True
+    )
+    i0, i1, i2, i3, x_out1, gn2, gn0, f_out0 = together(
+        i0, i1, i2, i3, x_out[1], gn2, gn0, f_out0
+    )
+    f1 = last(o0[h1], got0[h1], x_out1)
+    f_out1 = swap(f1, "my", 2)
+    gin2, gin0 = swap(i3, "mx", 1), swap(i1, "mx", 1)
+    loss_z = swap(after(loss, f1), "my", 1)
+    s2_on = (n2.astype(F32) + gn2.astype(F32)).astype(BF16)
+    gin2, gin0, s2_on, loss_z = together(gin2, gin0, s2_on, loss_z)
+    loss = loss + loss_z
     s2_in = (i2.astype(F32) + gin2.astype(F32)).astype(BF16)
     x_in = swap(s2_in, "mx", 2)
-    n0, n1, n2, n3 = grad_out_part(mx1, after(grad_own, s2_in), grad_pair, act_near, True)
-    n0, n1, n2, n3, x_out1, gin0, f_out0 = together(n0, n1, n2, n3, x_out[1], gin0, f_out0)
-    f1 = last(o0[h1], got0[h1], x_out1)
-    f_out1 = swap(f1, "my", 2)
-    gn2, gn0 = swap(after(n3, f1), "mx", 1), swap(after(n1, f1), "mx", 1)
-    gn2, gn0 = together(gn2, gn0)
-    s2_on = (n2.astype(F32) + gn2.astype(F32)).astype(BF16)
-    x_on = swap(s2_on, "mx", 2)
+    x_on = swap(after(s2_on, s2_in), "mx", 2)
     m0, m1, m2, m3 = grad_in_part(
-        mx1, after(grad_own, s2_on), grad_pair, out_near, slope_near, normed_t, True
+        mx1, after(grad_own, s2_on, s2_in), grad_pair, out_near, slope_near, normed_t, True
     )
     m0, m1, m2, m3, x_in, f_out1 = together(m0, m1, m2, m3, x_in, f_out1)
     f2 = [last(i0[c], gin0[c], x_in[c]) for c in (h0, h1)]
     f_in = [swap(v, "my", 2) for v in f2]
     gm2, gm0 = swap(after(m3, *f2), "mx", 1), swap(after(m1, *f2), "mx", 1)
-    gm2, gm0, x_on, f_in0 = together(gm2, gm0, x_on, f_in[0])
+    loss_z = swap(after(loss, *f2), "my", 2)
+    gm2, gm0, x_on, f_in0, loss_z = together(gm2, gm0, x_on, f_in[0], loss_z)
+    mse_loss = (loss + loss_z)[0, :1] / (tokens * DS)
     s2_mn = (m2.astype(F32) + gm2.astype(F32)).astype(BF16)
     x_mn = swap(s2_mn, "mx", 2)
     grad_out_near = n0.astype(F32) + gn0.astype(F32) + x_on.astype(F32)

time: 386 us -> 371 us (0.961)
  waiting for transfers between devices: 157 us -> 137 us
  starting transfers between devices: 28.7 us -> 33 us
  Pallas kernels: 121 us -> 125 us
    ppermute x37, waiting for transfers between devices: 156 us -> 135 us  [swap(): return lax.ppermute(value, axis, [(i, i ^ bit) for i in range(count)])]
    pallas_call x2 -> x4, Pallas kernels: 22.4 us -> 39.7 us  [the longest x1 12 us: forward_pieces(): pl.pallas_call(body, grid=(cols // FC,), in_specs=[pl.BlockSpec(memory_sp...]
    pallas_call x2 -> x1, Pallas kernels: 21.6 us -> 10.8 us  [forward_part(): pl.pallas_call(body, grid=(cols // FC,), in_specs=[whole((toks, DS)), who...]
    pallas_call x2 -> x1, Pallas kernels: 9.9 us -> 4.97 us  [assemble(): pl.pallas_call(body, out_shape=jax.ShapeDtypeStruct((rows, cols), arrays[...]
    ppermute x37, starting transfers between devices: 28.6 us -> 32.9 us  [swap(): return lax.ppermute(value, axis, [(i, i ^ bit) for i in range(count)])]
  transfers between devices with their start and end apart: 39 -> 39, of which waited for: 19 -> 17; matrix products, arithmetic and copies ran while one was open for 9% -> 9% of each run, Pallas kernels for 31% -> 29%
where the time goes in v3:
time: 371 us; the launch traced here: 370 us
  waiting for transfers between devices  137 us (37%)
  Pallas kernels  125 us (34%)
  starting transfers between devices  33 us (9%)
  other arithmetic  28.4 us (8%)
  local copies, waits for them, and re-layouts  18.8 us (5%)
  between operations  16.2 us (4%)
  blocking collectives  12 us (3%)
    ppermute x37, waiting for transfers between devices, swap(): return lax.ppermute(value, axis, [(i, i ^ bit) for i in range(count)])  135 us
    ppermute x37, starting transfers between devices, swap(): return lax.ppermute(value, axis, [(i, i ^ bit) for i in range(count)])  32.9 us
    pallas_call x2, Pallas kernels, grad_in_part(): pl.pallas_call(body, grid=(cols // FC,), in_specs=[pl.BlockSpec(memory_sp...  27.1 us
    pallas_call x1, Pallas kernels, target_parts(): pl.pallas_call(body, grid_spec=pltpu.PrefetchScalarGridSpec(num_scalar_pr...  18.4 us
    pallas_call x2, Pallas kernels, grad_out_part(): pl.pallas_call(body, grid=(cols // FC,), in_specs=[pl.BlockSpec(memory_sp...  17.3 us
    add x2, other arithmetic, gelu_slope(): 0.5 * (1.0 + lax.erf(value * 0.7071067811865476))  12.8 us
    psum x1, blocking collectives, pair_shards(): sums = lax.psum(sums[:2], 'mx')  12 us
    pallas_call x1, Pallas kernels, forward_pieces(): pl.pallas_call(body, grid=(cols // FC,), in_specs=[pl.BlockSpec(memory_sp...  12 us
  transfers between devices with their start and end apart: 39, of which 17 were waited for; matrix products, arithmetic and copies ran while one was open for 9% of the time, Pallas kernels for 29%

profile of v3, /device:TPU:0, one launch (start us, length us, event | category | flops | bytes accessed | tf_op | source)
XLA Modules:
  0.0 370.0 jit_solution(2523843913346655719)
XLA Ops:
  13.1 3.0 collective-permute-start.1
  16.1 2.6 collective-permute-start
  18.7 5.5 %teacher_sums.1 = f32[8,2048]{1,0:T(8,128)} custom-call(bf16[2048,1536]{1,0:T(8,128)(2,1)} %bitcast.34), custom_call_target="tpu_custom_call" | custom-call | flops 1000 | bytes 1000 | tf_op jit(solution)/shard_map/teacher_sums/pallas_call | solution.py:102
  26.3 12.0 %psum.7.s_ref = f32[2,2048]{1,0:T(2,128)} all-reduce(f32[2,2048]{1,0:T(2,128)S(1)} %slice.72), channel_id=1, replica_groups=mesh['group'=2,'mx'=4,'my'=4] {'mx'}, use_global_device_ids=true, to_apply=%region_0.0 | all-reduce | flops 4096 | bytes 32768 | tf_op jit(solution)/shard_map/psum | solution.py:499
  38.3 18.4 %targets.1 = (bf16[512,1408]{1,0:T(8,128)(2,1)}, bf16[512,1408]{1,0:T(8,128)(2,1)}, bf16[512,1408]{1,0:T(8,128)(2,1)}, bf16[512,1408]{1,0:T(8,128)(2,1)}) custom-call(s32[1]{0:T(128)} %bitcast.2.mx_ref, bf16[2048,1536]{1,0:T(8,128)(2,1)} %bitcast.35, f32[2,2048]{1,0:T(2,128)} %psum.7.s_ref, f32[1,1536]{1,0:T(1,128)} %reshape.39.g_ref, ...), custom_call_target="tpu_custom_call" | custom-call | flops 1000 | bytes 1000 | tf_op jit(solution)/shard_map/targets/pallas_call | solution.py:137
  56.7 13.8 %collective-permute-done.refs_0_ = bf16[352,1536]{1,0:T(8,128)(2,1)} collective-permute-done((bf16[352,1536]{1,0:T(8,128)(2,1)}, bf16[352,1536]{1,0:T(8,128)(2,1)}, u32[]{:S(2)}, u32[]{:S(2)}) %collective-permute-start) | collective-permute-done | bytes 1081376 | tf_op jit(solution)/shard_map/ppermute | solution.py:35
  74.9 2.6 copy.12.np_
  77.5 10.8 %forward.1 = (f32[1024,1536]{1,0:T(8,128)}, bf16[1024,1536]{1,0:T(8,128)(2,1)}) custom-call(bf16[512,1408]{1,0:T(8,128)(2,1)} %copy-done, bf16[512,1408]{1,0:T(8,128)(2,1)} %copy.12.np_, bf16[1408,1536]{1,0:T(8,128)(2,1)} %all-gather.3.cloned.1.call-done.w), custom_call_target="tpu_custom_call" | custom-call | flops 1000 | bytes 1000 | tf_op jit(solution)/shard_map/forward/pallas_call | solution.py:199
  88.3 9.4 %collective-permute-done.3.refs_2_ = bf16[352,1536]{1,0:T(8,128)(2,1)S(1)} collective-permute-done((bf16[352,1536]{1,0:T(8,128)(2,1)}, bf16[352,1536]{1,0:T(8,128)(2,1)S(1)}, u32[]{:S(2)}, u32[]{:S(2)}) %collective-permute-start.3) | collective-permute-done | bytes 1081376 | tf_op jit(solution)/shard_map/ppermute | solution.py:35
  97.7 8.6 %collective-permute-done.2.refs_4_ = bf16[352,1536]{1,0:T(8,128)(2,1)} collective-permute-done((bf16[352,1536]{1,0:T(8,128)(2,1)}, bf16[352,1536]{1,0:T(8,128)(2,1)}, u32[]{:S(2)}, u32[]{:S(2)}) %collective-permute-start.2) | collective-permute-done | bytes 1081376 | tf_op jit(solution)/shard_map/ppermute | solution.py:35
  111.6 2.8 add_convert_fusion
  114.4 11.1 %branch_near.1.nr = f32[1024,1408]{1,0:T(8,128)} custom-call(bf16[1024,1536]{1,0:T(8,128)(2,1)} %get-tuple-element.127.a, bf16[1408,1536]{1,0:T(8,128)(2,1)} %all-gather.5.cloned.1.call-done.w), custom_call_target="tpu_custom_call" | custom-call | flops 1000 | bytes 1000 | tf_op jit(solution)/shard_map/branch_near/pallas_call | solution.py:318
  129.0 12.0 %forward_far.1 = (f32[1024,1536]{1,0:T(8,128)}, bf16[1024,1536]{1,0:T(8,128)(2,1)}) custom-call(s32[8]{0:T(128)} %stack.71.offs_ref, bf16[512,1408]{1,0:T(8,128)(2,1)} %copy-done, bf16[512,1408]{1,0:T(8,128)(2,1)} %copy.12.np_, bf16[352,1536]{1,0:T(8,128)(2,1)} %collective-permute-done.refs_0_, bf16[352,1536]{1,0:T(8,128)(2,1)} %collective-permute-done.4.refs_1_, ...), custom_call_target="tpu_custom_call" | custom-call | flops 1000 | bytes 1000 | tf_op jit(solution)/shard_map/forward_far/pallas_call | solution.py:238
  141.0 8.6 %branch_far.1 = bf16[512,1408]{1,0:T(8,128)(2,1)} custom-call(s32[8]{0:T(128)} %stack.71.offs_ref, f32[1024,1408]{1,0:T(8,128)} %branch_near.1.nr, bf16[1024,1536]{1,0:T(8,128)(2,1)} %get-tuple-element.139.a, bf16[352,1536]{1,0:T(8,128)(2,1)} %collective-permute-done.refs_0_, bf16[352,1536]{1,0:T(8,128)(2,1)} %collective-permute-done.4.refs_1_, ...), custom_call_target="tpu_custom_call" | custom-call | flops 1000 | bytes 1000 | tf_op jit(solution)/shard_map/branch_far/pallas_call | solution.py:281
  153.3 5.0 %assemble.1.w = bf16[1408,1536]{1,0:T(8,128)(2,1)} custom-call(s32[8]{0:T(128)} %stack.80.offs_ref, bf16[352,1536]{1,0:T(8,128)(2,1)} %collective-permute-done.refs_0_, bf16[352,1536]{1,0:T(8,128)(2,1)} %collective-permute-done.4.refs_1_, bf16[352,1536]{1,0:T(8,128)(2,1)} %copy-done.7, bf16[352,1536]{1,0:T(8,128)(2,1)} %collective-permute-done.8.refs_3_, ...), custom_call_target="tpu_custom_call" | custom-call | flops 1000 | bytes 1000 | tf_op jit(solution)/shard_map/assemble/pallas_call | solution.py:68
  158.3 8.0 %branch.1 = f32[512,1408]{1,0:T(8,128)} custom-call(f32[1024,1408]{1,0:T(8,128)} %branch_near.1.nr, bf16[1024,1536]{1,0:T(8,128)(2,1)} %get-tuple-element.139.a, bf16[1408,1536]{1,0:T(8,128)(2,1)} %assemble.1.w), custom_call_target="tpu_custom_call" | custom-call | flops 1000 | bytes 1000 | tf_op jit(solution)/shard_map/branch/pallas_call | solution.py:352
  166.3 8.5 %fusion.3.sl = f32[1024,1536]{1,0:T(8,128)} fusion(f32[1024,1536]{1,0:T(8,128)} %get-tuple-element.150), kind=kLoop, calls=%fused_computation.5 | loop fusion | flops 12582912 | bytes 12582912 | tf_op jit(solution)/shard_map/add | solution.py:28
  174.8 9.0 %collective-permute-done.13 = bf16[512,1408]{1,0:T(8,128)(2,1)S(1)} collective-permute-done((bf16[512,1408]{1,0:T(8,128)(2,1)}, bf16[512,1408]{1,0:T(8,128)(2,1)S(1)}, u32[]{:S(2)}, u32[]{:S(2)}) %collective-permute-start.13) | collective-permute-done | bytes 1441824 | tf_op jit(solution)/shard_map/ppermute | solution.py:35
  185.2 3.7 multiply_reduce_fusion
  190.4 4.3 %fusion.7.sl = f32[1024,1536]{1,0:T(8,128)} fusion(f32[1024,1536]{1,0:T(8,128)S(1)} %bitcast.37), kind=kLoop, calls=%fused_computation.9 | loop fusion | flops 12582912 | bytes 12582912 | tf_op jit(solution)/shard_map/add | solution.py:28
  200.0 22.7 %collective-permute-done.15.gp = bf16[512,1408]{1,0:T(8,128)(2,1)} collective-permute-done((bf16[512,1408]{1,0:T(8,128)(2,1)S(1)}, bf16[512,1408]{1,0:T(8,128)(2,1)}, u32[]{:S(2)}, u32[]{:S(2)}) %collective-permute-start.15) | collective-permute-done | bytes 1441824 | tf_op jit(solution)/shard_map/ppermute | solution.py:35
  222.6 8.6 %grad_out.2 = (bf16[352,1536]{1,0:T(8,128)(2,1)S(1)}, bf16[352,1536]{1,0:T(8,128)(2,1)S(1)}, bf16[352,1536]{1,0:T(8,128)(2,1)S(1)}, bf16[352,1536]{1,0:T(8,128)(2,1)S(1)}) custom-call(s32[1]{0:T(128)} %bitcast.2.mx_ref, bf16[512,1408]{1,0:T(8,128)(2,1)S(1)} %multiply_convert_fusion.go, bf16[512,1408]{1,0:T(8,128)(2,1)} %collective-permute-done.15.gp, ...), custom_call_target="tpu_custom_call" | custom-call | flops 1000 | bytes 1000 | tf_op jit(solution)/shard_map/grad_out/pallas_call | solution.py:403
  235.9 8.7 %grad_out.3 = (bf16[352,1536]{1,0:T(8,128)(2,1)S(1)}, bf16[352,1536]{1,0:T(8,128)(2,1)S(1)}, bf16[352,1536]{1,0:T(8,128)(2,1)S(1)}, bf16[352,1536]{1,0:T(8,128)(2,1)S(1)}) custom-call(s32[1]{0:T(128)} %bitcast.2.mx_ref, bf16[512,1408]{1,0:T(8,128)(2,1)S(1)} %multiply_convert_fusion.go, bf16[512,1408]{1,0:T(8,128)(2,1)} %collective-permute-done.15.gp, ...), custom_call_target="tpu_custom_call" | custom-call | flops 1000 | bytes 1000 | tf_op jit(solution)/shard_map/grad_out/pallas_call | solution.py:403
  250.0 2.8 copy-done.3
  252.7 13.5 %grad_in.2 = (bf16[352,1536]{1,0:T(8,128)(2,1)S(1)}, bf16[352,1536]{1,0:T(8,128)(2,1)S(1)}, bf16[352,1536]{1,0:T(8,128)(2,1)S(1)}, bf16[352,1536]{1,0:T(8,128)(2,1)S(1)}) custom-call(s32[1]{0:T(128)} %bitcast.2.mx_ref, bf16[512,1408]{1,0:T(8,128)(2,1)S(1)} %multiply_convert_fusion.go, bf16[512,1408]{1,0:T(8,128)(2,1)} %collective-permute-done.15.gp, ...), custom_call_target="tpu_custom_call" | custom-call | flops 1000 | bytes 1000 | tf_op jit(solution)/shard_map/grad_in/pallas_call | solution.py:434
  268.8 3.3 collective-permute-done.27
  277.7 13.5 %grad_in.3 = (bf16[352,1536]{1,0:T(8,128)(2,1)S(1)}, bf16[352,1536]{1,0:T(8,128)(2,1)S(1)}, bf16[352,1536]{1,0:T(8,128)(2,1)S(1)}, bf16[352,1536]{1,0:T(8,128)(2,1)S(1)}) custom-call(s32[1]{0:T(128)} %bitcast.2.mx_ref, bf16[512,1408]{1,0:T(8,128)(2,1)S(1)} %multiply_convert_fusion.go, bf16[512,1408]{1,0:T(8,128)(2,1)} %collective-permute-done.15.gp, ...), custom_call_target="tpu_custom_call" | custom-call | flops 1000 | bytes 1000 | tf_op jit(solution)/shard_map/grad_in/pallas_call | solution.py:434
  291.3 14.2 %collective-permute-done.29 = bf16[224,1536]{1,0:T(8,128)(2,1)S(1)} collective-permute-done((bf16[224,1536]{1,0:T(8,128)(2,1)S(1)}, bf16[224,1536]{1,0:T(8,128)(2,1)S(1)}, u32[]{:S(2)}, u32[]{:S(2)}) %collective-permute-start.29) | collective-permute-done | bytes 688160 | tf_op jit(solution)/shard_map/ppermute | solution.py:35
  306.5 2.9 collective-permute-start.34
  309.4 11.9 %collective-permute-done.32 = bf16[352,1536]{1,0:T(8,128)(2,1)S(1)} collective-permute-done((bf16[352,1536]{1,0:T(8,128)(2,1)S(1)}, bf16[352,1536]{1,0:T(8,128)(2,1)S(1)}, u32[]{:S(2)}, u32[]{:S(2)}) %collective-permute-start.32) | collective-permute-done | bytes 1081376 | tf_op jit(solution)/shard_map/ppermute | solution.py:35
  321.4 4.5 %collective-permute-done.34 = f32[8,128]{1,0:T(8,128)S(1)} collective-permute-done((f32[8,128]{1,0:T(8,128)S(1)}, f32[8,128]{1,0:T(8,128)S(1)}, u32[]{:S(2)}, u32[]{:S(2)}) %collective-permute-start.34) | collective-permute-done | bytes 4128 | tf_op jit(solution)/shard_map/ppermute | solution.py:35
  330.7 29.5 %collective-permute-done.36 = bf16[224,1536]{1,0:T(8,128)(2,1)S(1)} collective-permute-done((bf16[224,1536]{1,0:T(8,128)(2,1)S(1)}, bf16[224,1536]{1,0:T(8,128)(2,1)S(1)}, u32[]{:S(2)}, u32[]{:S(2)}) %collective-permute-start.36) | collective-permute-done | bytes 688160 | tf_op jit(solution)/shard_map/ppermute | solution.py:35
  (152 shorter events, 57.9 us)
Async XLA Ops:
  7.2 70.3 %all-gather.3.cloned.1.call-start = ((), (), s32[]{:S(2)}) async-start(), calls=%async_computation | async-start | bytes 5406720 | tf_op jit(solution)/shard_map/all_gather | solution.py:491
  7.9 106.4 %all-gather.5.cloned.1.call-start = ((), (), s32[]{:S(2)}) async-start(), calls=%async_computation.1 | async-start | bytes 5406720 | tf_op jit(solution)/shard_map/all_gather | solution.py:492
  13.1 58.1 %collective-permute-start.1 = (bf16[512,1408]{0,1:T(8,128)(2,1)}, bf16[512,1408]{0,1:T(8,128)(2,1)}, u32[]{:S(2)}, u32[]{:S(2)}) collective-permute-start(bf16[512,1408]{0,1:T(8,128)(2,1)} %copy.11), channel_id=1, source_target_pairs={{0,1},{1,0},{2,3},{3,2},{4,5},{5,4},{6,7},{7,6},{8,9},{9,8},{10,11... | collective-permute-start | bytes 4325384 | tf_op jit(solution)/shard_map/ppermute | solution.py:35
  16.1 54.3 %collective-permute-start = (bf16[352,1536]{1,0:T(8,128)(2,1)}, bf16[352,1536]{1,0:T(8,128)(2,1)}, u32[]{:S(2)}, u32[]{:S(2)}) collective-permute-start(bf16[352,1536]{1,0:T(8,128)(2,1)} %pad_maximum_fusion.1), channel_id=1, source_target_pairs={{0,2},{1,3},{2,0},{3,1},{4,6},{5,7},{6,4},{7,5},{8,10},{9,11},{10,... | collective-permute-start | bytes 3244040 | tf_op jit(solution)/shard_map/ppermute | solution.py:35
  71.2 35.1 %collective-permute-start.5 = (bf16[512,1408]{1,0:T(8,128)(2,1)}, bf16[512,1408]{1,0:T(8,128)(2,1)}, u32[]{:S(2)}, u32[]{:S(2)}) collective-permute-start(bf16[512,1408]{1,0:T(8,128)(2,1)} %get-tuple-element.121), channel_id=1, source_target_pairs={{0,4},{4,0},{8,12},{12,8},{1,5},{5,1},{9,13},{13,9},{2,6},{6,2},{1... | collective-permute-start | bytes 4325384 | tf_op jit(solution)/shard_map/ppermute | solution.py:35
  71.2 17.1 %collective-permute-start.4 = (bf16[352,1536]{1,0:T(8,128)(2,1)}, bf16[352,1536]{1,0:T(8,128)(2,1)}, u32[]{:S(2)}, u32[]{:S(2)}) collective-permute-start(bf16[352,1536]{1,0:T(8,128)(2,1)} %collective-permute-done.refs_0_), channel_id=1, source_target_pairs={{0,4},{4,0},{8,12},{12,8},{1,5},{5,1},{9,13},{13,9},{2,6},{6,2},{1... | collective-permute-start | bytes 3244040 | tf_op jit(solution)/shard_map/ppermute | solution.py:35
  71.7 26.0 %collective-permute-start.3 = (bf16[352,1536]{1,0:T(8,128)(2,1)}, bf16[352,1536]{1,0:T(8,128)(2,1)S(1)}, u32[]{:S(2)}, u32[]{:S(2)}) collective-permute-start(bf16[352,1536]{1,0:T(8,128)(2,1)} %collective-permute-done.refs_0_), channel_id=1, source_target_pairs={{0,16},{16,0},{1,17},{17,1},{2,18},{18,2},{3,19},{19,3},{4,20},{20... | collective-permute-start | bytes 3244040 | tf_op jit(solution)/shard_map/ppermute | solution.py:35
  73.4 32.9 %collective-permute-start.2 = (bf16[352,1536]{1,0:T(8,128)(2,1)}, bf16[352,1536]{1,0:T(8,128)(2,1)}, u32[]{:S(2)}, u32[]{:S(2)}) collective-permute-start(bf16[352,1536]{1,0:T(8,128)(2,1)} %collective-permute-done.refs_0_), channel_id=1, source_target_pairs={{0,8},{4,12},{8,0},{12,4},{1,9},{5,13},{9,1},{13,5},{2,10},{6,14},... | collective-permute-start | bytes 3244040 | tf_op jit(solution)/shard_map/ppermute | solution.py:35
  106.3 19.2 %collective-permute-start.9 = (bf16[352,1536]{1,0:T(8,128)(2,1)}, bf16[352,1536]{1,0:T(8,128)(2,1)}, u32[]{:S(2)}, u32[]{:S(2)}) collective-permute-start(bf16[352,1536]{1,0:T(8,128)(2,1)} %collective-permute-done.2.refs_4_), channel_id=1, source_target_pairs={{0,4},{4,0},{8,12},{12,8},{1,5},{5,1},{9,13},{13,9},{2,6},{6,2},{1... | collective-permute-start | bytes 3244040 | tf_op jit(solution)/shard_map/ppermute | solution.py:35
  106.3 19.2 %collective-permute-start.8 = (bf16[352,1536]{1,0:T(8,128)(2,1)S(1)}, bf16[352,1536]{1,0:T(8,128)(2,1)}, u32[]{:S(2)}, u32[]{:S(2)}) collective-permute-start(bf16[352,1536]{1,0:T(8,128)(2,1)S(1)} %collective-permute-done.3.refs_2_), channel_id=1, source_target_pairs={{0,4},{4,0},{8,12},{12,8},{1,5},{5,1},{9,13},{13,9},{2,6},{6,2},{1... | collective-permute-start | bytes 3244040 | tf_op jit(solution)/shard_map/ppermute | solution.py:35
  109.5 15.9 %collective-permute-start.7 = (bf16[176,1536]{1,0:T(8,128)(2,1)}, bf16[176,1536]{1,0:T(8,128)(2,1)S(1)}, u32[]{:S(2)}, u32[]{:S(2)}) collective-permute-start(bf16[176,1536]{1,0:T(8,128)(2,1)} %slice.56), channel_id=1, source_target_pairs={{0,8},{4,12},{8,0},{12,4},{1,9},{5,13},{9,1},{13,5},{2,10},{6,14},... | collective-permute-start | bytes 1622024 | tf_op jit(solution)/shard_map/ppermute | solution.py:35
  109.8 15.6 %collective-permute-start.6 = (bf16[176,1536]{1,0:T(8,128)(2,1)}, bf16[176,1536]{1,0:T(8,128)(2,1)}, u32[]{:S(2)}, u32[]{:S(2)}) collective-permute-start(bf16[176,1536]{1,0:T(8,128)(2,1)} %slice.55), channel_id=1, source_target_pairs={{0,16},{16,0},{1,17},{17,1},{2,18},{18,2},{3,19},{19,3},{4,20},{20... | collective-permute-start | bytes 1622024 | tf_op jit(solution)/shard_map/ppermute | solution.py:35
  128.3 12.8 %collective-permute-start.12 = (bf16[512,1408]{1,0:T(8,128)(2,1)}, bf16[512,1408]{1,0:T(8,128)(2,1)}, u32[]{:S(2)}, u32[]{:S(2)}) collective-permute-start(bf16[512,1408]{1,0:T(8,128)(2,1)} %get-tuple-element.138), channel_id=1, source_target_pairs={{0,4},{4,0},{8,12},{12,8},{1,5},{5,1},{9,13},{13,9},{2,6},{6,2},{1... | collective-permute-start | bytes 4325384 | tf_op jit(solution)/shard_map/ppermute | solution.py:35
  149.7 34.1 %collective-permute-start.13 = (bf16[512,1408]{1,0:T(8,128)(2,1)}, bf16[512,1408]{1,0:T(8,128)(2,1)S(1)}, u32[]{:S(2)}, u32[]{:S(2)}) collective-permute-start(bf16[512,1408]{1,0:T(8,128)(2,1)} %branch_far.1), channel_id=1, source_target_pairs={{0,1},{1,0},{2,3},{3,2},{4,5},{5,4},{6,7},{7,6},{8,9},{9,8},{10,11... | collective-permute-start | bytes 4325384 | tf_op jit(solution)/shard_map/ppermute | solution.py:35
  151.3 33.9 %collective-permute-start.14 = (bf16[512,1408]{1,0:T(8,128)(2,1)}, bf16[512,1408]{1,0:T(8,128)(2,1)}, u32[]{:S(2)}, u32[]{:S(2)}) collective-permute-start(bf16[512,1408]{1,0:T(8,128)(2,1)} %add_convert_fusion), channel_id=1, source_target_pairs={{0,8},{4,12},{8,0},{12,4},{1,9},{5,13},{9,1},{13,5},{2,10},{6,14},... | collective-permute-start | bytes 4325384 | tf_op jit(solution)/shard_map/ppermute | solution.py:35
  189.7 32.9 %collective-permute-start.15 = (bf16[512,1408]{1,0:T(8,128)(2,1)S(1)}, bf16[512,1408]{1,0:T(8,128)(2,1)}, u32[]{:S(2)}, u32[]{:S(2)}) collective-permute-start(bf16[512,1408]{1,0:T(8,128)(2,1)S(1)} %multiply_convert_fusion.go), channel_id=1, source_target_pairs={{0,1},{1,0},{2,3},{3,2},{4,5},{5,4},{6,7},{7,6},{8,9},{9,8},{10,11... | collective-permute-start | bytes 4325384 | tf_op jit(solution)/shard_map/ppermute | solution.py:35
  190.3 5.8 %collective-permute-start.16 = (f32[8,128]{1,0:T(8,128)S(1)}, f32[8,128]{1,0:T(8,128)S(1)}, u32[]{:S(2)}, u32[]{:S(2)}) collective-permute-start(f32[8,128]{1,0:T(8,128)S(1)} %broadcast_in_dim.3), channel_id=1, source_target_pairs={{0,4},{4,0},{8,12},{12,8},{1,5},{5,1},{9,13},{13,9},{2,6},{6,2},{1... | collective-permute-start | bytes 12296 | tf_op jit(solution)/shard_map/ppermute | solution.py:35
  231.3 13.3 %collective-permute-start.20 = (bf16[352,1536]{1,0:T(8,128)(2,1)S(1)}, bf16[352,1536]{1,0:T(8,128)(2,1)S(1)}, u32[]{:S(2)}, u32[]{:S(2)}) collective-permute-start(bf16[352,1536]{1,0:T(8,128)(2,1)S(1)} %get-tuple-element.170), channel_id=1, source_target_pairs={{0,4},{4,0},{8,12},{12,8},{1,5},{5,1},{9,13},{13,9},{2,6},{6,2},{1... | collective-permute-start | bytes 3244040 | tf_op jit(solution)/shard_map/ppermute | solution.py:35
  234.1 11.2 %collective-permute-start.19 = (bf16[128,1536]{1,0:T(8,128)(2,1)S(1)}, bf16[128,1536]{1,0:T(8,128)(2,1)S(1)}, u32[]{:S(2)}, u32[]{:S(2)}) collective-permute-start(bf16[128,1536]{1,0:T(8,128)(2,1)S(1)} %add_convert_fusion.9), channel_id=1, source_target_pairs={{0,8},{4,12},{8,0},{12,4},{1,9},{5,13},{9,1},{13,5},{2,10},{6,14},... | collective-permute-start | bytes 1179656 | tf_op jit(solution)/shard_map/ppermute | solution.py:35
  245.5 22.2 %collective-permute-start.22 = (bf16[352,1536]{1,0:T(8,128)(2,1)S(1)}, bf16[352,1536]{1,0:T(8,128)(2,1)S(1)}, u32[]{:S(2)}, u32[]{:S(2)}) collective-permute-start(bf16[352,1536]{1,0:T(8,128)(2,1)S(1)} %get-tuple-element.180), channel_id=1, source_target_pairs={{0,4},{4,0},{8,12},{12,8},{1,5},{5,1},{9,13},{13,9},{2,6},{6,2},{1... | collective-permute-start | bytes 3244040 | tf_op jit(solution)/shard_map/ppermute | solution.py:35
  245.6 22.1 %collective-permute-start.23 = (bf16[352,1536]{1,0:T(8,128)(2,1)S(1)}, bf16[352,1536]{1,0:T(8,128)(2,1)S(1)}, u32[]{:S(2)}, u32[]{:S(2)}) collective-permute-start(bf16[352,1536]{1,0:T(8,128)(2,1)S(1)} %get-tuple-element.182), channel_id=1, source_target_pairs={{0,4},{4,0},{8,12},{12,8},{1,5},{5,1},{9,13},{13,9},{2,6},{6,2},{1... | collective-permute-start | bytes 3244040 | tf_op jit(solution)/shard_map/ppermute | solution.py:35
  246.1 20.2 %collective-permute-start.21 = (bf16[224,1536]{1,0:T(8,128)(2,1)S(1)}, bf16[224,1536]{1,0:T(8,128)(2,1)S(1)}, u32[]{:S(2)}, u32[]{:S(2)}) collective-permute-start(bf16[224,1536]{1,0:T(8,128)(2,1)S(1)} %add_convert_fusion.6), channel_id=1, source_target_pairs={{0,8},{4,12},{8,0},{12,4},{1,9},{5,13},{9,1},{13,5},{2,10},{6,14},... | collective-permute-start | bytes 2064392 | tf_op jit(solution)/shard_map/ppermute | solution.py:35
  247.6 20.1 %collective-permute-start.24 = (bf16[128,1536]{1,0:T(8,128)(2,1)S(1)}, bf16[128,1536]{1,0:T(8,128)(2,1)S(1)}, u32[]{:S(2)}, u32[]{:S(2)}) collective-permute-start(bf16[128,1536]{1,0:T(8,128)(2,1)S(1)} %add_convert_fusion.8), channel_id=1, source_target_pairs={{0,2},{1,3},{2,0},{3,1},{4,6},{5,7},{6,4},{7,5},{8,10},{9,11},{10,... | collective-permute-start | bytes 1179656 | tf_op jit(solution)/shard_map/ppermute | solution.py:35
  272.4 33.1 %collective-permute-start.28 = (bf16[352,1536]{1,0:T(8,128)(2,1)S(1)}, bf16[352,1536]{1,0:T(8,128)(2,1)S(1)}, u32[]{:S(2)}, u32[]{:S(2)}) collective-permute-start(bf16[352,1536]{1,0:T(8,128)(2,1)S(1)} %add_convert_fusion.2), channel_id=1, source_target_pairs={{0,8},{4,12},{8,0},{12,4},{1,9},{5,13},{9,1},{13,5},{2,10},{6,14},... | collective-permute-start | bytes 3244040 | tf_op jit(solution)/shard_map/ppermute | solution.py:35
  273.1 32.5 %collective-permute-start.29 = (bf16[224,1536]{1,0:T(8,128)(2,1)S(1)}, bf16[224,1536]{1,0:T(8,128)(2,1)S(1)}, u32[]{:S(2)}, u32[]{:S(2)}) collective-permute-start(bf16[224,1536]{1,0:T(8,128)(2,1)S(1)} %add_convert_fusion.5), channel_id=1, source_target_pairs={{0,2},{1,3},{2,0},{3,1},{4,6},{5,7},{6,4},{7,5},{8,10},{9,11},{10,... | collective-permute-start | bytes 2064392 | tf_op jit(solution)/shard_map/ppermute | solution.py:35
  274.0 47.3 %collective-permute-start.32 = (bf16[352,1536]{1,0:T(8,128)(2,1)S(1)}, bf16[352,1536]{1,0:T(8,128)(2,1)S(1)}, u32[]{:S(2)}, u32[]{:S(2)}) collective-permute-start(bf16[352,1536]{1,0:T(8,128)(2,1)S(1)} %add_convert_fusion.3), channel_id=1, source_target_pairs={{0,8},{4,12},{8,0},{12,4},{1,9},{5,13},{9,1},{13,5},{2,10},{6,14},... | collective-permute-start | bytes 3244040 | tf_op jit(solution)/shard_map/ppermute | solution.py:35
  305.9 19.9 %collective-permute-start.30 = (bf16[352,1536]{1,0:T(8,128)(2,1)S(1)}, bf16[352,1536]{1,0:T(8,128)(2,1)S(1)}, u32[]{:S(2)}, u32[]{:S(2)}) collective-permute-start(bf16[352,1536]{1,0:T(8,128)(2,1)S(1)} %get-tuple-element.203), channel_id=1, source_target_pairs={{0,4},{4,0},{8,12},{12,8},{1,5},{5,1},{9,13},{13,9},{2,6},{6,2},{1... | collective-permute-start | bytes 3244040 | tf_op jit(solution)/shard_map/ppermute | solution.py:35
  306.0 19.8 %collective-permute-start.31 = (bf16[352,1536]{1,0:T(8,128)(2,1)S(1)}, bf16[352,1536]{1,0:T(8,128)(2,1)S(1)}, u32[]{:S(2)}, u32[]{:S(2)}) collective-permute-start(bf16[352,1536]{1,0:T(8,128)(2,1)S(1)} %get-tuple-element.205), channel_id=1, source_target_pairs={{0,4},{4,0},{8,12},{12,8},{1,5},{5,1},{9,13},{13,9},{2,6},{6,2},{1... | collective-permute-start | bytes 3244040 | tf_op jit(solution)/shard_map/ppermute | solution.py:35
  306.5 19.3 %collective-permute-start.33 = (bf16[128,1536]{1,0:T(8,128)(2,1)S(1)}, bf16[128,1536]{1,0:T(8,128)(2,1)S(1)}, u32[]{:S(2)}, u32[]{:S(2)}) collective-permute-start(bf16[128,1536]{1,0:T(8,128)(2,1)S(1)} %add_convert_fusion.7), channel_id=1, source_target_pairs={{0,2},{1,3},{2,0},{3,1},{4,6},{5,7},{6,4},{7,5},{8,10},{9,11},{10,... | collective-permute-start | bytes 1179656 | tf_op jit(solution)/shard_map/ppermute | solution.py:35
  306.5 19.3 %collective-permute-start.34 = (f32[8,128]{1,0:T(8,128)S(1)}, f32[8,128]{1,0:T(8,128)S(1)}, u32[]{:S(2)}, u32[]{:S(2)}) collective-permute-start(f32[8,128]{1,0:T(8,128)S(1)} %add.161), channel_id=1, source_target_pairs={{0,2},{1,3},{2,0},{3,1},{4,6},{5,7},{6,4},{7,5},{8,10},{9,11},{10,... | collective-permute-start | bytes 12296 | tf_op jit(solution)/shard_map/ppermute | solution.py:35
  326.1 34.1 %collective-permute-start.35 = (bf16[352,1536]{1,0:T(8,128)(2,1)S(1)}, bf16[352,1536]{1,0:T(8,128)(2,1)S(1)}, u32[]{:S(2)}, u32[]{:S(2)}) collective-permute-start(bf16[352,1536]{1,0:T(8,128)(2,1)S(1)} %add_convert_fusion.1), channel_id=1, source_target_pairs={{0,8},{4,12},{8,0},{12,4},{1,9},{5,13},{9,1},{13,5},{2,10},{6,14},... | collective-permute-start | bytes 3244040 | tf_op jit(solution)/shard_map/ppermute | solution.py:35
  327.6 32.5 %collective-permute-start.36 = (bf16[224,1536]{1,0:T(8,128)(2,1)S(1)}, bf16[224,1536]{1,0:T(8,128)(2,1)S(1)}, u32[]{:S(2)}, u32[]{:S(2)}) collective-permute-start(bf16[224,1536]{1,0:T(8,128)(2,1)S(1)} %add_convert_fusion.4), channel_id=1, source_target_pairs={{0,2},{1,3},{2,0},{3,1},{4,6},{5,7},{6,4},{7,5},{8,10},{9,11},{10,... | collective-permute-start | bytes 2064392 | tf_op jit(solution)/shard_map/ppermute | solution.py:35
  (32 other events, 316.0 us)
Sparse Core Ops, SparseCore 0:
  9.6 38.1 all-gather.2
  49.4 42.1 all-gather.4

commit v4 on v3

--- a/solution.py
+++ b/solution.py
@@ -187,11 +187,11 @@
 
 def forward_part(normed_own, normed_pair, weight):
     toks = normed_own.shape[0]
-    cols = weight.shape[1]
+    cols = weight.shape[-1]
 
     def body(no, np_, w, pre, act):
         for part, off in ((no, 0), (np_, toks)):
-            value = jnp.dot(part[...], w[...], preferred_element_type=F32)
+            value = jnp.dot(part[...], flat(w), preferred_element_type=F32)
             pre[off : off + toks, :] = value
             act[off : off + toks, :] = gelu_value(value).astype(BF16)
 
@@ -199,7 +199,7 @@
     return pl.pallas_call(
         body,
         grid=(cols // FC,),
-        in_specs=[whole((toks, DS)), whole((toks, DS)), pl.BlockSpec((DS, FC), lambda j: (0, j))],
+        in_specs=[whole((toks, DS)), whole((toks, DS)), weight_spec(weight, 0, FC)],
         out_specs=[chunk, chunk],
         out_shape=[
             jax.ShapeDtypeStruct((2 * toks, cols), F32),
@@ -300,12 +300,22 @@
     )(piece_offsets(pieces), near, act, *[p[0] for p in pieces])
 
 
+def weight_spec(weight, which, width):
+    if weight.ndim == 2:
+        return pl.BlockSpec((DS, width), lambda j: (0, j))
+    return pl.BlockSpec((4, 1, DS // 4, width), lambda j: (0, which, 0, j))
+
+
+def flat(w):
+    return w[...].reshape(DS, w.shape[-1])
+
+
 def branch_near_part(act, weight):
     count, cols = act.shape
     step = 2 * FC
 
     def body(a, w, out):
-        value = nt(a[...], w[...])
+        value = nt(a[...], flat(w))
 
         @pl.when(pl.program_id(0) == 0)
         def _():
@@ -320,7 +330,7 @@
         grid=(cols // step,),
         in_specs=[
             pl.BlockSpec((count, step), lambda j: (0, j)),
-            pl.BlockSpec((DS, step), lambda j: (0, j)),
+            weight_spec(weight, 1, step),
         ],
         out_specs=whole((count, DS)),
         out_shape=jax.ShapeDtypeStruct((count, DS), F32),
@@ -420,13 +430,13 @@
 
 def grad_in_part(mx, grad_own, grad_pair, w_out, slope, normed_t, split):
     toks = grad_own.shape[0]
-    cols = w_out.shape[1]
+    cols = w_out.shape[-1]
     specs, shapes = block_outs(split, cols)
 
     def body(mx_ref, go, gp, w, sl, nrm, *rest):
         outs, (pre, scratch) = rest[:-2], rest[-2:]
         for part, off in ((go, 0), (gp, toks)):
-            act_grad = jnp.dot(part[...], w[...], preferred_element_type=F32)
+            act_grad = jnp.dot(part[...], flat(w), preferred_element_type=F32)
             pre[off : off + toks, :] = (act_grad * sl[off : off + toks, :]).astype(BF16)
         acc = jnp.dot(nrm[...], pre[...], preferred_element_type=F32)
         store_blocks(mx_ref[0], acc, scratch, outs)
@@ -438,7 +448,7 @@
             pl.BlockSpec(memory_space=pltpu.SMEM),
             whole((toks, DS)),
             whole((toks, DS)),
-            pl.BlockSpec((DS, FC), lambda j: (0, j)),
+            weight_spec(w_out, 1, FC),
             pl.BlockSpec((2 * toks, FC), lambda j: (0, j)),
             whole((DS, 2 * toks)),
         ],
@@ -488,8 +498,8 @@
 
     z_send = jnp.concatenate([my_half(w_in), my_half(w_out)], axis=0)
     z_g = swap(z_send, "my", 2)
-    in_near = lax.all_gather(w_in, "mx", axis=0, tiled=True)
-    out_near = lax.all_gather(w_out, "mx", axis=0, tiled=True)
+    near = lax.all_gather(jnp.concatenate([w_in, w_out], axis=0), "mx", axis=0, tiled=True)
+    near = near.reshape(4, 2, rows, cols)
 
     feats = teacher_feats.reshape(4 * toks, feat_loc)
     student = student_in.reshape(toks, DS)
@@ -506,13 +516,13 @@
     z_o = swap(z_g, "group", 1)
     zgc = swap(z_g, "mx", 1)
     q3c = swap(q3, "mx", 1)
-    pre_near, act_near = forward_part(normed_own, normed_pair, in_near)
+    pre_near, act_near = forward_part(normed_own, normed_pair, near)
     pre_near, act_near, d_g, z_o, zgc, q3c = together(pre_near, act_near, d_g, z_o, zgc, q3c)
     in_do = swap(d_g[:half], "group", 1)
     out_do = swap(z_o[half:], "mx", 2)
     zoc, dgc = swap(z_o, "mx", 1), swap(d_g, "mx", 1)
     t2 = (q2.astype(F32) + q3c.astype(F32)).astype(BF16)
-    near_share = branch_near_part(after(act_near, t2), out_near)
+    near_share = branch_near_part(after(act_near, t2), near)
     in_do, out_do, zoc, dgc, near_share = together(in_do, out_do, zoc, dgc, near_share)
     in_doc, out_doc = swap(in_do, "mx", 1), swap(out_do, "mx", 1)
     in_doc, out_doc = together(in_doc, out_doc)
@@ -577,19 +587,19 @@
         i0, i1, i2, i3, x_out[1], gn2, gn0, f_out0
     )
     f1 = last(o0[h1], got0[h1], x_out1)
-    f_out1 = swap(f1, "my", 2)
+    f_out1, f_out2 = (swap(f1[c], "my", 2) for c in (slice(0, 48), slice(48, None)))
     gin2, gin0 = swap(i3, "mx", 1), swap(i1, "mx", 1)
     loss_z = swap(after(loss, f1), "my", 1)
     s2_on = (n2.astype(F32) + gn2.astype(F32)).astype(BF16)
-    gin2, gin0, s2_on, loss_z = together(gin2, gin0, s2_on, loss_z)
+    gin2, gin0, s2_on, loss_z, f_out1 = together(gin2, gin0, s2_on, loss_z, f_out1)
     loss = loss + loss_z
     s2_in = (i2.astype(F32) + gin2.astype(F32)).astype(BF16)
     x_in = swap(s2_in, "mx", 2)
     x_on = swap(after(s2_on, s2_in), "mx", 2)
     m0, m1, m2, m3 = grad_in_part(
-        mx1, after(grad_own, s2_on, s2_in), grad_pair, out_near, slope_near, normed_t, True
-    )
-    m0, m1, m2, m3, x_in, f_out1 = together(m0, m1, m2, m3, x_in, f_out1)
+        mx1, after(grad_own, s2_on, s2_in), grad_pair, near, slope_near, normed_t, True
+    )
+    m0, m1, m2, m3, x_in, f_out2 = together(m0, m1, m2, m3, x_in, f_out2)
     f2 = [last(i0[c], gin0[c], x_in[c]) for c in (h0, h1)]
     f_in = [swap(v, "my", 2) for v in f2]
     gm2, gm0 = swap(after(m3, *f2), "mx", 1), swap(after(m1, *f2), "mx", 1)
@@ -600,7 +610,7 @@
     x_mn = swap(s2_mn, "mx", 2)
     grad_out_near = n0.astype(F32) + gn0.astype(F32) + x_on.astype(F32)
     grad_in_near = m0.astype(F32) + gm0.astype(F32) + x_mn.astype(F32)
-    f_out = jnp.concatenate([f_out0, f_out1], axis=0)
+    f_out = jnp.concatenate([f_out0, f_out1, f_out2], axis=0)
     f_in = jnp.concatenate([f_in0, f_in[1]], axis=0)
     grad_out = (grad_out_near + f_out.astype(F32)).T
     grad_in = grad_in_near + f_in.astype(F32)

time: 371 us -> 368 us (level)
  waiting for transfers between devices: 137 us -> 131 us
    ppermute x37 -> x38, waiting for transfers between devices: 135 us -> 131 us  [swap(): return lax.ppermute(value, axis, [(i, i ^ bit) for i in range(count)])]
    ppermute x37 -> x38, starting transfers between devices: 32.9 us -> 30 us  [swap(): return lax.ppermute(value, axis, [(i, i ^ bit) for i in range(count)])]
    unnamed x50 -> x56, local copies, waits for them, and re-layouts: 5.83 us -> 8.03 us
  transfers between devices with their start and end apart: 39 -> 39, of which waited for: 17 -> 19; matrix products, arithmetic and copies ran while one was open for 9% -> 9% of each run, Pallas kernels for 29% -> 29%
where the time goes in v4:
time: 368 us
  waiting for transfers between devices  131 us (36%)
  Pallas kernels  125 us (34%)
  other arithmetic  31.7 us (9%)
  starting transfers between devices  30.1 us (8%)
  local copies, waits for them, and re-layouts  21 us (6%)
  between operations  16.2 us (4%)
  blocking collectives  12.3 us (3%)
    ppermute x38, waiting for transfers between devices, swap(): return lax.ppermute(value, axis, [(i, i ^ bit) for i in range(count)])  131 us
    ppermute x38, starting transfers between devices, swap(): return lax.ppermute(value, axis, [(i, i ^ bit) for i in range(count)])  30 us
    pallas_call x2, Pallas kernels, grad_in_part(): pl.pallas_call(body, grid=(cols // FC,), in_specs=[pl.BlockSpec(memory_sp...  27.3 us
    pallas_call x1, Pallas kernels, target_parts(): pl.pallas_call(body, grid_spec=pltpu.PrefetchScalarGridSpec(num_scalar_pr...  18.5 us
    pallas_call x2, Pallas kernels, grad_out_part(): pl.pallas_call(body, grid=(cols // FC,), in_specs=[pl.BlockSpec(memory_sp...  17.4 us
    add x2, other arithmetic, gelu_slope(): 0.5 * (1.0 + lax.erf(value * 0.7071067811865476))  12.8 us
    psum x1, blocking collectives, pair_shards(): sums = lax.psum(sums[:2], 'mx')  12.3 us
    pallas_call x1, Pallas kernels, forward_pieces(): pl.pallas_call(body, grid=(cols // FC,), in_specs=[pl.BlockSpec(memory_sp...  11.8 us
  transfers between devices with their start and end apart: 39, of which 19 were waited for; matrix products, arithmetic and copies ran while one was open for 9% of the time, Pallas kernels for 29%

profile of v4, /device:TPU:0, one launch (start us, length us, event | category | flops | bytes accessed | tf_op | source)
XLA Modules:
  0.0 367.6 jit_solution(3898194177269120410)
XLA Ops:
  7.2 3.0 pad_maximum_fusion.1
  16.1 3.0 collective-permute-start.1
  19.2 2.6 collective-permute-start
  21.8 5.6 %teacher_sums.1 = f32[8,2048]{1,0:T(8,128)} custom-call(bf16[2048,1536]{1,0:T(8,128)(2,1)} %bitcast.38), custom_call_target="tpu_custom_call" | custom-call | flops 1000 | bytes 1000 | tf_op jit(solution)/shard_map/teacher_sums/pallas_call | solution.py:102
  29.4 12.3 %psum.7.s_ref = f32[2,2048]{1,0:T(2,128)} all-reduce(f32[2,2048]{1,0:T(2,128)S(1)} %slice.80), channel_id=1, replica_groups=mesh['group'=2,'mx'=4,'my'=4] {'mx'}, use_global_device_ids=true, to_apply=%region_0.0 | all-reduce | flops 4096 | bytes 32768 | tf_op jit(solution)/shard_map/psum | solution.py:509
  41.7 18.5 %targets.1 = (bf16[512,1408]{1,0:T(8,128)(2,1)}, bf16[512,1408]{1,0:T(8,128)(2,1)}, bf16[512,1408]{1,0:T(8,128)(2,1)}, bf16[512,1408]{1,0:T(8,128)(2,1)}) custom-call(s32[1]{0:T(128)} %bitcast.2.mx_ref, bf16[2048,1536]{1,0:T(8,128)(2,1)} %bitcast.39, f32[2,2048]{1,0:T(2,128)} %psum.7.s_ref, f32[1,1536]{1,0:T(1,128)} %reshape.43.g_ref, ...), custom_call_target="tpu_custom_call" | custom-call | flops 1000 | bytes 1000 | tf_op jit(solution)/shard_map/targets/pallas_call | solution.py:137
  60.2 13.3 %collective-permute-done.refs_0_ = bf16[352,1536]{1,0:T(8,128)(2,1)} collective-permute-done((bf16[352,1536]{1,0:T(8,128)(2,1)}, bf16[352,1536]{1,0:T(8,128)(2,1)}, u32[]{:S(2)}, u32[]{:S(2)}) %collective-permute-start) | collective-permute-done | bytes 1081376 | tf_op jit(solution)/shard_map/ppermute | solution.py:35
  77.9 2.5 copy.12.np_
  80.5 10.8 %forward.1 = (f32[1024,1536]{1,0:T(8,128)}, bf16[1024,1536]{1,0:T(8,128)(2,1)}) custom-call(bf16[512,1408]{1,0:T(8,128)(2,1)} %copy-done, bf16[512,1408]{1,0:T(8,128)(2,1)} %copy.12.np_, bf16[4,2,352,1536]{3,2,1,0:T(8,128)(2,1)} %bitcast.30), custom_call_target="tpu_custom_call" | custom-call | flops 1000 | bytes 1000 | tf_op jit(solution)/shard_map/forward/pallas_call | solution.py:199
  91.3 9.4 %collective-permute-done.3.refs_2_ = bf16[352,1536]{1,0:T(8,128)(2,1)S(1)} collective-permute-done((bf16[352,1536]{1,0:T(8,128)(2,1)}, bf16[352,1536]{1,0:T(8,128)(2,1)S(1)}, u32[]{:S(2)}, u32[]{:S(2)}) %collective-permute-start.3) | collective-permute-done | bytes 1081376 | tf_op jit(solution)/shard_map/ppermute | solution.py:35
  107.5 2.8 add_convert_fusion
  110.3 11.1 %branch_near.1.nr = f32[1024,1408]{1,0:T(8,128)} custom-call(bf16[1024,1536]{1,0:T(8,128)(2,1)} %get-tuple-element.128.a, bf16[4,2,352,1536]{3,2,1,0:T(8,128)(2,1)} %bitcast.31), custom_call_target="tpu_custom_call" | custom-call | flops 1000 | bytes 1000 | tf_op jit(solution)/shard_map/branch_near/pallas_call | solution.py:328
  126.2 11.8 %forward_far.1 = (f32[1024,1536]{1,0:T(8,128)}, bf16[1024,1536]{1,0:T(8,128)(2,1)}) custom-call(s32[8]{0:T(128)} %stack.71.offs_ref, bf16[512,1408]{1,0:T(8,128)(2,1)} %copy-done, bf16[512,1408]{1,0:T(8,128)(2,1)} %copy.12.np_, bf16[352,1536]{1,0:T(8,128)(2,1)} %collective-permute-done.refs_0_, bf16[352,1536]{1,0:T(8,128)(2,1)} %collective-permute-done.4.refs_1_, ...), custom_call_target="tpu_custom_call" | custom-call | flops 1000 | bytes 1000 | tf_op jit(solution)/shard_map/forward_far/pallas_call | solution.py:238
  138.1 8.7 %branch_far.1 = bf16[512,1408]{1,0:T(8,128)(2,1)} custom-call(s32[8]{0:T(128)} %stack.71.offs_ref, f32[1024,1408]{1,0:T(8,128)} %branch_near.1.nr, bf16[1024,1536]{1,0:T(8,128)(2,1)} %get-tuple-element.140.a, bf16[352,1536]{1,0:T(8,128)(2,1)} %collective-permute-done.refs_0_, bf16[352,1536]{1,0:T(8,128)(2,1)} %collective-permute-done.4.refs_1_, ...), custom_call_target="tpu_custom_call" | custom-call | flops 1000 | bytes 1000 | tf_op jit(solution)/shard_map/branch_far/pallas_call | solution.py:281
  146.7 2.7 collective-permute-start.13
  150.5 4.9 %assemble.1.w = bf16[1408,1536]{1,0:T(8,128)(2,1)} custom-call(s32[8]{0:T(128)} %stack.80.offs_ref, bf16[352,1536]{1,0:T(8,128)(2,1)} %collective-permute-done.refs_0_, bf16[352,1536]{1,0:T(8,128)(2,1)} %collective-permute-done.4.refs_1_, bf16[352,1536]{1,0:T(8,128)(2,1)} %copy-done.7, bf16[352,1536]{1,0:T(8,128)(2,1)} %copy-done.10, ...), custom_call_target="tpu_custom_call" | custom-call | flops 1000 | bytes 1000 | tf_op jit(solution)/shard_map/assemble/pallas_call | solution.py:68
  155.4 8.0 %branch.1 = f32[512,1408]{1,0:T(8,128)} custom-call(f32[1024,1408]{1,0:T(8,128)} %branch_near.1.nr, bf16[1024,1536]{1,0:T(8,128)(2,1)} %get-tuple-element.140.a, bf16[1408,1536]{1,0:T(8,128)(2,1)} %assemble.1.w), custom_call_target="tpu_custom_call" | custom-call | flops 1000 | bytes 1000 | tf_op jit(solution)/shard_map/branch/pallas_call | solution.py:362
  163.5 8.5 %fusion.3.sl = f32[1024,1536]{1,0:T(8,128)} fusion(f32[1024,1536]{1,0:T(8,128)} %get-tuple-element.151), kind=kLoop, calls=%fused_computation.5 | loop fusion | flops 12582912 | bytes 12582912 | tf_op jit(solution)/shard_map/add | solution.py:28
  172.0 9.7 %collective-permute-done.13 = bf16[512,1408]{1,0:T(8,128)(2,1)S(1)} collective-permute-done((bf16[512,1408]{1,0:T(8,128)(2,1)}, bf16[512,1408]{1,0:T(8,128)(2,1)S(1)}, u32[]{:S(2)}, u32[]{:S(2)}) %collective-permute-start.13) | collective-permute-done | bytes 1441824 | tf_op jit(solution)/shard_map/ppermute | solution.py:35
  183.3 3.7 %multiply_reduce_fusion = (f32[]{:T(128)}, f32[512,1408]{1,0:T(8,128)S(1)}) fusion(bf16[512,1408]{1,0:T(8,128)(2,1)} %collective-permute-done.14, bf16[512,1408]{1,0:T(8,128)(2,1)} %collective-permute-done.12, bf16[512,1408]{1,0:T(8,128)(2,1)S(1)} %copy-done.15, f32[512,1408]{1,0:T(8,128)S(1)} %copy-done.8, ...), kind=kLoop, calls=%fused_computation.11 | loop fusion | flops 8650751 | bytes 12976132 | tf_op jit(solution)/shard_map/reduce_sum | solution.py:559
  188.3 4.3 %fusion.7.sl = f32[1024,1536]{1,0:T(8,128)} fusion(f32[1024,1536]{1,0:T(8,128)S(1)} %bitcast.41), kind=kLoop, calls=%fused_computation.9 | loop fusion | flops 12582912 | bytes 12582912 | tf_op jit(solution)/shard_map/add | solution.py:28
  197.8 23.0 %collective-permute-done.15.gp = bf16[512,1408]{1,0:T(8,128)(2,1)} collective-permute-done((bf16[512,1408]{1,0:T(8,128)(2,1)S(1)}, bf16[512,1408]{1,0:T(8,128)(2,1)}, u32[]{:S(2)}, u32[]{:S(2)}) %collective-permute-start.15) | collective-permute-done | bytes 1441824 | tf_op jit(solution)/shard_map/ppermute | solution.py:35
  220.8 8.6 %grad_out.2 = (bf16[352,1536]{1,0:T(8,128)(2,1)S(1)}, bf16[352,1536]{1,0:T(8,128)(2,1)S(1)}, bf16[352,1536]{1,0:T(8,128)(2,1)S(1)}, bf16[352,1536]{1,0:T(8,128)(2,1)S(1)}) custom-call(s32[1]{0:T(128)} %bitcast.2.mx_ref, bf16[512,1408]{1,0:T(8,128)(2,1)S(1)} %multiply_convert_fusion.go, bf16[512,1408]{1,0:T(8,128)(2,1)} %collective-permute-done.15.gp, ...), custom_call_target="tpu_custom_call" | custom-call | flops 1000 | bytes 1000 | tf_op jit(solution)/shard_map/grad_out/pallas_call | solution.py:413
  234.0 8.8 %grad_out.3 = (bf16[352,1536]{1,0:T(8,128)(2,1)S(1)}, bf16[352,1536]{1,0:T(8,128)(2,1)S(1)}, bf16[352,1536]{1,0:T(8,128)(2,1)S(1)}, bf16[352,1536]{1,0:T(8,128)(2,1)S(1)}) custom-call(s32[1]{0:T(128)} %bitcast.2.mx_ref, bf16[512,1408]{1,0:T(8,128)(2,1)S(1)} %multiply_convert_fusion.go, bf16[512,1408]{1,0:T(8,128)(2,1)} %collective-permute-done.15.gp, ...), custom_call_target="tpu_custom_call" | custom-call | flops 1000 | bytes 1000 | tf_op jit(solution)/shard_map/grad_out/pallas_call | solution.py:413
  246.3 2.8 copy-done.3
  249.1 13.7 %grad_in.2 = (bf16[352,1536]{1,0:T(8,128)(2,1)S(1)}, bf16[352,1536]{1,0:T(8,128)(2,1)S(1)}, bf16[352,1536]{1,0:T(8,128)(2,1)S(1)}, bf16[352,1536]{1,0:T(8,128)(2,1)S(1)}) custom-call(s32[1]{0:T(128)} %bitcast.2.mx_ref, bf16[512,1408]{1,0:T(8,128)(2,1)S(1)} %multiply_convert_fusion.go, bf16[512,1408]{1,0:T(8,128)(2,1)} %collective-permute-done.15.gp, ...), custom_call_target="tpu_custom_call" | custom-call | flops 1000 | bytes 1000 | tf_op jit(solution)/shard_map/grad_in/pallas_call | solution.py:444
  269.4 6.4 %collective-permute-done.28 = bf16[48,1536]{1,0:T(8,128)(2,1)S(1)} collective-permute-done((bf16[48,1536]{1,0:T(8,128)(2,1)S(1)}, bf16[48,1536]{1,0:T(8,128)(2,1)S(1)}, u32[]{:S(2)}, u32[]{:S(2)}) %collective-permute-start.28) | collective-permute-done | bytes 147488 | tf_op jit(solution)/shard_map/ppermute | solution.py:35
  278.4 13.6 %grad_in.3 = (bf16[352,1536]{1,0:T(8,128)(2,1)S(1)}, bf16[352,1536]{1,0:T(8,128)(2,1)S(1)}, bf16[352,1536]{1,0:T(8,128)(2,1)S(1)}, bf16[352,1536]{1,0:T(8,128)(2,1)S(1)}) custom-call(s32[1]{0:T(128)} %bitcast.2.mx_ref, bf16[512,1408]{1,0:T(8,128)(2,1)S(1)} %multiply_convert_fusion.go, bf16[512,1408]{1,0:T(8,128)(2,1)} %collective-permute-done.15.gp, ...), custom_call_target="tpu_custom_call" | custom-call | flops 1000 | bytes 1000 | tf_op jit(solution)/shard_map/grad_in/pallas_call | solution.py:444
  292.0 10.4 %collective-permute-done.30 = bf16[176,1536]{1,0:T(8,128)(2,1)S(1)} collective-permute-done((bf16[176,1536]{1,0:T(8,128)(2,1)S(1)}, bf16[176,1536]{1,0:T(8,128)(2,1)S(1)}, u32[]{:S(2)}, u32[]{:S(2)}) %collective-permute-start.30) | collective-permute-done | bytes 540704 | tf_op jit(solution)/shard_map/ppermute | solution.py:35
  304.0 2.9 collective-permute-start.35
  306.9 17.4 %collective-permute-done.33 = bf16[352,1536]{1,0:T(8,128)(2,1)S(1)} collective-permute-done((bf16[352,1536]{1,0:T(8,128)(2,1)S(1)}, bf16[352,1536]{1,0:T(8,128)(2,1)S(1)}, u32[]{:S(2)}, u32[]{:S(2)}) %collective-permute-start.33) | collective-permute-done | bytes 1081376 | tf_op jit(solution)/shard_map/ppermute | solution.py:35
  329.2 28.5 %collective-permute-done.37 = bf16[224,1536]{1,0:T(8,128)(2,1)S(1)} collective-permute-done((bf16[224,1536]{1,0:T(8,128)(2,1)S(1)}, bf16[224,1536]{1,0:T(8,128)(2,1)S(1)}, u32[]{:S(2)}, u32[]{:S(2)}) %collective-permute-start.37) | collective-permute-done | bytes 688160 | tf_op jit(solution)/shard_map/ppermute | solution.py:35
  (160 shorter events, 58.1 us)
Async XLA Ops:
  7.2 73.3 %all-gather.2.cloned.1.call-start = ((), (), s32[]{:S(2)}) async-start(), calls=%async_computation | async-start | bytes 10813440 | tf_op jit(solution)/shard_map/all_gather | solution.py:501
  16.1 58.1 %collective-permute-start.1 = (bf16[512,1408]{0,1:T(8,128)(2,1)}, bf16[512,1408]{0,1:T(8,128)(2,1)}, u32[]{:S(2)}, u32[]{:S(2)}) collective-permute-start(bf16[512,1408]{0,1:T(8,128)(2,1)} %copy.11), channel_id=1, source_target_pairs={{0,1},{1,0},{2,3},{3,2},{4,5},{5,4},{6,7},{7,6},{8,9},{9,8},{10,11... | collective-permute-start | bytes 4325384 | tf_op jit(solution)/shard_map/ppermute | solution.py:35
  19.2 54.3 %collective-permute-start = (bf16[352,1536]{1,0:T(8,128)(2,1)}, bf16[352,1536]{1,0:T(8,128)(2,1)}, u32[]{:S(2)}, u32[]{:S(2)}) collective-permute-start(bf16[352,1536]{1,0:T(8,128)(2,1)} %pad_maximum_fusion.2), channel_id=1, source_target_pairs={{0,2},{1,3},{2,0},{3,1},{4,6},{5,7},{6,4},{7,5},{8,10},{9,11},{10,... | collective-permute-start | bytes 3244040 | tf_op jit(solution)/shard_map/ppermute | solution.py:35
  74.2 28.0 %collective-permute-start.5 = (bf16[512,1408]{1,0:T(8,128)(2,1)}, bf16[512,1408]{1,0:T(8,128)(2,1)}, u32[]{:S(2)}, u32[]{:S(2)}) collective-permute-start(bf16[512,1408]{1,0:T(8,128)(2,1)} %get-tuple-element.122), channel_id=1, source_target_pairs={{0,4},{4,0},{8,12},{12,8},{1,5},{5,1},{9,13},{13,9},{2,6},{6,2},{1... | collective-permute-start | bytes 4325384 | tf_op jit(solution)/shard_map/ppermute | solution.py:35
  74.2 17.1 %collective-permute-start.4 = (bf16[352,1536]{1,0:T(8,128)(2,1)}, bf16[352,1536]{1,0:T(8,128)(2,1)}, u32[]{:S(2)}, u32[]{:S(2)}) collective-permute-start(bf16[352,1536]{1,0:T(8,128)(2,1)} %collective-permute-done.refs_0_), channel_id=1, source_target_pairs={{0,4},{4,0},{8,12},{12,8},{1,5},{5,1},{9,13},{13,9},{2,6},{6,2},{1... | collective-permute-start | bytes 3244040 | tf_op jit(solution)/shard_map/ppermute | solution.py:35
  74.7 26.0 %collective-permute-start.3 = (bf16[352,1536]{1,0:T(8,128)(2,1)}, bf16[352,1536]{1,0:T(8,128)(2,1)S(1)}, u32[]{:S(2)}, u32[]{:S(2)}) collective-permute-start(bf16[352,1536]{1,0:T(8,128)(2,1)} %collective-permute-done.refs_0_), channel_id=1, source_target_pairs={{0,16},{16,0},{1,17},{17,1},{2,18},{18,2},{3,19},{19,3},{4,20},{20... | collective-permute-start | bytes 3244040 | tf_op jit(solution)/shard_map/ppermute | solution.py:35
  76.4 25.8 %collective-permute-start.2 = (bf16[352,1536]{1,0:T(8,128)(2,1)}, bf16[352,1536]{1,0:T(8,128)(2,1)}, u32[]{:S(2)}, u32[]{:S(2)}) collective-permute-start(bf16[352,1536]{1,0:T(8,128)(2,1)} %collective-permute-done.refs_0_), channel_id=1, source_target_pairs={{0,8},{4,12},{8,0},{12,4},{1,9},{5,13},{9,1},{13,5},{2,10},{6,14},... | collective-permute-start | bytes 3244040 | tf_op jit(solution)/shard_map/ppermute | solution.py:35
  102.2 19.2 %collective-permute-start.9 = (bf16[352,1536]{1,0:T(8,128)(2,1)}, bf16[352,1536]{1,0:T(8,128)(2,1)S(1)}, u32[]{:S(2)}, u32[]{:S(2)}) collective-permute-start(bf16[352,1536]{1,0:T(8,128)(2,1)} %collective-permute-done.2.refs_4_), channel_id=1, source_target_pairs={{0,4},{4,0},{8,12},{12,8},{1,5},{5,1},{9,13},{13,9},{2,6},{6,2},{1... | collective-permute-start | bytes 3244040 | tf_op jit(solution)/shard_map/ppermute | solution.py:35
  102.2 19.2 %collective-permute-start.8 = (bf16[352,1536]{1,0:T(8,128)(2,1)S(1)}, bf16[352,1536]{1,0:T(8,128)(2,1)S(1)}, u32[]{:S(2)}, u32[]{:S(2)}) collective-permute-start(bf16[352,1536]{1,0:T(8,128)(2,1)S(1)} %collective-permute-done.3.refs_2_), channel_id=1, source_target_pairs={{0,4},{4,0},{8,12},{12,8},{1,5},{5,1},{9,13},{13,9},{2,6},{6,2},{1... | collective-permute-start | bytes 3244040 | tf_op jit(solution)/shard_map/ppermute | solution.py:35
  105.5 15.9 %collective-permute-start.7 = (bf16[176,1536]{1,0:T(8,128)(2,1)}, bf16[176,1536]{1,0:T(8,128)(2,1)S(1)}, u32[]{:S(2)}, u32[]{:S(2)}) collective-permute-start(bf16[176,1536]{1,0:T(8,128)(2,1)} %slice.62), channel_id=1, source_target_pairs={{0,8},{4,12},{8,0},{12,4},{1,9},{5,13},{9,1},{13,5},{2,10},{6,14},... | collective-permute-start | bytes 1622024 | tf_op jit(solution)/shard_map/ppermute | solution.py:35
  107.0 14.4 %collective-permute-start.6 = (bf16[176,1536]{1,0:T(8,128)(2,1)}, bf16[176,1536]{1,0:T(8,128)(2,1)}, u32[]{:S(2)}, u32[]{:S(2)}) collective-permute-start(bf16[176,1536]{1,0:T(8,128)(2,1)} %slice.61), channel_id=1, source_target_pairs={{0,16},{16,0},{1,17},{17,1},{2,18},{18,2},{3,19},{19,3},{4,20},{20... | collective-permute-start | bytes 1622024 | tf_op jit(solution)/shard_map/ppermute | solution.py:35
  125.4 12.6 %collective-permute-start.12 = (bf16[512,1408]{1,0:T(8,128)(2,1)}, bf16[512,1408]{1,0:T(8,128)(2,1)}, u32[]{:S(2)}, u32[]{:S(2)}) collective-permute-start(bf16[512,1408]{1,0:T(8,128)(2,1)} %get-tuple-element.139), channel_id=1, source_target_pairs={{0,4},{4,0},{8,12},{12,8},{1,5},{5,1},{9,13},{13,9},{2,6},{6,2},{1... | collective-permute-start | bytes 4325384 | tf_op jit(solution)/shard_map/ppermute | solution.py:35
  146.7 35.0 %collective-permute-start.13 = (bf16[512,1408]{1,0:T(8,128)(2,1)}, bf16[512,1408]{1,0:T(8,128)(2,1)S(1)}, u32[]{:S(2)}, u32[]{:S(2)}) collective-permute-start(bf16[512,1408]{1,0:T(8,128)(2,1)} %branch_far.1), channel_id=1, source_target_pairs={{0,1},{1,0},{2,3},{3,2},{4,5},{5,4},{6,7},{7,6},{8,9},{9,8},{10,11... | collective-permute-start | bytes 4325384 | tf_op jit(solution)/shard_map/ppermute | solution.py:35
  149.4 33.9 %collective-permute-start.14 = (bf16[512,1408]{1,0:T(8,128)(2,1)}, bf16[512,1408]{1,0:T(8,128)(2,1)}, u32[]{:S(2)}, u32[]{:S(2)}) collective-permute-start(bf16[512,1408]{1,0:T(8,128)(2,1)} %add_convert_fusion), channel_id=1, source_target_pairs={{0,8},{4,12},{8,0},{12,4},{1,9},{5,13},{9,1},{13,5},{2,10},{6,14},... | collective-permute-start | bytes 4325384 | tf_op jit(solution)/shard_map/ppermute | solution.py:35
  187.9 32.9 %collective-permute-start.15 = (bf16[512,1408]{1,0:T(8,128)(2,1)S(1)}, bf16[512,1408]{1,0:T(8,128)(2,1)}, u32[]{:S(2)}, u32[]{:S(2)}) collective-permute-start(bf16[512,1408]{1,0:T(8,128)(2,1)S(1)} %multiply_convert_fusion.go), channel_id=1, source_target_pairs={{0,1},{1,0},{2,3},{3,2},{4,5},{5,4},{6,7},{7,6},{8,9},{9,8},{10,11... | collective-permute-start | bytes 4325384 | tf_op jit(solution)/shard_map/ppermute | solution.py:35
  229.4 13.4 %collective-permute-start.20 = (bf16[352,1536]{1,0:T(8,128)(2,1)S(1)}, bf16[352,1536]{1,0:T(8,128)(2,1)S(1)}, u32[]{:S(2)}, u32[]{:S(2)}) collective-permute-start(bf16[352,1536]{1,0:T(8,128)(2,1)S(1)} %get-tuple-element.171), channel_id=1, source_target_pairs={{0,4},{4,0},{8,12},{12,8},{1,5},{5,1},{9,13},{13,9},{2,6},{6,2},{1... | collective-permute-start | bytes 3244040 | tf_op jit(solution)/shard_map/ppermute | solution.py:35
  232.2 11.2 %collective-permute-start.19 = (bf16[128,1536]{1,0:T(8,128)(2,1)S(1)}, bf16[128,1536]{1,0:T(8,128)(2,1)S(1)}, u32[]{:S(2)}, u32[]{:S(2)}) collective-permute-start(bf16[128,1536]{1,0:T(8,128)(2,1)S(1)} %add_convert_fusion.9), channel_id=1, source_target_pairs={{0,8},{4,12},{8,0},{12,4},{1,9},{5,13},{9,1},{13,5},{2,10},{6,14},... | collective-permute-start | bytes 1179656 | tf_op jit(solution)/shard_map/ppermute | solution.py:35
  243.6 21.3 %collective-permute-start.22 = (bf16[352,1536]{1,0:T(8,128)(2,1)S(1)}, bf16[352,1536]{1,0:T(8,128)(2,1)S(1)}, u32[]{:S(2)}, u32[]{:S(2)}) collective-permute-start(bf16[352,1536]{1,0:T(8,128)(2,1)S(1)} %get-tuple-element.181), channel_id=1, source_target_pairs={{0,4},{4,0},{8,12},{12,8},{1,5},{5,1},{9,13},{13,9},{2,6},{6,2},{1... | collective-permute-start | bytes 3244040 | tf_op jit(solution)/shard_map/ppermute | solution.py:35
  243.7 21.2 %collective-permute-start.23 = (bf16[352,1536]{1,0:T(8,128)(2,1)S(1)}, bf16[352,1536]{1,0:T(8,128)(2,1)S(1)}, u32[]{:S(2)}, u32[]{:S(2)}) collective-permute-start(bf16[352,1536]{1,0:T(8,128)(2,1)S(1)} %get-tuple-element.183), channel_id=1, source_target_pairs={{0,4},{4,0},{8,12},{12,8},{1,5},{5,1},{9,13},{13,9},{2,6},{6,2},{1... | collective-permute-start | bytes 3244040 | tf_op jit(solution)/shard_map/ppermute | solution.py:35
  244.2 18.6 %collective-permute-start.21 = (bf16[224,1536]{1,0:T(8,128)(2,1)S(1)}, bf16[224,1536]{1,0:T(8,128)(2,1)S(1)}, u32[]{:S(2)}, u32[]{:S(2)}) collective-permute-start(bf16[224,1536]{1,0:T(8,128)(2,1)S(1)} %add_convert_fusion.6), channel_id=1, source_target_pairs={{0,8},{4,12},{8,0},{12,4},{1,9},{5,13},{9,1},{13,5},{2,10},{6,14},... | collective-permute-start | bytes 2064392 | tf_op jit(solution)/shard_map/ppermute | solution.py:35
  244.7 20.1 %collective-permute-start.24 = (bf16[128,1536]{1,0:T(8,128)(2,1)S(1)}, bf16[128,1536]{1,0:T(8,128)(2,1)S(1)}, u32[]{:S(2)}, u32[]{:S(2)}) collective-permute-start(bf16[128,1536]{1,0:T(8,128)(2,1)S(1)} %add_convert_fusion.8), channel_id=1, source_target_pairs={{0,2},{1,3},{2,0},{3,1},{4,6},{5,7},{6,4},{7,5},{8,10},{9,11},{10,... | collective-permute-start | bytes 1179656 | tf_op jit(solution)/shard_map/ppermute | solution.py:35
  264.9 10.9 %collective-permute-start.25 = (bf16[352,1536]{1,0:T(8,128)(2,1)S(1)}, bf16[352,1536]{1,0:T(8,128)(2,1)S(1)}, u32[]{:S(2)}, u32[]{:S(2)}) collective-permute-start(bf16[352,1536]{1,0:T(8,128)(2,1)S(1)} %get-tuple-element.184), channel_id=1, source_target_pairs={{0,4},{4,0},{8,12},{12,8},{1,5},{5,1},{9,13},{13,9},{2,6},{6,2},{1... | collective-permute-start | bytes 3244040 | tf_op jit(solution)/shard_map/ppermute | solution.py:35
  265.0 10.8 %collective-permute-start.26 = (bf16[352,1536]{1,0:T(8,128)(2,1)S(1)}, bf16[352,1536]{1,0:T(8,128)(2,1)S(1)}, u32[]{:S(2)}, u32[]{:S(2)}) collective-permute-start(bf16[352,1536]{1,0:T(8,128)(2,1)S(1)} %get-tuple-element.185), channel_id=1, source_target_pairs={{0,4},{4,0},{8,12},{12,8},{1,5},{5,1},{9,13},{13,9},{2,6},{6,2},{1... | collective-permute-start | bytes 3244040 | tf_op jit(solution)/shard_map/ppermute | solution.py:35
  276.1 26.9 %collective-permute-start.29 = (bf16[352,1536]{1,0:T(8,128)(2,1)S(1)}, bf16[352,1536]{1,0:T(8,128)(2,1)S(1)}, u32[]{:S(2)}, u32[]{:S(2)}) collective-permute-start(bf16[352,1536]{1,0:T(8,128)(2,1)S(1)} %add_convert_fusion.2), channel_id=1, source_target_pairs={{0,8},{4,12},{8,0},{12,4},{1,9},{5,13},{9,1},{13,5},{2,10},{6,14},... | collective-permute-start | bytes 3244040 | tf_op jit(solution)/shard_map/ppermute | solution.py:35
  277.7 24.7 %collective-permute-start.30 = (bf16[176,1536]{1,0:T(8,128)(2,1)S(1)}, bf16[176,1536]{1,0:T(8,128)(2,1)S(1)}, u32[]{:S(2)}, u32[]{:S(2)}) collective-permute-start(bf16[176,1536]{1,0:T(8,128)(2,1)S(1)} %slice.84), channel_id=1, source_target_pairs={{0,2},{1,3},{2,0},{3,1},{4,6},{5,7},{6,4},{7,5},{8,10},{9,11},{10,... | collective-permute-start | bytes 1622024 | tf_op jit(solution)/shard_map/ppermute | solution.py:35
  277.8 46.6 %collective-permute-start.33 = (bf16[352,1536]{1,0:T(8,128)(2,1)S(1)}, bf16[352,1536]{1,0:T(8,128)(2,1)S(1)}, u32[]{:S(2)}, u32[]{:S(2)}) collective-permute-start(bf16[352,1536]{1,0:T(8,128)(2,1)S(1)} %add_convert_fusion.3), channel_id=1, source_target_pairs={{0,8},{4,12},{8,0},{12,4},{1,9},{5,13},{9,1},{13,5},{2,10},{6,14},... | collective-permute-start | bytes 3244040 | tf_op jit(solution)/shard_map/ppermute | solution.py:35
  303.4 20.9 %collective-permute-start.31 = (bf16[352,1536]{1,0:T(8,128)(2,1)S(1)}, bf16[352,1536]{1,0:T(8,128)(2,1)S(1)}, u32[]{:S(2)}, u32[]{:S(2)}) collective-permute-start(bf16[352,1536]{1,0:T(8,128)(2,1)S(1)} %get-tuple-element.204), channel_id=1, source_target_pairs={{0,4},{4,0},{8,12},{12,8},{1,5},{5,1},{9,13},{13,9},{2,6},{6,2},{1... | collective-permute-start | bytes 3244040 | tf_op jit(solution)/shard_map/ppermute | solution.py:35
  303.5 20.8 %collective-permute-start.32 = (bf16[352,1536]{1,0:T(8,128)(2,1)S(1)}, bf16[352,1536]{1,0:T(8,128)(2,1)S(1)}, u32[]{:S(2)}, u32[]{:S(2)}) collective-permute-start(bf16[352,1536]{1,0:T(8,128)(2,1)S(1)} %get-tuple-element.206), channel_id=1, source_target_pairs={{0,4},{4,0},{8,12},{12,8},{1,5},{5,1},{9,13},{13,9},{2,6},{6,2},{1... | collective-permute-start | bytes 3244040 | tf_op jit(solution)/shard_map/ppermute | solution.py:35
  304.0 20.3 %collective-permute-start.34 = (bf16[128,1536]{1,0:T(8,128)(2,1)S(1)}, bf16[128,1536]{1,0:T(8,128)(2,1)S(1)}, u32[]{:S(2)}, u32[]{:S(2)}) collective-permute-start(bf16[128,1536]{1,0:T(8,128)(2,1)S(1)} %add_convert_fusion.7), channel_id=1, source_target_pairs={{0,2},{1,3},{2,0},{3,1},{4,6},{5,7},{6,4},{7,5},{8,10},{9,11},{10,... | collective-permute-start | bytes 1179656 | tf_op jit(solution)/shard_map/ppermute | solution.py:35
  304.0 20.3 %collective-permute-start.35 = (f32[8,128]{1,0:T(8,128)S(1)}, f32[8,128]{1,0:T(8,128)S(1)}, u32[]{:S(2)}, u32[]{:S(2)}) collective-permute-start(f32[8,128]{1,0:T(8,128)S(1)} %add.161), channel_id=1, source_target_pairs={{0,2},{1,3},{2,0},{3,1},{4,6},{5,7},{6,4},{7,5},{8,10},{9,11},{10,... | collective-permute-start | bytes 12296 | tf_op jit(solution)/shard_map/ppermute | solution.py:35
  324.7 33.1 %collective-permute-start.36 = (bf16[352,1536]{1,0:T(8,128)(2,1)S(1)}, bf16[352,1536]{1,0:T(8,128)(2,1)S(1)}, u32[]{:S(2)}, u32[]{:S(2)}) collective-permute-start(bf16[352,1536]{1,0:T(8,128)(2,1)S(1)} %add_convert_fusion.1), channel_id=1, source_target_pairs={{0,8},{4,12},{8,0},{12,4},{1,9},{5,13},{9,1},{13,5},{2,10},{6,14},... | collective-permute-start | bytes 3244040 | tf_op jit(solution)/shard_map/ppermute | solution.py:35
  326.2 31.5 %collective-permute-start.37 = (bf16[224,1536]{1,0:T(8,128)(2,1)S(1)}, bf16[224,1536]{1,0:T(8,128)(2,1)S(1)}, u32[]{:S(2)}, u32[]{:S(2)}) collective-permute-start(bf16[224,1536]{1,0:T(8,128)(2,1)S(1)} %add_convert_fusion.4), channel_id=1, source_target_pairs={{0,2},{1,3},{2,0},{3,1},{4,6},{5,7},{6,4},{7,5},{8,10},{9,11},{10,... | collective-permute-start | bytes 2064392 | tf_op jit(solution)/shard_map/ppermute | solution.py:35
  (35 other events, 331.9 us)
Sparse Core Ops, SparseCore 0:
  10.4 62.7 all-gather.1

commit v5 on v4

--- a/solution.py
+++ b/solution.py
@@ -550,6 +550,7 @@
     branch_recv = swap(branch_pair, "my", 1)
     out_far = assemble([(p, at, n, after(o, branch_pair)) for p, at, n, o in out_rows], DS)
     branch_own = branch_part(near_share, act_far, out_far, 0, F32)
+    branch_own, target_x = together(branch_own, target_x)
     slope_far = gelu_slope(after(pre_far, branch_own))
     branch_recv = after(branch_recv, slope_far)
 

time: 368 us -> 368 us (level)
  transfers between devices with their start and end apart: 39 -> 39, of which waited for: 19 -> 17; matrix products, arithmetic and copies ran while one was open for 9% -> 9% of each run, Pallas kernels for 29% -> 32%
where the time goes in v5:
time: 368 us; the launch traced here: 367 us
  waiting for transfers between devices  128 us (35%)
  Pallas kernels  125 us (34%)
  starting transfers between devices  33.7 us (9%)
  other arithmetic  31.8 us (9%)
  local copies, waits for them, and re-layouts  20.1 us (5%)
  between operations  16.2 us (4%)
  blocking collectives  12.3 us (3%)
    ppermute x38, waiting for transfers between devices, swap(): return lax.ppermute(value, axis, [(i, i ^ bit) for i in range(count)])  128 us
    ppermute x38, starting transfers between devices, swap(): return lax.ppermute(value, axis, [(i, i ^ bit) for i in range(count)])  33.6 us
    pallas_call x2, Pallas kernels, grad_in_part(): pl.pallas_call(body, grid=(cols // FC,), in_specs=[pl.BlockSpec(memory_sp...  27.3 us
    pallas_call x1, Pallas kernels, target_parts(): pl.pallas_call(body, grid_spec=pltpu.PrefetchScalarGridSpec(num_scalar_pr...  18.5 us
    pallas_call x2, Pallas kernels, grad_out_part(): pl.pallas_call(body, grid=(cols // FC,), in_specs=[pl.BlockSpec(memory_sp...  17.3 us
    add x2, other arithmetic, gelu_slope(): 0.5 * (1.0 + lax.erf(value * 0.7071067811865476))  12.8 us
    psum x1, blocking collectives, pair_shards(): sums = lax.psum(sums[:2], 'mx')  12.3 us
    pallas_call x1, Pallas kernels, forward_pieces(): pl.pallas_call(body, grid=(cols // FC,), in_specs=[pl.BlockSpec(memory_sp...  11.9 us
  transfers between devices with their start and end apart: 39, of which 17 were waited for; matrix products, arithmetic and copies ran while one was open for 9% of the time, Pallas kernels for 32%

profile of v5, /device:TPU:0, one launch (start us, length us, event | category | flops | bytes accessed | tf_op | source)
XLA Modules:
  0.0 366.8 jit_solution(11272743218635271101)
XLA Ops:
  7.2 3.0 pad_maximum_fusion.1
  16.1 3.0 collective-permute-start.1
  19.1 2.6 collective-permute-start
  21.7 5.6 %teacher_sums.1 = f32[8,2048]{1,0:T(8,128)} custom-call(bf16[2048,1536]{1,0:T(8,128)(2,1)} %bitcast.38), custom_call_target="tpu_custom_call" | custom-call | flops 1000 | bytes 1000 | tf_op jit(solution)/shard_map/teacher_sums/pallas_call | solution.py:102
  29.4 12.3 %psum.7.s_ref = f32[2,2048]{1,0:T(2,128)} all-reduce(f32[2,2048]{1,0:T(2,128)S(1)} %slice.80), channel_id=1, replica_groups=mesh['group'=2,'mx'=4,'my'=4] {'mx'}, use_global_device_ids=true, to_apply=%region_0.0 | all-reduce | flops 4096 | bytes 32768 | tf_op jit(solution)/shard_map/psum | solution.py:509
  41.7 18.5 %targets.1 = (bf16[512,1408]{1,0:T(8,128)(2,1)}, bf16[512,1408]{1,0:T(8,128)(2,1)}, bf16[512,1408]{1,0:T(8,128)(2,1)}, bf16[512,1408]{1,0:T(8,128)(2,1)}) custom-call(s32[1]{0:T(128)} %bitcast.2.mx_ref, bf16[2048,1536]{1,0:T(8,128)(2,1)} %bitcast.39, f32[2,2048]{1,0:T(2,128)} %psum.7.s_ref, f32[1,1536]{1,0:T(1,128)} %reshape.43.g_ref, ...), custom_call_target="tpu_custom_call" | custom-call | flops 1000 | bytes 1000 | tf_op jit(solution)/shard_map/targets/pallas_call | solution.py:137
  60.2 13.3 %collective-permute-done.refs_0_ = bf16[352,1536]{1,0:T(8,128)(2,1)} collective-permute-done((bf16[352,1536]{1,0:T(8,128)(2,1)}, bf16[352,1536]{1,0:T(8,128)(2,1)}, u32[]{:S(2)}, u32[]{:S(2)}) %collective-permute-start) | collective-permute-done | bytes 1081376 | tf_op jit(solution)/shard_map/ppermute | solution.py:35
  80.4 10.8 %forward.1 = (f32[1024,1536]{1,0:T(8,128)}, bf16[1024,1536]{1,0:T(8,128)(2,1)}) custom-call(bf16[512,1408]{1,0:T(8,128)(2,1)} %copy-done, bf16[512,1408]{1,0:T(8,128)(2,1)} %copy.12.np_, bf16[4,2,352,1536]{3,2,1,0:T(8,128)(2,1)} %bitcast.30), custom_call_target="tpu_custom_call" | custom-call | flops 1000 | bytes 1000 | tf_op jit(solution)/shard_map/forward/pallas_call | solution.py:199
  91.3 9.4 %collective-permute-done.3.refs_2_ = bf16[352,1536]{1,0:T(8,128)(2,1)S(1)} collective-permute-done((bf16[352,1536]{1,0:T(8,128)(2,1)}, bf16[352,1536]{1,0:T(8,128)(2,1)S(1)}, u32[]{:S(2)}, u32[]{:S(2)}) %collective-permute-start.3) | collective-permute-done | bytes 1081376 | tf_op jit(solution)/shard_map/ppermute | solution.py:35
  107.5 2.8 add_convert_fusion
  110.3 11.1 %branch_near.1.nr = f32[1024,1408]{1,0:T(8,128)} custom-call(bf16[1024,1536]{1,0:T(8,128)(2,1)} %get-tuple-element.130.a, bf16[4,2,352,1536]{3,2,1,0:T(8,128)(2,1)} %bitcast.31), custom_call_target="tpu_custom_call" | custom-call | flops 1000 | bytes 1000 | tf_op jit(solution)/shard_map/branch_near/pallas_call | solution.py:328
  126.6 11.9 %forward_far.1 = (f32[1024,1536]{1,0:T(8,128)}, bf16[1024,1536]{1,0:T(8,128)(2,1)}) custom-call(s32[8]{0:T(128)} %stack.71.offs_ref, bf16[512,1408]{1,0:T(8,128)(2,1)} %copy-done, bf16[512,1408]{1,0:T(8,128)(2,1)} %copy.12.np_, bf16[352,1536]{1,0:T(8,128)(2,1)} %collective-permute-done.refs_0_, bf16[352,1536]{1,0:T(8,128)(2,1)} %collective-permute-done.4.refs_1_, ...), custom_call_target="tpu_custom_call" | custom-call | flops 1000 | bytes 1000 | tf_op jit(solution)/shard_map/forward_far/pallas_call | solution.py:238
  138.6 8.7 %branch_far.1 = bf16[512,1408]{1,0:T(8,128)(2,1)} custom-call(s32[8]{0:T(128)} %stack.71.offs_ref, f32[1024,1408]{1,0:T(8,128)} %branch_near.1.nr, bf16[1024,1536]{1,0:T(8,128)(2,1)} %get-tuple-element.142.a, bf16[352,1536]{1,0:T(8,128)(2,1)} %collective-permute-done.refs_0_, bf16[352,1536]{1,0:T(8,128)(2,1)} %collective-permute-done.4.refs_1_, ...), custom_call_target="tpu_custom_call" | custom-call | flops 1000 | bytes 1000 | tf_op jit(solution)/shard_map/branch_far/pallas_call | solution.py:281
  147.3 2.8 collective-permute-start.14
  150.7 5.0 %assemble.1.w = bf16[1408,1536]{1,0:T(8,128)(2,1)} custom-call(s32[8]{0:T(128)} %stack.80.offs_ref, bf16[352,1536]{1,0:T(8,128)(2,1)} %collective-permute-done.refs_0_, bf16[352,1536]{1,0:T(8,128)(2,1)} %collective-permute-done.4.refs_1_, bf16[352,1536]{1,0:T(8,128)(2,1)} %copy-done.7, bf16[352,1536]{1,0:T(8,128)(2,1)} %copy-done.10, ...), custom_call_target="tpu_custom_call" | custom-call | flops 1000 | bytes 1000 | tf_op jit(solution)/shard_map/assemble/pallas_call | solution.py:68
  155.7 8.0 %branch.1 = f32[512,1408]{1,0:T(8,128)} custom-call(f32[1024,1408]{1,0:T(8,128)} %branch_near.1.nr, bf16[1024,1536]{1,0:T(8,128)(2,1)} %get-tuple-element.142.a, bf16[1408,1536]{1,0:T(8,128)(2,1)} %assemble.1.w), custom_call_target="tpu_custom_call" | custom-call | flops 1000 | bytes 1000 | tf_op jit(solution)/shard_map/branch/pallas_call | solution.py:362
  163.7 8.5 %fusion.3.sl = f32[1024,1536]{1,0:T(8,128)} fusion(f32[1024,1536]{1,0:T(8,128)} %get-tuple-element.155), kind=kLoop, calls=%fused_computation.5 | loop fusion | flops 12582912 | bytes 12582912 | tf_op jit(solution)/shard_map/add | solution.py:28
  172.2 9.9 %collective-permute-done.14 = bf16[512,1408]{1,0:T(8,128)(2,1)S(1)} collective-permute-done((bf16[512,1408]{1,0:T(8,128)(2,1)}, bf16[512,1408]{1,0:T(8,128)(2,1)S(1)}, u32[]{:S(2)}, u32[]{:S(2)}) %collective-permute-start.14) | collective-permute-done | bytes 1441824 | tf_op jit(solution)/shard_map/ppermute | solution.py:35
  182.1 3.7 %multiply_reduce_fusion = (f32[]{:T(128)}, f32[512,1408]{1,0:T(8,128)S(1)}) fusion(bf16[512,1408]{1,0:T(8,128)(2,1)} %collective-permute-done.13, bf16[512,1408]{1,0:T(8,128)(2,1)} %collective-permute-done.12, bf16[512,1408]{1,0:T(8,128)(2,1)S(1)} %copy-done.15, f32[512,1408]{1,0:T(8,128)S(1)} %copy-done.8, ...), kind=kLoop, calls=%fused_computation.11 | loop fusion | flops 8650751 | bytes 12976132 | tf_op jit(solution)/shard_map/reduce_sum | solution.py:560
  188.5 4.3 %fusion.7.sl = f32[1024,1536]{1,0:T(8,128)} fusion(f32[1024,1536]{1,0:T(8,128)S(1)} %bitcast.41), kind=kLoop, calls=%fused_computation.9 | loop fusion | flops 12582912 | bytes 12582912 | tf_op jit(solution)/shard_map/add | solution.py:28
  198.2 21.7 %collective-permute-done.15.gp = bf16[512,1408]{1,0:T(8,128)(2,1)} collective-permute-done((bf16[512,1408]{1,0:T(8,128)(2,1)S(1)}, bf16[512,1408]{1,0:T(8,128)(2,1)}, u32[]{:S(2)}, u32[]{:S(2)}) %collective-permute-start.15) | collective-permute-done | bytes 1441824 | tf_op jit(solution)/shard_map/ppermute | solution.py:35
  219.9 8.6 %grad_out.2 = (bf16[352,1536]{1,0:T(8,128)(2,1)S(1)}, bf16[352,1536]{1,0:T(8,128)(2,1)S(1)}, bf16[352,1536]{1,0:T(8,128)(2,1)S(1)}, bf16[352,1536]{1,0:T(8,128)(2,1)S(1)}) custom-call(s32[1]{0:T(128)} %bitcast.2.mx_ref, bf16[512,1408]{1,0:T(8,128)(2,1)S(1)} %multiply_convert_fusion.go, bf16[512,1408]{1,0:T(8,128)(2,1)} %collective-permute-done.15.gp, ...), custom_call_target="tpu_custom_call" | custom-call | flops 1000 | bytes 1000 | tf_op jit(solution)/shard_map/grad_out/pallas_call | solution.py:413
  233.2 8.7 %grad_out.3 = (bf16[352,1536]{1,0:T(8,128)(2,1)S(1)}, bf16[352,1536]{1,0:T(8,128)(2,1)S(1)}, bf16[352,1536]{1,0:T(8,128)(2,1)S(1)}, bf16[352,1536]{1,0:T(8,128)(2,1)S(1)}) custom-call(s32[1]{0:T(128)} %bitcast.2.mx_ref, bf16[512,1408]{1,0:T(8,128)(2,1)S(1)} %multiply_convert_fusion.go, bf16[512,1408]{1,0:T(8,128)(2,1)} %collective-permute-done.15.gp, ...), custom_call_target="tpu_custom_call" | custom-call | flops 1000 | bytes 1000 | tf_op jit(solution)/shard_map/grad_out/pallas_call | solution.py:413
  246.2 2.8 copy-done.3
  249.0 13.7 %grad_in.2 = (bf16[352,1536]{1,0:T(8,128)(2,1)S(1)}, bf16[352,1536]{1,0:T(8,128)(2,1)S(1)}, bf16[352,1536]{1,0:T(8,128)(2,1)S(1)}, bf16[352,1536]{1,0:T(8,128)(2,1)S(1)}) custom-call(s32[1]{0:T(128)} %bitcast.2.mx_ref, bf16[512,1408]{1,0:T(8,128)(2,1)S(1)} %multiply_convert_fusion.go, bf16[512,1408]{1,0:T(8,128)(2,1)} %collective-permute-done.15.gp, ...), custom_call_target="tpu_custom_call" | custom-call | flops 1000 | bytes 1000 | tf_op jit(solution)/shard_map/grad_in/pallas_call | solution.py:444
  266.0 2.7 collective-permute-start.28
  269.6 6.4 %collective-permute-done.28 = bf16[48,1536]{1,0:T(8,128)(2,1)S(1)} collective-permute-done((bf16[48,1536]{1,0:T(8,128)(2,1)S(1)}, bf16[48,1536]{1,0:T(8,128)(2,1)S(1)}, u32[]{:S(2)}, u32[]{:S(2)}) %collective-permute-start.28) | collective-permute-done | bytes 147488 | tf_op jit(solution)/shard_map/ppermute | solution.py:35
  278.5 13.6 %grad_in.3 = (bf16[352,1536]{1,0:T(8,128)(2,1)S(1)}, bf16[352,1536]{1,0:T(8,128)(2,1)S(1)}, bf16[352,1536]{1,0:T(8,128)(2,1)S(1)}, bf16[352,1536]{1,0:T(8,128)(2,1)S(1)}) custom-call(s32[1]{0:T(128)} %bitcast.2.mx_ref, bf16[512,1408]{1,0:T(8,128)(2,1)S(1)} %multiply_convert_fusion.go, bf16[512,1408]{1,0:T(8,128)(2,1)} %collective-permute-done.15.gp, ...), custom_call_target="tpu_custom_call" | custom-call | flops 1000 | bytes 1000 | tf_op jit(solution)/shard_map/grad_in/pallas_call | solution.py:444
  292.1 10.0 %collective-permute-done.30 = bf16[176,1536]{1,0:T(8,128)(2,1)S(1)} collective-permute-done((bf16[176,1536]{1,0:T(8,128)(2,1)S(1)}, bf16[176,1536]{1,0:T(8,128)(2,1)S(1)}, u32[]{:S(2)}, u32[]{:S(2)}) %collective-permute-start.30) | collective-permute-done | bytes 540704 | tf_op jit(solution)/shard_map/ppermute | solution.py:35
  304.1 2.9 collective-permute-start.35
  307.1 17.4 %collective-permute-done.33 = bf16[352,1536]{1,0:T(8,128)(2,1)S(1)} collective-permute-done((bf16[352,1536]{1,0:T(8,128)(2,1)S(1)}, bf16[352,1536]{1,0:T(8,128)(2,1)S(1)}, u32[]{:S(2)}, u32[]{:S(2)}) %collective-permute-start.33) | collective-permute-done | bytes 1081376 | tf_op jit(solution)/shard_map/ppermute | solution.py:35
  328.4 28.5 %collective-permute-done.37 = bf16[224,1536]{1,0:T(8,128)(2,1)S(1)} collective-permute-done((bf16[224,1536]{1,0:T(8,128)(2,1)S(1)}, bf16[224,1536]{1,0:T(8,128)(2,1)S(1)}, u32[]{:S(2)}, u32[]{:S(2)}) %collective-permute-start.37) | collective-permute-done | bytes 688160 | tf_op jit(solution)/shard_map/ppermute | solution.py:35
  (160 shorter events, 58.2 us)
Async XLA Ops:
  7.2 73.3 %all-gather.2.cloned.1.call-start = ((), (), s32[]{:S(2)}) async-start(), calls=%async_computation | async-start | bytes 10813440 | tf_op jit(solution)/shard_map/all_gather | solution.py:501
  16.1 58.1 %collective-permute-start.1 = (bf16[512,1408]{0,1:T(8,128)(2,1)}, bf16[512,1408]{0,1:T(8,128)(2,1)}, u32[]{:S(2)}, u32[]{:S(2)}) collective-permute-start(bf16[512,1408]{0,1:T(8,128)(2,1)} %copy.11), channel_id=1, source_target_pairs={{0,1},{1,0},{2,3},{3,2},{4,5},{5,4},{6,7},{7,6},{8,9},{9,8},{10,11... | collective-permute-start | bytes 4325384 | tf_op jit(solution)/shard_map/ppermute | solution.py:35
  19.1 54.3 %collective-permute-start = (bf16[352,1536]{1,0:T(8,128)(2,1)}, bf16[352,1536]{1,0:T(8,128)(2,1)}, u32[]{:S(2)}, u32[]{:S(2)}) collective-permute-start(bf16[352,1536]{1,0:T(8,128)(2,1)} %pad_maximum_fusion.2), channel_id=1, source_target_pairs={{0,2},{1,3},{2,0},{3,1},{4,6},{5,7},{6,4},{7,5},{8,10},{9,11},{10,... | collective-permute-start | bytes 3244040 | tf_op jit(solution)/shard_map/ppermute | solution.py:35
  74.2 28.0 %collective-permute-start.5 = (bf16[512,1408]{1,0:T(8,128)(2,1)}, bf16[512,1408]{1,0:T(8,128)(2,1)}, u32[]{:S(2)}, u32[]{:S(2)}) collective-permute-start(bf16[512,1408]{1,0:T(8,128)(2,1)} %get-tuple-element.124), channel_id=1, source_target_pairs={{0,4},{4,0},{8,12},{12,8},{1,5},{5,1},{9,13},{13,9},{2,6},{6,2},{1... | collective-permute-start | bytes 4325384 | tf_op jit(solution)/shard_map/ppermute | solution.py:35
  74.2 17.1 %collective-permute-start.4 = (bf16[352,1536]{1,0:T(8,128)(2,1)}, bf16[352,1536]{1,0:T(8,128)(2,1)}, u32[]{:S(2)}, u32[]{:S(2)}) collective-permute-start(bf16[352,1536]{1,0:T(8,128)(2,1)} %collective-permute-done.refs_0_), channel_id=1, source_target_pairs={{0,4},{4,0},{8,12},{12,8},{1,5},{5,1},{9,13},{13,9},{2,6},{6,2},{1... | collective-permute-start | bytes 3244040 | tf_op jit(solution)/shard_map/ppermute | solution.py:35
  74.7 26.0 %collective-permute-start.3 = (bf16[352,1536]{1,0:T(8,128)(2,1)}, bf16[352,1536]{1,0:T(8,128)(2,1)S(1)}, u32[]{:S(2)}, u32[]{:S(2)}) collective-permute-start(bf16[352,1536]{1,0:T(8,128)(2,1)} %collective-permute-done.refs_0_), channel_id=1, source_target_pairs={{0,16},{16,0},{1,17},{17,1},{2,18},{18,2},{3,19},{19,3},{4,20},{20... | collective-permute-start | bytes 3244040 | tf_op jit(solution)/shard_map/ppermute | solution.py:35
  76.4 25.8 %collective-permute-start.2 = (bf16[352,1536]{1,0:T(8,128)(2,1)}, bf16[352,1536]{1,0:T(8,128)(2,1)}, u32[]{:S(2)}, u32[]{:S(2)}) collective-permute-start(bf16[352,1536]{1,0:T(8,128)(2,1)} %collective-permute-done.refs_0_), channel_id=1, source_target_pairs={{0,8},{4,12},{8,0},{12,4},{1,9},{5,13},{9,1},{13,5},{2,10},{6,14},... | collective-permute-start | bytes 3244040 | tf_op jit(solution)/shard_map/ppermute | solution.py:35
  102.2 19.2 %collective-permute-start.9 = (bf16[352,1536]{1,0:T(8,128)(2,1)}, bf16[352,1536]{1,0:T(8,128)(2,1)S(1)}, u32[]{:S(2)}, u32[]{:S(2)}) collective-permute-start(bf16[352,1536]{1,0:T(8,128)(2,1)} %collective-permute-done.2.refs_4_), channel_id=1, source_target_pairs={{0,4},{4,0},{8,12},{12,8},{1,5},{5,1},{9,13},{13,9},{2,6},{6,2},{1... | collective-permute-start | bytes 3244040 | tf_op jit(solution)/shard_map/ppermute | solution.py:35
  102.2 19.2 %collective-permute-start.8 = (bf16[352,1536]{1,0:T(8,128)(2,1)S(1)}, bf16[352,1536]{1,0:T(8,128)(2,1)S(1)}, u32[]{:S(2)}, u32[]{:S(2)}) collective-permute-start(bf16[352,1536]{1,0:T(8,128)(2,1)S(1)} %collective-permute-done.3.refs_2_), channel_id=1, source_target_pairs={{0,4},{4,0},{8,12},{12,8},{1,5},{5,1},{9,13},{13,9},{2,6},{6,2},{1... | collective-permute-start | bytes 3244040 | tf_op jit(solution)/shard_map/ppermute | solution.py:35
  105.5 15.9 %collective-permute-start.7 = (bf16[176,1536]{1,0:T(8,128)(2,1)}, bf16[176,1536]{1,0:T(8,128)(2,1)S(1)}, u32[]{:S(2)}, u32[]{:S(2)}) collective-permute-start(bf16[176,1536]{1,0:T(8,128)(2,1)} %slice.62), channel_id=1, source_target_pairs={{0,8},{4,12},{8,0},{12,4},{1,9},{5,13},{9,1},{13,5},{2,10},{6,14},... | collective-permute-start | bytes 1622024 | tf_op jit(solution)/shard_map/ppermute | solution.py:35
  107.0 14.4 %collective-permute-start.6 = (bf16[176,1536]{1,0:T(8,128)(2,1)}, bf16[176,1536]{1,0:T(8,128)(2,1)}, u32[]{:S(2)}, u32[]{:S(2)}) collective-permute-start(bf16[176,1536]{1,0:T(8,128)(2,1)} %slice.61), channel_id=1, source_target_pairs={{0,16},{16,0},{1,17},{17,1},{2,18},{18,2},{3,19},{19,3},{4,20},{20... | collective-permute-start | bytes 1622024 | tf_op jit(solution)/shard_map/ppermute | solution.py:35
  125.4 13.2 %collective-permute-start.12 = (bf16[512,1408]{1,0:T(8,128)(2,1)}, bf16[512,1408]{1,0:T(8,128)(2,1)}, u32[]{:S(2)}, u32[]{:S(2)}) collective-permute-start(bf16[512,1408]{1,0:T(8,128)(2,1)} %get-tuple-element.141), channel_id=1, source_target_pairs={{0,4},{4,0},{8,12},{12,8},{1,5},{5,1},{9,13},{13,9},{2,6},{6,2},{1... | collective-permute-start | bytes 4325384 | tf_op jit(solution)/shard_map/ppermute | solution.py:35
  125.6 38.2 %collective-permute-start.13 = (bf16[512,1408]{1,0:T(8,128)(2,1)}, bf16[512,1408]{1,0:T(8,128)(2,1)}, u32[]{:S(2)}, u32[]{:S(2)}) collective-permute-start(bf16[512,1408]{1,0:T(8,128)(2,1)} %add_convert_fusion), channel_id=1, source_target_pairs={{0,8},{4,12},{8,0},{12,4},{1,9},{5,13},{9,1},{13,5},{2,10},{6,14},... | collective-permute-start | bytes 4325384 | tf_op jit(solution)/shard_map/ppermute | solution.py:35
  147.3 34.9 %collective-permute-start.14 = (bf16[512,1408]{1,0:T(8,128)(2,1)}, bf16[512,1408]{1,0:T(8,128)(2,1)S(1)}, u32[]{:S(2)}, u32[]{:S(2)}) collective-permute-start(bf16[512,1408]{1,0:T(8,128)(2,1)} %branch_far.1), channel_id=1, source_target_pairs={{0,1},{1,0},{2,3},{3,2},{4,5},{5,4},{6,7},{7,6},{8,9},{9,8},{10,11... | collective-permute-start | bytes 4325384 | tf_op jit(solution)/shard_map/ppermute | solution.py:35
  186.7 33.2 %collective-permute-start.15 = (bf16[512,1408]{1,0:T(8,128)(2,1)S(1)}, bf16[512,1408]{1,0:T(8,128)(2,1)}, u32[]{:S(2)}, u32[]{:S(2)}) collective-permute-start(bf16[512,1408]{1,0:T(8,128)(2,1)S(1)} %multiply_convert_fusion.go), channel_id=1, source_target_pairs={{0,1},{1,0},{2,3},{3,2},{4,5},{5,4},{6,7},{7,6},{8,9},{9,8},{10,11... | collective-permute-start | bytes 4325384 | tf_op jit(solution)/shard_map/ppermute | solution.py:35
  228.6 13.3 %collective-permute-start.20 = (bf16[352,1536]{1,0:T(8,128)(2,1)S(1)}, bf16[352,1536]{1,0:T(8,128)(2,1)S(1)}, u32[]{:S(2)}, u32[]{:S(2)}) collective-permute-start(bf16[352,1536]{1,0:T(8,128)(2,1)S(1)} %get-tuple-element.175), channel_id=1, source_target_pairs={{0,4},{4,0},{8,12},{12,8},{1,5},{5,1},{9,13},{13,9},{2,6},{6,2},{1... | collective-permute-start | bytes 3244040 | tf_op jit(solution)/shard_map/ppermute | solution.py:35
  231.4 11.2 %collective-permute-start.19 = (bf16[128,1536]{1,0:T(8,128)(2,1)S(1)}, bf16[128,1536]{1,0:T(8,128)(2,1)S(1)}, u32[]{:S(2)}, u32[]{:S(2)}) collective-permute-start(bf16[128,1536]{1,0:T(8,128)(2,1)S(1)} %add_convert_fusion.9), channel_id=1, source_target_pairs={{0,8},{4,12},{8,0},{12,4},{1,9},{5,13},{9,1},{13,5},{2,10},{6,14},... | collective-permute-start | bytes 1179656 | tf_op jit(solution)/shard_map/ppermute | solution.py:35
  242.8 22.2 %collective-permute-start.22 = (bf16[352,1536]{1,0:T(8,128)(2,1)S(1)}, bf16[352,1536]{1,0:T(8,128)(2,1)S(1)}, u32[]{:S(2)}, u32[]{:S(2)}) collective-permute-start(bf16[352,1536]{1,0:T(8,128)(2,1)S(1)} %get-tuple-element.185), channel_id=1, source_target_pairs={{0,4},{4,0},{8,12},{12,8},{1,5},{5,1},{9,13},{13,9},{2,6},{6,2},{1... | collective-permute-start | bytes 3244040 | tf_op jit(solution)/shard_map/ppermute | solution.py:35
  242.9 22.1 %collective-permute-start.23 = (bf16[352,1536]{1,0:T(8,128)(2,1)S(1)}, bf16[352,1536]{1,0:T(8,128)(2,1)S(1)}, u32[]{:S(2)}, u32[]{:S(2)}) collective-permute-start(bf16[352,1536]{1,0:T(8,128)(2,1)S(1)} %get-tuple-element.187), channel_id=1, source_target_pairs={{0,4},{4,0},{8,12},{12,8},{1,5},{5,1},{9,13},{13,9},{2,6},{6,2},{1... | collective-permute-start | bytes 3244040 | tf_op jit(solution)/shard_map/ppermute | solution.py:35
  243.4 19.3 %collective-permute-start.21 = (bf16[224,1536]{1,0:T(8,128)(2,1)S(1)}, bf16[224,1536]{1,0:T(8,128)(2,1)S(1)}, u32[]{:S(2)}, u32[]{:S(2)}) collective-permute-start(bf16[224,1536]{1,0:T(8,128)(2,1)S(1)} %add_convert_fusion.6), channel_id=1, source_target_pairs={{0,8},{4,12},{8,0},{12,4},{1,9},{5,13},{9,1},{13,5},{2,10},{6,14},... | collective-permute-start | bytes 2064392 | tf_op jit(solution)/shard_map/ppermute | solution.py:35
  244.9 20.1 %collective-permute-start.24 = (bf16[128,1536]{1,0:T(8,128)(2,1)S(1)}, bf16[128,1536]{1,0:T(8,128)(2,1)S(1)}, u32[]{:S(2)}, u32[]{:S(2)}) collective-permute-start(bf16[128,1536]{1,0:T(8,128)(2,1)S(1)} %add_convert_fusion.8), channel_id=1, source_target_pairs={{0,2},{1,3},{2,0},{3,1},{4,6},{5,7},{6,4},{7,5},{8,10},{9,11},{10,... | collective-permute-start | bytes 1179656 | tf_op jit(solution)/shard_map/ppermute | solution.py:35
  265.0 10.9 %collective-permute-start.25 = (bf16[352,1536]{1,0:T(8,128)(2,1)S(1)}, bf16[352,1536]{1,0:T(8,128)(2,1)S(1)}, u32[]{:S(2)}, u32[]{:S(2)}) collective-permute-start(bf16[352,1536]{1,0:T(8,128)(2,1)S(1)} %get-tuple-element.188), channel_id=1, source_target_pairs={{0,4},{4,0},{8,12},{12,8},{1,5},{5,1},{9,13},{13,9},{2,6},{6,2},{1... | collective-permute-start | bytes 3244040 | tf_op jit(solution)/shard_map/ppermute | solution.py:35
  265.1 10.8 %collective-permute-start.26 = (bf16[352,1536]{1,0:T(8,128)(2,1)S(1)}, bf16[352,1536]{1,0:T(8,128)(2,1)S(1)}, u32[]{:S(2)}, u32[]{:S(2)}) collective-permute-start(bf16[352,1536]{1,0:T(8,128)(2,1)S(1)} %get-tuple-element.189), channel_id=1, source_target_pairs={{0,4},{4,0},{8,12},{12,8},{1,5},{5,1},{9,13},{13,9},{2,6},{6,2},{1... | collective-permute-start | bytes 3244040 | tf_op jit(solution)/shard_map/ppermute | solution.py:35
  276.2 26.9 %collective-permute-start.29 = (bf16[352,1536]{1,0:T(8,128)(2,1)S(1)}, bf16[352,1536]{1,0:T(8,128)(2,1)S(1)}, u32[]{:S(2)}, u32[]{:S(2)}) collective-permute-start(bf16[352,1536]{1,0:T(8,128)(2,1)S(1)} %add_convert_fusion.2), channel_id=1, source_target_pairs={{0,8},{4,12},{8,0},{12,4},{1,9},{5,13},{9,1},{13,5},{2,10},{6,14},... | collective-permute-start | bytes 3244040 | tf_op jit(solution)/shard_map/ppermute | solution.py:35
  276.9 25.2 %collective-permute-start.30 = (bf16[176,1536]{1,0:T(8,128)(2,1)S(1)}, bf16[176,1536]{1,0:T(8,128)(2,1)S(1)}, u32[]{:S(2)}, u32[]{:S(2)}) collective-permute-start(bf16[176,1536]{1,0:T(8,128)(2,1)S(1)} %slice.84), channel_id=1, source_target_pairs={{0,2},{1,3},{2,0},{3,1},{4,6},{5,7},{6,4},{7,5},{8,10},{9,11},{10,... | collective-permute-start | bytes 1622024 | tf_op jit(solution)/shard_map/ppermute | solution.py:35
  276.9 47.5 %collective-permute-start.33 = (bf16[352,1536]{1,0:T(8,128)(2,1)S(1)}, bf16[352,1536]{1,0:T(8,128)(2,1)S(1)}, u32[]{:S(2)}, u32[]{:S(2)}) collective-permute-start(bf16[352,1536]{1,0:T(8,128)(2,1)S(1)} %add_convert_fusion.3), channel_id=1, source_target_pairs={{0,8},{4,12},{8,0},{12,4},{1,9},{5,13},{9,1},{13,5},{2,10},{6,14},... | collective-permute-start | bytes 3244040 | tf_op jit(solution)/shard_map/ppermute | solution.py:35
  303.6 20.9 %collective-permute-start.31 = (bf16[352,1536]{1,0:T(8,128)(2,1)S(1)}, bf16[352,1536]{1,0:T(8,128)(2,1)S(1)}, u32[]{:S(2)}, u32[]{:S(2)}) collective-permute-start(bf16[352,1536]{1,0:T(8,128)(2,1)S(1)} %get-tuple-element.208), channel_id=1, source_target_pairs={{0,4},{4,0},{8,12},{12,8},{1,5},{5,1},{9,13},{13,9},{2,6},{6,2},{1... | collective-permute-start | bytes 3244040 | tf_op jit(solution)/shard_map/ppermute | solution.py:35
  303.6 20.8 %collective-permute-start.32 = (bf16[352,1536]{1,0:T(8,128)(2,1)S(1)}, bf16[352,1536]{1,0:T(8,128)(2,1)S(1)}, u32[]{:S(2)}, u32[]{:S(2)}) collective-permute-start(bf16[352,1536]{1,0:T(8,128)(2,1)S(1)} %get-tuple-element.210), channel_id=1, source_target_pairs={{0,4},{4,0},{8,12},{12,8},{1,5},{5,1},{9,13},{13,9},{2,6},{6,2},{1... | collective-permute-start | bytes 3244040 | tf_op jit(solution)/shard_map/ppermute | solution.py:35
  304.1 20.3 %collective-permute-start.34 = (bf16[128,1536]{1,0:T(8,128)(2,1)S(1)}, bf16[128,1536]{1,0:T(8,128)(2,1)S(1)}, u32[]{:S(2)}, u32[]{:S(2)}) collective-permute-start(bf16[128,1536]{1,0:T(8,128)(2,1)S(1)} %add_convert_fusion.7), channel_id=1, source_target_pairs={{0,2},{1,3},{2,0},{3,1},{4,6},{5,7},{6,4},{7,5},{8,10},{9,11},{10,... | collective-permute-start | bytes 1179656 | tf_op jit(solution)/shard_map/ppermute | solution.py:35
  304.1 20.3 %collective-permute-start.35 = (f32[8,128]{1,0:T(8,128)S(1)}, f32[8,128]{1,0:T(8,128)S(1)}, u32[]{:S(2)}, u32[]{:S(2)}) collective-permute-start(f32[8,128]{1,0:T(8,128)S(1)} %add.161), channel_id=1, source_target_pairs={{0,2},{1,3},{2,0},{3,1},{4,6},{5,7},{6,4},{7,5},{8,10},{9,11},{10,... | collective-permute-start | bytes 12296 | tf_op jit(solution)/shard_map/ppermute | solution.py:35
  324.8 32.1 %collective-permute-start.36 = (bf16[352,1536]{1,0:T(8,128)(2,1)S(1)}, bf16[352,1536]{1,0:T(8,128)(2,1)S(1)}, u32[]{:S(2)}, u32[]{:S(2)}) collective-permute-start(bf16[352,1536]{1,0:T(8,128)(2,1)S(1)} %add_convert_fusion.1), channel_id=1, source_target_pairs={{0,8},{4,12},{8,0},{12,4},{1,9},{5,13},{9,1},{13,5},{2,10},{6,14},... | collective-permute-start | bytes 3244040 | tf_op jit(solution)/shard_map/ppermute | solution.py:35
  325.4 31.5 %collective-permute-start.37 = (bf16[224,1536]{1,0:T(8,128)(2,1)S(1)}, bf16[224,1536]{1,0:T(8,128)(2,1)S(1)}, u32[]{:S(2)}, u32[]{:S(2)}) collective-permute-start(bf16[224,1536]{1,0:T(8,128)(2,1)S(1)} %add_convert_fusion.4), channel_id=1, source_target_pairs={{0,2},{1,3},{2,0},{3,1},{4,6},{5,7},{6,4},{7,5},{8,10},{9,11},{10,... | collective-permute-start | bytes 2064392 | tf_op jit(solution)/shard_map/ppermute | solution.py:35
  (35 other events, 330.5 us)
Sparse Core Ops, SparseCore 0:
  10.4 62.7 all-gather.1

commit v6 on v5

--- a/solution.py
+++ b/solution.py
@@ -517,13 +517,15 @@
     zgc = swap(z_g, "mx", 1)
     q3c = swap(q3, "mx", 1)
     pre_near, act_near = forward_part(normed_own, normed_pair, near)
-    pre_near, act_near, d_g, z_o, zgc, q3c = together(pre_near, act_near, d_g, z_o, zgc, q3c)
+    near_share = branch_near_part(act_near, near)
+    pre_near, act_near, near_share, d_g, z_o, zgc, q3c = together(
+        pre_near, act_near, near_share, d_g, z_o, zgc, q3c
+    )
     in_do = swap(d_g[:half], "group", 1)
     out_do = swap(z_o[half:], "mx", 2)
     zoc, dgc = swap(z_o, "mx", 1), swap(d_g, "mx", 1)
     t2 = (q2.astype(F32) + q3c.astype(F32)).astype(BF16)
-    near_share = branch_near_part(after(act_near, t2), near)
-    in_do, out_do, zoc, dgc, near_share = together(in_do, out_do, zoc, dgc, near_share)
+    in_do, out_do, zoc, dgc, t2 = together(in_do, out_do, zoc, dgc, t2)
     in_doc, out_doc = swap(in_do, "mx", 1), swap(out_do, "mx", 1)
     in_doc, out_doc = together(in_doc, out_doc)
 

time: 368 us -> 366 us (level)
    unnamed x56 -> x58, local copies, waits for them, and re-layouts: 7.05 us -> 7.69 us
  transfers between devices with their start and end apart: 39 -> 39, of which waited for: 17 -> 18; matrix products, arithmetic and copies ran while one was open for 9% -> 9% of each run, Pallas kernels for 32% -> 32%
where the time goes in v6:
time: 366 us; the launch traced here: 365 us
  waiting for transfers between devices  127 us (35%)
  Pallas kernels  125 us (34%)
  starting transfers between devices  33.3 us (9%)
  other arithmetic  31.6 us (9%)
  local copies, waits for them, and re-layouts  19.2 us (5%)
  between operations  16.2 us (4%)
  blocking collectives  12.3 us (3%)
    ppermute x38, waiting for transfers between devices, swap(): return lax.ppermute(value, axis, [(i, i ^ bit) for i in range(count)])  127 us
    ppermute x38, starting transfers between devices, swap(): return lax.ppermute(value, axis, [(i, i ^ bit) for i in range(count)])  33.3 us
    pallas_call x2, Pallas kernels, grad_in_part(): pl.pallas_call(body, grid=(cols // FC,), in_specs=[pl.BlockSpec(memory_sp...  27.3 us
    pallas_call x1, Pallas kernels, target_parts(): pl.pallas_call(body, grid_spec=pltpu.PrefetchScalarGridSpec(num_scalar_pr...  18.4 us
    pallas_call x2, Pallas kernels, grad_out_part(): pl.pallas_call(body, grid=(cols // FC,), in_specs=[pl.BlockSpec(memory_sp...  17.5 us
    add x2, other arithmetic, gelu_slope(): 0.5 * (1.0 + lax.erf(value * 0.7071067811865476))  12.6 us
    psum x1, blocking collectives, pair_shards(): sums = lax.psum(sums[:2], 'mx')  12.3 us
    pallas_call x1, Pallas kernels, forward_pieces(): pl.pallas_call(body, grid=(cols // FC,), in_specs=[pl.BlockSpec(memory_sp...  11.9 us
  transfers between devices with their start and end apart: 39, of which 18 were waited for; matrix products, arithmetic and copies ran while one was open for 9% of the time, Pallas kernels for 32%

profile of v6, /device:TPU:0, one launch (start us, length us, event | category | flops | bytes accessed | tf_op | source)
XLA Modules:
  0.0 365.4 jit_solution(14614249927554070898)
XLA Ops:
  7.2 3.0 pad_maximum_fusion.1
  16.1 3.0 collective-permute-start.1
  19.2 2.6 collective-permute-start
  21.8 5.6 %teacher_sums.1 = f32[8,2048]{1,0:T(8,128)} custom-call(bf16[2048,1536]{1,0:T(8,128)(2,1)} %bitcast.38), custom_call_target="tpu_custom_call" | custom-call | flops 1000 | bytes 1000 | tf_op jit(solution)/shard_map/teacher_sums/pallas_call | solution.py:102
  29.4 12.3 %psum.7.s_ref = f32[2,2048]{1,0:T(2,128)} all-reduce(f32[2,2048]{1,0:T(2,128)S(1)} %slice.80), channel_id=1, replica_groups=mesh['group'=2,'mx'=4,'my'=4] {'mx'}, use_global_device_ids=true, to_apply=%region_0.0 | all-reduce | flops 4096 | bytes 32768 | tf_op jit(solution)/shard_map/psum | solution.py:509
  41.8 18.4 %targets.1 = (bf16[512,1408]{1,0:T(8,128)(2,1)}, bf16[512,1408]{1,0:T(8,128)(2,1)}, bf16[512,1408]{1,0:T(8,128)(2,1)}, bf16[512,1408]{1,0:T(8,128)(2,1)}) custom-call(s32[1]{0:T(128)} %bitcast.2.mx_ref, bf16[2048,1536]{1,0:T(8,128)(2,1)} %bitcast.39, f32[2,2048]{1,0:T(2,128)} %psum.7.s_ref, f32[1,1536]{1,0:T(1,128)} %reshape.43.g_ref, ...), custom_call_target="tpu_custom_call" | custom-call | flops 1000 | bytes 1000 | tf_op jit(solution)/shard_map/targets/pallas_call | solution.py:137
  60.2 13.3 %collective-permute-done.refs_0_ = bf16[352,1536]{1,0:T(8,128)(2,1)} collective-permute-done((bf16[352,1536]{1,0:T(8,128)(2,1)}, bf16[352,1536]{1,0:T(8,128)(2,1)}, u32[]{:S(2)}, u32[]{:S(2)}) %collective-permute-start) | collective-permute-done | bytes 1081376 | tf_op jit(solution)/shard_map/ppermute | solution.py:35
  80.5 10.8 %forward.1 = (f32[1024,1536]{1,0:T(8,128)}, bf16[1024,1536]{1,0:T(8,128)(2,1)}) custom-call(bf16[512,1408]{1,0:T(8,128)(2,1)} %copy-done, bf16[512,1408]{1,0:T(8,128)(2,1)} %copy.12.np_, bf16[4,2,352,1536]{3,2,1,0:T(8,128)(2,1)} %bitcast.30), custom_call_target="tpu_custom_call" | custom-call | flops 1000 | bytes 1000 | tf_op jit(solution)/shard_map/forward/pallas_call | solution.py:199
  91.3 11.1 %branch_near.1.nr = f32[1024,1408]{1,0:T(8,128)} custom-call(bf16[1024,1536]{1,0:T(8,128)(2,1)} %get-tuple-element.170.a, bf16[4,2,352,1536]{3,2,1,0:T(8,128)(2,1)} %bitcast.31), custom_call_target="tpu_custom_call" | custom-call | flops 1000 | bytes 1000 | tf_op jit(solution)/shard_map/branch_near/pallas_call | solution.py:328
  106.0 2.8 add_convert_fusion
  108.8 9.7 %collective-permute-done.6.refs_6_ = bf16[176,1536]{1,0:T(8,128)(2,1)S(1)} collective-permute-done((bf16[176,1536]{1,0:T(8,128)(2,1)S(1)}, bf16[176,1536]{1,0:T(8,128)(2,1)S(1)}, u32[]{:S(2)}, u32[]{:S(2)}) %collective-permute-start.6) | collective-permute-done | bytes 540704 | tf_op jit(solution)/shard_map/ppermute | solution.py:35
  125.5 11.9 %forward_far.1 = (f32[1024,1536]{1,0:T(8,128)}, bf16[1024,1536]{1,0:T(8,128)(2,1)}) custom-call(s32[8]{0:T(128)} %stack.71.offs_ref, bf16[512,1408]{1,0:T(8,128)(2,1)} %copy-done, bf16[512,1408]{1,0:T(8,128)(2,1)} %copy.12.np_, bf16[352,1536]{1,0:T(8,128)(2,1)} %collective-permute-done.refs_0_, bf16[352,1536]{1,0:T(8,128)(2,1)} %collective-permute-done.4.refs_1_, ...), custom_call_target="tpu_custom_call" | custom-call | flops 1000 | bytes 1000 | tf_op jit(solution)/shard_map/forward_far/pallas_call | solution.py:238
  137.4 8.6 %branch_far.1 = bf16[512,1408]{1,0:T(8,128)(2,1)} custom-call(s32[8]{0:T(128)} %stack.71.offs_ref, f32[1024,1408]{1,0:T(8,128)} %branch_near.1.nr, bf16[1024,1536]{1,0:T(8,128)(2,1)} %get-tuple-element.140.a, bf16[352,1536]{1,0:T(8,128)(2,1)} %collective-permute-done.refs_0_, bf16[352,1536]{1,0:T(8,128)(2,1)} %collective-permute-done.4.refs_1_, ...), custom_call_target="tpu_custom_call" | custom-call | flops 1000 | bytes 1000 | tf_op jit(solution)/shard_map/branch_far/pallas_call | solution.py:281
  146.1 2.7 collective-permute-start.14
  149.3 5.0 %assemble.1.w = bf16[1408,1536]{1,0:T(8,128)(2,1)} custom-call(s32[8]{0:T(128)} %stack.80.offs_ref, bf16[352,1536]{1,0:T(8,128)(2,1)} %collective-permute-done.refs_0_, bf16[352,1536]{1,0:T(8,128)(2,1)} %collective-permute-done.4.refs_1_, bf16[352,1536]{1,0:T(8,128)(2,1)} %copy-done.7, bf16[352,1536]{1,0:T(8,128)(2,1)} %copy-done.9, ...), custom_call_target="tpu_custom_call" | custom-call | flops 1000 | bytes 1000 | tf_op jit(solution)/shard_map/assemble/pallas_call | solution.py:68
  154.3 8.0 %branch.1 = f32[512,1408]{1,0:T(8,128)} custom-call(f32[1024,1408]{1,0:T(8,128)} %branch_near.1.nr, bf16[1024,1536]{1,0:T(8,128)(2,1)} %get-tuple-element.140.a, bf16[1408,1536]{1,0:T(8,128)(2,1)} %assemble.1.w), custom_call_target="tpu_custom_call" | custom-call | flops 1000 | bytes 1000 | tf_op jit(solution)/shard_map/branch/pallas_call | solution.py:362
  162.3 8.5 %fusion.3.sl = f32[1024,1536]{1,0:T(8,128)} fusion(f32[1024,1536]{1,0:T(8,128)} %get-tuple-element.154), kind=kLoop, calls=%fused_computation.5 | loop fusion | flops 12582912 | bytes 12582912 | tf_op jit(solution)/shard_map/add | solution.py:28
  170.8 9.9 %collective-permute-done.14 = bf16[512,1408]{1,0:T(8,128)(2,1)S(1)} collective-permute-done((bf16[512,1408]{1,0:T(8,128)(2,1)}, bf16[512,1408]{1,0:T(8,128)(2,1)S(1)}, u32[]{:S(2)}, u32[]{:S(2)}) %collective-permute-start.14) | collective-permute-done | bytes 1441824 | tf_op jit(solution)/shard_map/ppermute | solution.py:35
  180.8 3.7 %multiply_reduce_fusion = (f32[]{:T(128)}, f32[512,1408]{1,0:T(8,128)S(1)}) fusion(bf16[512,1408]{1,0:T(8,128)(2,1)} %collective-permute-done.13, bf16[512,1408]{1,0:T(8,128)(2,1)} %collective-permute-done.12, bf16[512,1408]{1,0:T(8,128)(2,1)S(1)} %copy-done.15, f32[512,1408]{1,0:T(8,128)S(1)} %copy-done.8, ...), kind=kLoop, calls=%fused_computation.11 | loop fusion | flops 8650751 | bytes 12976132 | tf_op jit(solution)/shard_map/reduce_sum | solution.py:562
  187.2 4.1 %fusion.7.sl = f32[1024,1536]{1,0:T(8,128)} fusion(f32[1024,1536]{1,0:T(8,128)S(1)} %bitcast.41), kind=kLoop, calls=%fused_computation.9 | loop fusion | flops 12582912 | bytes 12582912 | tf_op jit(solution)/shard_map/add | solution.py:28
  196.5 22.1 %collective-permute-done.15.gp = bf16[512,1408]{1,0:T(8,128)(2,1)} collective-permute-done((bf16[512,1408]{1,0:T(8,128)(2,1)S(1)}, bf16[512,1408]{1,0:T(8,128)(2,1)}, u32[]{:S(2)}, u32[]{:S(2)}) %collective-permute-start.15) | collective-permute-done | bytes 1441824 | tf_op jit(solution)/shard_map/ppermute | solution.py:35
  218.6 8.6 %grad_out.2 = (bf16[352,1536]{1,0:T(8,128)(2,1)S(1)}, bf16[352,1536]{1,0:T(8,128)(2,1)S(1)}, bf16[352,1536]{1,0:T(8,128)(2,1)S(1)}, bf16[352,1536]{1,0:T(8,128)(2,1)S(1)}) custom-call(s32[1]{0:T(128)} %bitcast.2.mx_ref, bf16[512,1408]{1,0:T(8,128)(2,1)S(1)} %multiply_convert_fusion.go, bf16[512,1408]{1,0:T(8,128)(2,1)} %collective-permute-done.15.gp, ...), custom_call_target="tpu_custom_call" | custom-call | flops 1000 | bytes 1000 | tf_op jit(solution)/shard_map/grad_out/pallas_call | solution.py:413
  231.8 8.9 %grad_out.3 = (bf16[352,1536]{1,0:T(8,128)(2,1)S(1)}, bf16[352,1536]{1,0:T(8,128)(2,1)S(1)}, bf16[352,1536]{1,0:T(8,128)(2,1)S(1)}, bf16[352,1536]{1,0:T(8,128)(2,1)S(1)}) custom-call(s32[1]{0:T(128)} %bitcast.2.mx_ref, bf16[512,1408]{1,0:T(8,128)(2,1)S(1)} %multiply_convert_fusion.go, bf16[512,1408]{1,0:T(8,128)(2,1)} %collective-permute-done.15.gp, ...), custom_call_target="tpu_custom_call" | custom-call | flops 1000 | bytes 1000 | tf_op jit(solution)/shard_map/grad_out/pallas_call | solution.py:413
  244.2 2.8 copy-done.3
  247.0 13.7 %grad_in.2 = (bf16[352,1536]{1,0:T(8,128)(2,1)S(1)}, bf16[352,1536]{1,0:T(8,128)(2,1)S(1)}, bf16[352,1536]{1,0:T(8,128)(2,1)S(1)}, bf16[352,1536]{1,0:T(8,128)(2,1)S(1)}) custom-call(s32[1]{0:T(128)} %bitcast.2.mx_ref, bf16[512,1408]{1,0:T(8,128)(2,1)S(1)} %multiply_convert_fusion.go, bf16[512,1408]{1,0:T(8,128)(2,1)} %collective-permute-done.15.gp, ...), custom_call_target="tpu_custom_call" | custom-call | flops 1000 | bytes 1000 | tf_op jit(solution)/shard_map/grad_in/pallas_call | solution.py:444
  264.0 2.8 collective-permute-start.28
  267.6 6.4 %collective-permute-done.28 = bf16[48,1536]{1,0:T(8,128)(2,1)S(1)} collective-permute-done((bf16[48,1536]{1,0:T(8,128)(2,1)S(1)}, bf16[48,1536]{1,0:T(8,128)(2,1)S(1)}, u32[]{:S(2)}, u32[]{:S(2)}) %collective-permute-start.28) | collective-permute-done | bytes 147488 | tf_op jit(solution)/shard_map/ppermute | solution.py:35
  276.5 13.6 %grad_in.3 = (bf16[352,1536]{1,0:T(8,128)(2,1)S(1)}, bf16[352,1536]{1,0:T(8,128)(2,1)S(1)}, bf16[352,1536]{1,0:T(8,128)(2,1)S(1)}, bf16[352,1536]{1,0:T(8,128)(2,1)S(1)}) custom-call(s32[1]{0:T(128)} %bitcast.2.mx_ref, bf16[512,1408]{1,0:T(8,128)(2,1)S(1)} %multiply_convert_fusion.go, bf16[512,1408]{1,0:T(8,128)(2,1)} %collective-permute-done.15.gp, ...), custom_call_target="tpu_custom_call" | custom-call | flops 1000 | bytes 1000 | tf_op jit(solution)/shard_map/grad_in/pallas_call | solution.py:444
  290.1 10.6 %collective-permute-done.30 = bf16[176,1536]{1,0:T(8,128)(2,1)S(1)} collective-permute-done((bf16[176,1536]{1,0:T(8,128)(2,1)S(1)}, bf16[176,1536]{1,0:T(8,128)(2,1)S(1)}, u32[]{:S(2)}, u32[]{:S(2)}) %collective-permute-start.30) | collective-permute-done | bytes 540704 | tf_op jit(solution)/shard_map/ppermute | solution.py:35
  302.2 2.9 collective-permute-start.35
  305.1 17.4 %collective-permute-done.33 = bf16[352,1536]{1,0:T(8,128)(2,1)S(1)} collective-permute-done((bf16[352,1536]{1,0:T(8,128)(2,1)S(1)}, bf16[352,1536]{1,0:T(8,128)(2,1)S(1)}, u32[]{:S(2)}, u32[]{:S(2)}) %collective-permute-start.33) | collective-permute-done | bytes 1081376 | tf_op jit(solution)/shard_map/ppermute | solution.py:35
  327.1 28.5 %collective-permute-done.37 = bf16[224,1536]{1,0:T(8,128)(2,1)S(1)} collective-permute-done((bf16[224,1536]{1,0:T(8,128)(2,1)S(1)}, bf16[224,1536]{1,0:T(8,128)(2,1)S(1)}, u32[]{:S(2)}, u32[]{:S(2)}) %collective-permute-start.37) | collective-permute-done | bytes 688160 | tf_op jit(solution)/shard_map/ppermute | solution.py:35
  (162 shorter events, 55.7 us)
Async XLA Ops:
  7.2 73.3 %all-gather.2.cloned.1.call-start = ((), (), s32[]{:S(2)}) async-start(), calls=%async_computation | async-start | bytes 10813440 | tf_op jit(solution)/shard_map/all_gather | solution.py:501
  16.1 58.1 %collective-permute-start.1 = (bf16[512,1408]{0,1:T(8,128)(2,1)}, bf16[512,1408]{0,1:T(8,128)(2,1)}, u32[]{:S(2)}, u32[]{:S(2)}) collective-permute-start(bf16[512,1408]{0,1:T(8,128)(2,1)} %copy.11), channel_id=1, source_target_pairs={{0,1},{1,0},{2,3},{3,2},{4,5},{5,4},{6,7},{7,6},{8,9},{9,8},{10,11... | collective-permute-start | bytes 4325384 | tf_op jit(solution)/shard_map/ppermute | solution.py:35
  19.2 54.3 %collective-permute-start = (bf16[352,1536]{1,0:T(8,128)(2,1)}, bf16[352,1536]{1,0:T(8,128)(2,1)}, u32[]{:S(2)}, u32[]{:S(2)}) collective-permute-start(bf16[352,1536]{1,0:T(8,128)(2,1)} %pad_maximum_fusion.2), channel_id=1, source_target_pairs={{0,2},{1,3},{2,0},{3,1},{4,6},{5,7},{6,4},{7,5},{8,10},{9,11},{10,... | collective-permute-start | bytes 3244040 | tf_op jit(solution)/shard_map/ppermute | solution.py:35
  74.2 28.2 %collective-permute-start.5 = (bf16[512,1408]{1,0:T(8,128)(2,1)}, bf16[512,1408]{1,0:T(8,128)(2,1)}, u32[]{:S(2)}, u32[]{:S(2)}) collective-permute-start(bf16[512,1408]{1,0:T(8,128)(2,1)} %get-tuple-element.124), channel_id=1, source_target_pairs={{0,4},{4,0},{8,12},{12,8},{1,5},{5,1},{9,13},{13,9},{2,6},{6,2},{1... | collective-permute-start | bytes 4325384 | tf_op jit(solution)/shard_map/ppermute | solution.py:35
  74.2 28.2 %collective-permute-start.4 = (bf16[352,1536]{1,0:T(8,128)(2,1)}, bf16[352,1536]{1,0:T(8,128)(2,1)}, u32[]{:S(2)}, u32[]{:S(2)}) collective-permute-start(bf16[352,1536]{1,0:T(8,128)(2,1)} %collective-permute-done.refs_0_), channel_id=1, source_target_pairs={{0,4},{4,0},{8,12},{12,8},{1,5},{5,1},{9,13},{13,9},{2,6},{6,2},{1... | collective-permute-start | bytes 3244040 | tf_op jit(solution)/shard_map/ppermute | solution.py:35
  74.8 27.7 %collective-permute-start.3 = (bf16[352,1536]{1,0:T(8,128)(2,1)}, bf16[352,1536]{1,0:T(8,128)(2,1)S(1)}, u32[]{:S(2)}, u32[]{:S(2)}) collective-permute-start(bf16[352,1536]{1,0:T(8,128)(2,1)} %collective-permute-done.refs_0_), channel_id=1, source_target_pairs={{0,16},{16,0},{1,17},{17,1},{2,18},{18,2},{3,19},{19,3},{4,20},{20... | collective-permute-start | bytes 3244040 | tf_op jit(solution)/shard_map/ppermute | solution.py:35
  76.4 26.0 %collective-permute-start.2 = (bf16[352,1536]{1,0:T(8,128)(2,1)}, bf16[352,1536]{1,0:T(8,128)(2,1)}, u32[]{:S(2)}, u32[]{:S(2)}) collective-permute-start(bf16[352,1536]{1,0:T(8,128)(2,1)} %collective-permute-done.refs_0_), channel_id=1, source_target_pairs={{0,8},{4,12},{8,0},{12,4},{1,9},{5,13},{9,1},{13,5},{2,10},{6,14},... | collective-permute-start | bytes 3244040 | tf_op jit(solution)/shard_map/ppermute | solution.py:35
  102.4 16.3 %collective-permute-start.8 = (bf16[352,1536]{1,0:T(8,128)(2,1)S(1)}, bf16[352,1536]{1,0:T(8,128)(2,1)S(1)}, u32[]{:S(2)}, u32[]{:S(2)}) collective-permute-start(bf16[352,1536]{1,0:T(8,128)(2,1)S(1)} %collective-permute-done.3.refs_2_), channel_id=1, source_target_pairs={{0,4},{4,0},{8,12},{12,8},{1,5},{5,1},{9,13},{13,9},{2,6},{6,2},{1... | collective-permute-start | bytes 3244040 | tf_op jit(solution)/shard_map/ppermute | solution.py:35
  102.5 17.3 %collective-permute-start.9 = (bf16[352,1536]{1,0:T(8,128)(2,1)}, bf16[352,1536]{1,0:T(8,128)(2,1)S(1)}, u32[]{:S(2)}, u32[]{:S(2)}) collective-permute-start(bf16[352,1536]{1,0:T(8,128)(2,1)} %collective-permute-done.2.refs_4_), channel_id=1, source_target_pairs={{0,4},{4,0},{8,12},{12,8},{1,5},{5,1},{9,13},{13,9},{2,6},{6,2},{1... | collective-permute-start | bytes 3244040 | tf_op jit(solution)/shard_map/ppermute | solution.py:35
  104.3 14.2 %collective-permute-start.6 = (bf16[176,1536]{1,0:T(8,128)(2,1)S(1)}, bf16[176,1536]{1,0:T(8,128)(2,1)S(1)}, u32[]{:S(2)}, u32[]{:S(2)}) collective-permute-start(bf16[176,1536]{1,0:T(8,128)(2,1)S(1)} %slice.61), channel_id=1, source_target_pairs={{0,16},{16,0},{1,17},{17,1},{2,18},{18,2},{3,19},{19,3},{4,20},{20... | collective-permute-start | bytes 1622024 | tf_op jit(solution)/shard_map/ppermute | solution.py:35
  104.9 13.8 %collective-permute-start.7 = (bf16[176,1536]{1,0:T(8,128)(2,1)S(1)}, bf16[176,1536]{1,0:T(8,128)(2,1)S(1)}, u32[]{:S(2)}, u32[]{:S(2)}) collective-permute-start(bf16[176,1536]{1,0:T(8,128)(2,1)S(1)} %slice.62), channel_id=1, source_target_pairs={{0,8},{4,12},{8,0},{12,4},{1,9},{5,13},{9,1},{13,5},{2,10},{6,14},... | collective-permute-start | bytes 1622024 | tf_op jit(solution)/shard_map/ppermute | solution.py:35
  123.5 13.9 %collective-permute-start.12 = (bf16[512,1408]{1,0:T(8,128)(2,1)}, bf16[512,1408]{1,0:T(8,128)(2,1)}, u32[]{:S(2)}, u32[]{:S(2)}) collective-permute-start(bf16[512,1408]{1,0:T(8,128)(2,1)} %get-tuple-element.139), channel_id=1, source_target_pairs={{0,4},{4,0},{8,12},{12,8},{1,5},{5,1},{9,13},{13,9},{2,6},{6,2},{1... | collective-permute-start | bytes 4325384 | tf_op jit(solution)/shard_map/ppermute | solution.py:35
  123.6 38.7 %collective-permute-start.13 = (bf16[512,1408]{1,0:T(8,128)(2,1)}, bf16[512,1408]{1,0:T(8,128)(2,1)}, u32[]{:S(2)}, u32[]{:S(2)}) collective-permute-start(bf16[512,1408]{1,0:T(8,128)(2,1)} %add_convert_fusion), channel_id=1, source_target_pairs={{0,8},{4,12},{8,0},{12,4},{1,9},{5,13},{9,1},{13,5},{2,10},{6,14},... | collective-permute-start | bytes 4325384 | tf_op jit(solution)/shard_map/ppermute | solution.py:35
  146.1 34.7 %collective-permute-start.14 = (bf16[512,1408]{1,0:T(8,128)(2,1)}, bf16[512,1408]{1,0:T(8,128)(2,1)S(1)}, u32[]{:S(2)}, u32[]{:S(2)}) collective-permute-start(bf16[512,1408]{1,0:T(8,128)(2,1)} %branch_far.1), channel_id=1, source_target_pairs={{0,1},{1,0},{2,3},{3,2},{4,5},{5,4},{6,7},{7,6},{8,9},{9,8},{10,11... | collective-permute-start | bytes 4325384 | tf_op jit(solution)/shard_map/ppermute | solution.py:35
  185.4 33.2 %collective-permute-start.15 = (bf16[512,1408]{1,0:T(8,128)(2,1)S(1)}, bf16[512,1408]{1,0:T(8,128)(2,1)}, u32[]{:S(2)}, u32[]{:S(2)}) collective-permute-start(bf16[512,1408]{1,0:T(8,128)(2,1)S(1)} %multiply_convert_fusion.go), channel_id=1, source_target_pairs={{0,1},{1,0},{2,3},{3,2},{4,5},{5,4},{6,7},{7,6},{8,9},{9,8},{10,11... | collective-permute-start | bytes 4325384 | tf_op jit(solution)/shard_map/ppermute | solution.py:35
  227.3 13.5 %collective-permute-start.20 = (bf16[352,1536]{1,0:T(8,128)(2,1)S(1)}, bf16[352,1536]{1,0:T(8,128)(2,1)S(1)}, u32[]{:S(2)}, u32[]{:S(2)}) collective-permute-start(bf16[352,1536]{1,0:T(8,128)(2,1)S(1)} %get-tuple-element.175), channel_id=1, source_target_pairs={{0,4},{4,0},{8,12},{12,8},{1,5},{5,1},{9,13},{13,9},{2,6},{6,2},{1... | collective-permute-start | bytes 3244040 | tf_op jit(solution)/shard_map/ppermute | solution.py:35
  230.1 11.2 %collective-permute-start.19 = (bf16[128,1536]{1,0:T(8,128)(2,1)S(1)}, bf16[128,1536]{1,0:T(8,128)(2,1)S(1)}, u32[]{:S(2)}, u32[]{:S(2)}) collective-permute-start(bf16[128,1536]{1,0:T(8,128)(2,1)S(1)} %add_convert_fusion.9), channel_id=1, source_target_pairs={{0,8},{4,12},{8,0},{12,4},{1,9},{5,13},{9,1},{13,5},{2,10},{6,14},... | collective-permute-start | bytes 1179656 | tf_op jit(solution)/shard_map/ppermute | solution.py:35
  241.4 21.6 %collective-permute-start.22 = (bf16[352,1536]{1,0:T(8,128)(2,1)S(1)}, bf16[352,1536]{1,0:T(8,128)(2,1)S(1)}, u32[]{:S(2)}, u32[]{:S(2)}) collective-permute-start(bf16[352,1536]{1,0:T(8,128)(2,1)S(1)} %get-tuple-element.185), channel_id=1, source_target_pairs={{0,4},{4,0},{8,12},{12,8},{1,5},{5,1},{9,13},{13,9},{2,6},{6,2},{1... | collective-permute-start | bytes 3244040 | tf_op jit(solution)/shard_map/ppermute | solution.py:35
  241.5 21.5 %collective-permute-start.23 = (bf16[352,1536]{1,0:T(8,128)(2,1)S(1)}, bf16[352,1536]{1,0:T(8,128)(2,1)S(1)}, u32[]{:S(2)}, u32[]{:S(2)}) collective-permute-start(bf16[352,1536]{1,0:T(8,128)(2,1)S(1)} %get-tuple-element.187), channel_id=1, source_target_pairs={{0,4},{4,0},{8,12},{12,8},{1,5},{5,1},{9,13},{13,9},{2,6},{6,2},{1... | collective-permute-start | bytes 3244040 | tf_op jit(solution)/shard_map/ppermute | solution.py:35
  242.0 18.7 %collective-permute-start.21 = (bf16[224,1536]{1,0:T(8,128)(2,1)S(1)}, bf16[224,1536]{1,0:T(8,128)(2,1)S(1)}, u32[]{:S(2)}, u32[]{:S(2)}) collective-permute-start(bf16[224,1536]{1,0:T(8,128)(2,1)S(1)} %add_convert_fusion.6), channel_id=1, source_target_pairs={{0,8},{4,12},{8,0},{12,4},{1,9},{5,13},{9,1},{13,5},{2,10},{6,14},... | collective-permute-start | bytes 2064392 | tf_op jit(solution)/shard_map/ppermute | solution.py:35
  242.9 20.1 %collective-permute-start.24 = (bf16[128,1536]{1,0:T(8,128)(2,1)S(1)}, bf16[128,1536]{1,0:T(8,128)(2,1)S(1)}, u32[]{:S(2)}, u32[]{:S(2)}) collective-permute-start(bf16[128,1536]{1,0:T(8,128)(2,1)S(1)} %add_convert_fusion.8), channel_id=1, source_target_pairs={{0,2},{1,3},{2,0},{3,1},{4,6},{5,7},{6,4},{7,5},{8,10},{9,11},{10,... | collective-permute-start | bytes 1179656 | tf_op jit(solution)/shard_map/ppermute | solution.py:35
  263.1 10.9 %collective-permute-start.25 = (bf16[352,1536]{1,0:T(8,128)(2,1)S(1)}, bf16[352,1536]{1,0:T(8,128)(2,1)S(1)}, u32[]{:S(2)}, u32[]{:S(2)}) collective-permute-start(bf16[352,1536]{1,0:T(8,128)(2,1)S(1)} %get-tuple-element.188), channel_id=1, source_target_pairs={{0,4},{4,0},{8,12},{12,8},{1,5},{5,1},{9,13},{13,9},{2,6},{6,2},{1... | collective-permute-start | bytes 3244040 | tf_op jit(solution)/shard_map/ppermute | solution.py:35
  263.1 10.8 %collective-permute-start.26 = (bf16[352,1536]{1,0:T(8,128)(2,1)S(1)}, bf16[352,1536]{1,0:T(8,128)(2,1)S(1)}, u32[]{:S(2)}, u32[]{:S(2)}) collective-permute-start(bf16[352,1536]{1,0:T(8,128)(2,1)S(1)} %get-tuple-element.189), channel_id=1, source_target_pairs={{0,4},{4,0},{8,12},{12,8},{1,5},{5,1},{9,13},{13,9},{2,6},{6,2},{1... | collective-permute-start | bytes 3244040 | tf_op jit(solution)/shard_map/ppermute | solution.py:35
  274.2 26.9 %collective-permute-start.29 = (bf16[352,1536]{1,0:T(8,128)(2,1)S(1)}, bf16[352,1536]{1,0:T(8,128)(2,1)S(1)}, u32[]{:S(2)}, u32[]{:S(2)}) collective-permute-start(bf16[352,1536]{1,0:T(8,128)(2,1)S(1)} %add_convert_fusion.2), channel_id=1, source_target_pairs={{0,8},{4,12},{8,0},{12,4},{1,9},{5,13},{9,1},{13,5},{2,10},{6,14},... | collective-permute-start | bytes 3244040 | tf_op jit(solution)/shard_map/ppermute | solution.py:35
  275.5 25.3 %collective-permute-start.30 = (bf16[176,1536]{1,0:T(8,128)(2,1)S(1)}, bf16[176,1536]{1,0:T(8,128)(2,1)S(1)}, u32[]{:S(2)}, u32[]{:S(2)}) collective-permute-start(bf16[176,1536]{1,0:T(8,128)(2,1)S(1)} %slice.84), channel_id=1, source_target_pairs={{0,2},{1,3},{2,0},{3,1},{4,6},{5,7},{6,4},{7,5},{8,10},{9,11},{10,... | collective-permute-start | bytes 1622024 | tf_op jit(solution)/shard_map/ppermute | solution.py:35
  275.6 46.9 %collective-permute-start.33 = (bf16[352,1536]{1,0:T(8,128)(2,1)S(1)}, bf16[352,1536]{1,0:T(8,128)(2,1)S(1)}, u32[]{:S(2)}, u32[]{:S(2)}) collective-permute-start(bf16[352,1536]{1,0:T(8,128)(2,1)S(1)} %add_convert_fusion.3), channel_id=1, source_target_pairs={{0,8},{4,12},{8,0},{12,4},{1,9},{5,13},{9,1},{13,5},{2,10},{6,14},... | collective-permute-start | bytes 3244040 | tf_op jit(solution)/shard_map/ppermute | solution.py:35
  301.6 20.9 %collective-permute-start.31 = (bf16[352,1536]{1,0:T(8,128)(2,1)S(1)}, bf16[352,1536]{1,0:T(8,128)(2,1)S(1)}, u32[]{:S(2)}, u32[]{:S(2)}) collective-permute-start(bf16[352,1536]{1,0:T(8,128)(2,1)S(1)} %get-tuple-element.208), channel_id=1, source_target_pairs={{0,4},{4,0},{8,12},{12,8},{1,5},{5,1},{9,13},{13,9},{2,6},{6,2},{1... | collective-permute-start | bytes 3244040 | tf_op jit(solution)/shard_map/ppermute | solution.py:35
  301.7 20.8 %collective-permute-start.32 = (bf16[352,1536]{1,0:T(8,128)(2,1)S(1)}, bf16[352,1536]{1,0:T(8,128)(2,1)S(1)}, u32[]{:S(2)}, u32[]{:S(2)}) collective-permute-start(bf16[352,1536]{1,0:T(8,128)(2,1)S(1)} %get-tuple-element.210), channel_id=1, source_target_pairs={{0,4},{4,0},{8,12},{12,8},{1,5},{5,1},{9,13},{13,9},{2,6},{6,2},{1... | collective-permute-start | bytes 3244040 | tf_op jit(solution)/shard_map/ppermute | solution.py:35
  302.2 20.3 %collective-permute-start.34 = (bf16[128,1536]{1,0:T(8,128)(2,1)S(1)}, bf16[128,1536]{1,0:T(8,128)(2,1)S(1)}, u32[]{:S(2)}, u32[]{:S(2)}) collective-permute-start(bf16[128,1536]{1,0:T(8,128)(2,1)S(1)} %add_convert_fusion.7), channel_id=1, source_target_pairs={{0,2},{1,3},{2,0},{3,1},{4,6},{5,7},{6,4},{7,5},{8,10},{9,11},{10,... | collective-permute-start | bytes 1179656 | tf_op jit(solution)/shard_map/ppermute | solution.py:35
  302.2 20.3 %collective-permute-start.35 = (f32[8,128]{1,0:T(8,128)S(1)}, f32[8,128]{1,0:T(8,128)S(1)}, u32[]{:S(2)}, u32[]{:S(2)}) collective-permute-start(f32[8,128]{1,0:T(8,128)S(1)} %add.161), channel_id=1, source_target_pairs={{0,2},{1,3},{2,0},{3,1},{4,6},{5,7},{6,4},{7,5},{8,10},{9,11},{10,... | collective-permute-start | bytes 12296 | tf_op jit(solution)/shard_map/ppermute | solution.py:35
  322.8 32.8 %collective-permute-start.36 = (bf16[352,1536]{1,0:T(8,128)(2,1)S(1)}, bf16[352,1536]{1,0:T(8,128)(2,1)S(1)}, u32[]{:S(2)}, u32[]{:S(2)}) collective-permute-start(bf16[352,1536]{1,0:T(8,128)(2,1)S(1)} %add_convert_fusion.1), channel_id=1, source_target_pairs={{0,8},{4,12},{8,0},{12,4},{1,9},{5,13},{9,1},{13,5},{2,10},{6,14},... | collective-permute-start | bytes 3244040 | tf_op jit(solution)/shard_map/ppermute | solution.py:35
  324.0 31.5 %collective-permute-start.37 = (bf16[224,1536]{1,0:T(8,128)(2,1)S(1)}, bf16[224,1536]{1,0:T(8,128)(2,1)S(1)}, u32[]{:S(2)}, u32[]{:S(2)}) collective-permute-start(bf16[224,1536]{1,0:T(8,128)(2,1)S(1)} %add_convert_fusion.4), channel_id=1, source_target_pairs={{0,2},{1,3},{2,0},{3,1},{4,6},{5,7},{6,4},{7,5},{8,10},{9,11},{10,... | collective-permute-start | bytes 2064392 | tf_op jit(solution)/shard_map/ppermute | solution.py:35
  (36 other events, 322.9 us)
Sparse Core Ops, SparseCore 0:
  10.4 62.7 all-gather.1

commit v7 on v6

--- a/solution.py
+++ b/solution.py
@@ -570,7 +570,7 @@
 
     o0, o1, o2, o3 = grad_out_part(mx1, grad_own, grad_pair, act_far, True)
     got2, got0 = swap(o3, "mx", 1), swap(o1, "mx", 1)
-    early = rows // 48 * 16 + 16
+    early = rows // 48 * 16
     h0, h1 = slice(0, early), slice(early, rows)
     s2_out = [(o2[c].astype(F32) + got2[c].astype(F32)).astype(BF16) for c in (h0, h1)]
     x_out = [swap(v, "mx", 2) for v in s2_out]
@@ -590,7 +590,7 @@
         i0, i1, i2, i3, x_out[1], gn2, gn0, f_out0
     )
     f1 = last(o0[h1], got0[h1], x_out1)
-    f_out1, f_out2 = (swap(f1[c], "my", 2) for c in (slice(0, 48), slice(48, None)))
+    f_out1, f_out2 = (swap(f1[c], "my", 2) for c in (slice(0, 64), slice(64, None)))
     gin2, gin0 = swap(i3, "mx", 1), swap(i1, "mx", 1)
     loss_z = swap(after(loss, f1), "my", 1)
     s2_on = (n2.astype(F32) + gn2.astype(F32)).astype(BF16)

time: 366 us -> 367 us (level)
  transfers between devices with their start and end apart: 39 -> 39, of which waited for: 18 -> 17; matrix products, arithmetic and copies ran while one was open for 9% -> 9% of each run, Pallas kernels for 32% -> 32%
where the time goes in v7:
time: 367 us; the launch traced here: 366 us
  waiting for transfers between devices  128 us (35%)
  Pallas kernels  125 us (34%)
  starting transfers between devices  33.3 us (9%)
  other arithmetic  31.6 us (9%)
  local copies, waits for them, and re-layouts  19.2 us (5%)
  between operations  16.2 us (4%)
  blocking collectives  12.3 us (3%)
    ppermute x38, waiting for transfers between devices, swap(): return lax.ppermute(value, axis, [(i, i ^ bit) for i in range(count)])  128 us
    ppermute x38, starting transfers between devices, swap(): return lax.ppermute(value, axis, [(i, i ^ bit) for i in range(count)])  33.3 us
    pallas_call x2, Pallas kernels, grad_in_part(): pl.pallas_call(body, grid=(cols // FC,), in_specs=[pl.BlockSpec(memory_sp...  27.3 us
    pallas_call x1, Pallas kernels, target_parts(): pl.pallas_call(body, grid_spec=pltpu.PrefetchScalarGridSpec(num_scalar_pr...  18.4 us
    pallas_call x2, Pallas kernels, grad_out_part(): pl.pallas_call(body, grid=(cols // FC,), in_specs=[pl.BlockSpec(memory_sp...  17.3 us
    add x2, other arithmetic, gelu_slope(): 0.5 * (1.0 + lax.erf(value * 0.7071067811865476))  12.6 us
    psum x1, blocking collectives, pair_shards(): sums = lax.psum(sums[:2], 'mx')  12.3 us
    pallas_call x1, Pallas kernels, forward_pieces(): pl.pallas_call(body, grid=(cols // FC,), in_specs=[pl.BlockSpec(memory_sp...  11.9 us
  transfers between devices with their start and end apart: 39, of which 17 were waited for; matrix products, arithmetic and copies ran while one was open for 9% of the time, Pallas kernels for 32%

profile of v7, /device:TPU:0, one launch (start us, length us, event | category | flops | bytes accessed | tf_op | source)
XLA Modules:
  0.0 366.0 jit_solution(16712932462266729003)
XLA Ops:
  7.2 3.0 pad_maximum_fusion.1
  16.1 3.0 collective-permute-start.1
  19.2 2.6 collective-permute-start
  21.8 5.6 %teacher_sums.1 = f32[8,2048]{1,0:T(8,128)} custom-call(bf16[2048,1536]{1,0:T(8,128)(2,1)} %bitcast.38), custom_call_target="tpu_custom_call" | custom-call | flops 1000 | bytes 1000 | tf_op jit(solution)/shard_map/teacher_sums/pallas_call | solution.py:102
  29.4 12.3 %psum.7.s_ref = f32[2,2048]{1,0:T(2,128)} all-reduce(f32[2,2048]{1,0:T(2,128)S(1)} %slice.80), channel_id=1, replica_groups=mesh['group'=2,'mx'=4,'my'=4] {'mx'}, use_global_device_ids=true, to_apply=%region_0.0 | all-reduce | flops 4096 | bytes 32768 | tf_op jit(solution)/shard_map/psum | solution.py:509
  41.8 18.4 %targets.1 = (bf16[512,1408]{1,0:T(8,128)(2,1)}, bf16[512,1408]{1,0:T(8,128)(2,1)}, bf16[512,1408]{1,0:T(8,128)(2,1)}, bf16[512,1408]{1,0:T(8,128)(2,1)}) custom-call(s32[1]{0:T(128)} %bitcast.2.mx_ref, bf16[2048,1536]{1,0:T(8,128)(2,1)} %bitcast.39, f32[2,2048]{1,0:T(2,128)} %psum.7.s_ref, f32[1,1536]{1,0:T(1,128)} %reshape.43.g_ref, ...), custom_call_target="tpu_custom_call" | custom-call | flops 1000 | bytes 1000 | tf_op jit(solution)/shard_map/targets/pallas_call | solution.py:137
  60.2 13.3 %collective-permute-done.refs_0_ = bf16[352,1536]{1,0:T(8,128)(2,1)} collective-permute-done((bf16[352,1536]{1,0:T(8,128)(2,1)}, bf16[352,1536]{1,0:T(8,128)(2,1)}, u32[]{:S(2)}, u32[]{:S(2)}) %collective-permute-start) | collective-permute-done | bytes 1081376 | tf_op jit(solution)/shard_map/ppermute | solution.py:35
  77.9 2.5 copy.12.np_
  80.5 10.8 %forward.1 = (f32[1024,1536]{1,0:T(8,128)}, bf16[1024,1536]{1,0:T(8,128)(2,1)}) custom-call(bf16[512,1408]{1,0:T(8,128)(2,1)} %copy-done, bf16[512,1408]{1,0:T(8,128)(2,1)} %copy.12.np_, bf16[4,2,352,1536]{3,2,1,0:T(8,128)(2,1)} %bitcast.30), custom_call_target="tpu_custom_call" | custom-call | flops 1000 | bytes 1000 | tf_op jit(solution)/shard_map/forward/pallas_call | solution.py:199
  91.3 11.1 %branch_near.1.nr = f32[1024,1408]{1,0:T(8,128)} custom-call(bf16[1024,1536]{1,0:T(8,128)(2,1)} %get-tuple-element.170.a, bf16[4,2,352,1536]{3,2,1,0:T(8,128)(2,1)} %bitcast.31), custom_call_target="tpu_custom_call" | custom-call | flops 1000 | bytes 1000 | tf_op jit(solution)/shard_map/branch_near/pallas_call | solution.py:328
  105.9 2.8 add_convert_fusion
  108.8 9.7 %collective-permute-done.6.refs_6_ = bf16[176,1536]{1,0:T(8,128)(2,1)S(1)} collective-permute-done((bf16[176,1536]{1,0:T(8,128)(2,1)S(1)}, bf16[176,1536]{1,0:T(8,128)(2,1)S(1)}, u32[]{:S(2)}, u32[]{:S(2)}) %collective-permute-start.6) | collective-permute-done | bytes 540704 | tf_op jit(solution)/shard_map/ppermute | solution.py:35
  125.5 11.9 %forward_far.1 = (f32[1024,1536]{1,0:T(8,128)}, bf16[1024,1536]{1,0:T(8,128)(2,1)}) custom-call(s32[8]{0:T(128)} %stack.71.offs_ref, bf16[512,1408]{1,0:T(8,128)(2,1)} %copy-done, bf16[512,1408]{1,0:T(8,128)(2,1)} %copy.12.np_, bf16[352,1536]{1,0:T(8,128)(2,1)} %collective-permute-done.refs_0_, bf16[352,1536]{1,0:T(8,128)(2,1)} %collective-permute-done.4.refs_1_, ...), custom_call_target="tpu_custom_call" | custom-call | flops 1000 | bytes 1000 | tf_op jit(solution)/shard_map/forward_far/pallas_call | solution.py:238
  137.4 8.7 %branch_far.1 = bf16[512,1408]{1,0:T(8,128)(2,1)} custom-call(s32[8]{0:T(128)} %stack.71.offs_ref, f32[1024,1408]{1,0:T(8,128)} %branch_near.1.nr, bf16[1024,1536]{1,0:T(8,128)(2,1)} %get-tuple-element.140.a, bf16[352,1536]{1,0:T(8,128)(2,1)} %collective-permute-done.refs_0_, bf16[352,1536]{1,0:T(8,128)(2,1)} %collective-permute-done.4.refs_1_, ...), custom_call_target="tpu_custom_call" | custom-call | flops 1000 | bytes 1000 | tf_op jit(solution)/shard_map/branch_far/pallas_call | solution.py:281
  146.1 2.7 collective-permute-start.14
  149.3 5.0 %assemble.1.w = bf16[1408,1536]{1,0:T(8,128)(2,1)} custom-call(s32[8]{0:T(128)} %stack.80.offs_ref, bf16[352,1536]{1,0:T(8,128)(2,1)} %collective-permute-done.refs_0_, bf16[352,1536]{1,0:T(8,128)(2,1)} %collective-permute-done.4.refs_1_, bf16[352,1536]{1,0:T(8,128)(2,1)} %copy-done.7, bf16[352,1536]{1,0:T(8,128)(2,1)} %copy-done.9, ...), custom_call_target="tpu_custom_call" | custom-call | flops 1000 | bytes 1000 | tf_op jit(solution)/shard_map/assemble/pallas_call | solution.py:68
  154.3 8.0 %branch.1 = f32[512,1408]{1,0:T(8,128)} custom-call(f32[1024,1408]{1,0:T(8,128)} %branch_near.1.nr, bf16[1024,1536]{1,0:T(8,128)(2,1)} %get-tuple-element.140.a, bf16[1408,1536]{1,0:T(8,128)(2,1)} %assemble.1.w), custom_call_target="tpu_custom_call" | custom-call | flops 1000 | bytes 1000 | tf_op jit(solution)/shard_map/branch/pallas_call | solution.py:362
  162.3 8.5 %fusion.3.sl = f32[1024,1536]{1,0:T(8,128)} fusion(f32[1024,1536]{1,0:T(8,128)} %get-tuple-element.154), kind=kLoop, calls=%fused_computation.5 | loop fusion | flops 12582912 | bytes 12582912 | tf_op jit(solution)/shard_map/add | solution.py:28
  170.8 9.9 %collective-permute-done.14 = bf16[512,1408]{1,0:T(8,128)(2,1)S(1)} collective-permute-done((bf16[512,1408]{1,0:T(8,128)(2,1)}, bf16[512,1408]{1,0:T(8,128)(2,1)S(1)}, u32[]{:S(2)}, u32[]{:S(2)}) %collective-permute-start.14) | collective-permute-done | bytes 1441824 | tf_op jit(solution)/shard_map/ppermute | solution.py:35
  180.8 3.7 %multiply_reduce_fusion = (f32[]{:T(128)}, f32[512,1408]{1,0:T(8,128)S(1)}) fusion(bf16[512,1408]{1,0:T(8,128)(2,1)} %collective-permute-done.13, bf16[512,1408]{1,0:T(8,128)(2,1)} %collective-permute-done.12, bf16[512,1408]{1,0:T(8,128)(2,1)S(1)} %copy-done.15, f32[512,1408]{1,0:T(8,128)S(1)} %copy-done.8, ...), kind=kLoop, calls=%fused_computation.11 | loop fusion | flops 8650751 | bytes 12976132 | tf_op jit(solution)/shard_map/reduce_sum | solution.py:562
  187.2 4.1 %fusion.7.sl = f32[1024,1536]{1,0:T(8,128)} fusion(f32[1024,1536]{1,0:T(8,128)S(1)} %bitcast.41), kind=kLoop, calls=%fused_computation.9 | loop fusion | flops 12582912 | bytes 12582912 | tf_op jit(solution)/shard_map/add | solution.py:28
  196.5 22.1 %collective-permute-done.15.gp = bf16[512,1408]{1,0:T(8,128)(2,1)} collective-permute-done((bf16[512,1408]{1,0:T(8,128)(2,1)S(1)}, bf16[512,1408]{1,0:T(8,128)(2,1)}, u32[]{:S(2)}, u32[]{:S(2)}) %collective-permute-start.15) | collective-permute-done | bytes 1441824 | tf_op jit(solution)/shard_map/ppermute | solution.py:35
  218.6 8.7 %grad_out.2 = (bf16[352,1536]{1,0:T(8,128)(2,1)S(1)}, bf16[352,1536]{1,0:T(8,128)(2,1)S(1)}, bf16[352,1536]{1,0:T(8,128)(2,1)S(1)}, bf16[352,1536]{1,0:T(8,128)(2,1)S(1)}) custom-call(s32[1]{0:T(128)} %bitcast.2.mx_ref, bf16[512,1408]{1,0:T(8,128)(2,1)S(1)} %multiply_convert_fusion.go, bf16[512,1408]{1,0:T(8,128)(2,1)} %collective-permute-done.15.gp, ...), custom_call_target="tpu_custom_call" | custom-call | flops 1000 | bytes 1000 | tf_op jit(solution)/shard_map/grad_out/pallas_call | solution.py:413
  232.0 8.6 %grad_out.3 = (bf16[352,1536]{1,0:T(8,128)(2,1)S(1)}, bf16[352,1536]{1,0:T(8,128)(2,1)S(1)}, bf16[352,1536]{1,0:T(8,128)(2,1)S(1)}, bf16[352,1536]{1,0:T(8,128)(2,1)S(1)}) custom-call(s32[1]{0:T(128)} %bitcast.2.mx_ref, bf16[512,1408]{1,0:T(8,128)(2,1)S(1)} %multiply_convert_fusion.go, bf16[512,1408]{1,0:T(8,128)(2,1)} %collective-permute-done.15.gp, ...), custom_call_target="tpu_custom_call" | custom-call | flops 1000 | bytes 1000 | tf_op jit(solution)/shard_map/grad_out/pallas_call | solution.py:413
  243.5 2.8 copy-done.3
  246.3 13.7 %grad_in.2 = (bf16[352,1536]{1,0:T(8,128)(2,1)S(1)}, bf16[352,1536]{1,0:T(8,128)(2,1)S(1)}, bf16[352,1536]{1,0:T(8,128)(2,1)S(1)}, bf16[352,1536]{1,0:T(8,128)(2,1)S(1)}) custom-call(s32[1]{0:T(128)} %bitcast.2.mx_ref, bf16[512,1408]{1,0:T(8,128)(2,1)S(1)} %multiply_convert_fusion.go, bf16[512,1408]{1,0:T(8,128)(2,1)} %collective-permute-done.15.gp, ...), custom_call_target="tpu_custom_call" | custom-call | flops 1000 | bytes 1000 | tf_op jit(solution)/shard_map/grad_in/pallas_call | solution.py:444
  264.9 9.5 %collective-permute-done.28 = bf16[64,1536]{1,0:T(8,128)(2,1)S(1)} collective-permute-done((bf16[64,1536]{1,0:T(8,128)(2,1)S(1)}, bf16[64,1536]{1,0:T(8,128)(2,1)S(1)}, u32[]{:S(2)}, u32[]{:S(2)}) %collective-permute-start.28) | collective-permute-done | bytes 196640 | tf_op jit(solution)/shard_map/ppermute | solution.py:35
  277.0 13.6 %grad_in.3 = (bf16[352,1536]{1,0:T(8,128)(2,1)S(1)}, bf16[352,1536]{1,0:T(8,128)(2,1)S(1)}, bf16[352,1536]{1,0:T(8,128)(2,1)S(1)}, bf16[352,1536]{1,0:T(8,128)(2,1)S(1)}) custom-call(s32[1]{0:T(128)} %bitcast.2.mx_ref, bf16[512,1408]{1,0:T(8,128)(2,1)S(1)} %multiply_convert_fusion.go, bf16[512,1408]{1,0:T(8,128)(2,1)} %collective-permute-done.15.gp, ...), custom_call_target="tpu_custom_call" | custom-call | flops 1000 | bytes 1000 | tf_op jit(solution)/shard_map/grad_in/pallas_call | solution.py:444
  290.6 9.7 %collective-permute-done.30 = bf16[176,1536]{1,0:T(8,128)(2,1)S(1)} collective-permute-done((bf16[176,1536]{1,0:T(8,128)(2,1)S(1)}, bf16[176,1536]{1,0:T(8,128)(2,1)S(1)}, u32[]{:S(2)}, u32[]{:S(2)}) %collective-permute-start.30) | collective-permute-done | bytes 540704 | tf_op jit(solution)/shard_map/ppermute | solution.py:35
  302.5 2.9 collective-permute-start.35
  305.5 18.2 %collective-permute-done.33 = bf16[352,1536]{1,0:T(8,128)(2,1)S(1)} collective-permute-done((bf16[352,1536]{1,0:T(8,128)(2,1)S(1)}, bf16[352,1536]{1,0:T(8,128)(2,1)S(1)}, u32[]{:S(2)}, u32[]{:S(2)}) %collective-permute-start.33) | collective-permute-done | bytes 1081376 | tf_op jit(solution)/shard_map/ppermute | solution.py:35
  328.3 27.9 %collective-permute-done.37 = bf16[240,1536]{1,0:T(8,128)(2,1)S(1)} collective-permute-done((bf16[240,1536]{1,0:T(8,128)(2,1)S(1)}, bf16[240,1536]{1,0:T(8,128)(2,1)S(1)}, u32[]{:S(2)}, u32[]{:S(2)}) %collective-permute-start.37) | collective-permute-done | bytes 737312 | tf_op jit(solution)/shard_map/ppermute | solution.py:35
  (162 shorter events, 54.2 us)
Async XLA Ops:
  7.2 73.3 %all-gather.2.cloned.1.call-start = ((), (), s32[]{:S(2)}) async-start(), calls=%async_computation | async-start | bytes 10813440 | tf_op jit(solution)/shard_map/all_gather | solution.py:501
  16.1 58.1 %collective-permute-start.1 = (bf16[512,1408]{0,1:T(8,128)(2,1)}, bf16[512,1408]{0,1:T(8,128)(2,1)}, u32[]{:S(2)}, u32[]{:S(2)}) collective-permute-start(bf16[512,1408]{0,1:T(8,128)(2,1)} %copy.11), channel_id=1, source_target_pairs={{0,1},{1,0},{2,3},{3,2},{4,5},{5,4},{6,7},{7,6},{8,9},{9,8},{10,11... | collective-permute-start | bytes 4325384 | tf_op jit(solution)/shard_map/ppermute | solution.py:35
  19.2 54.3 %collective-permute-start = (bf16[352,1536]{1,0:T(8,128)(2,1)}, bf16[352,1536]{1,0:T(8,128)(2,1)}, u32[]{:S(2)}, u32[]{:S(2)}) collective-permute-start(bf16[352,1536]{1,0:T(8,128)(2,1)} %pad_maximum_fusion.2), channel_id=1, source_target_pairs={{0,2},{1,3},{2,0},{3,1},{4,6},{5,7},{6,4},{7,5},{8,10},{9,11},{10,... | collective-permute-start | bytes 3244040 | tf_op jit(solution)/shard_map/ppermute | solution.py:35
  74.2 28.2 %collective-permute-start.5 = (bf16[512,1408]{1,0:T(8,128)(2,1)}, bf16[512,1408]{1,0:T(8,128)(2,1)}, u32[]{:S(2)}, u32[]{:S(2)}) collective-permute-start(bf16[512,1408]{1,0:T(8,128)(2,1)} %get-tuple-element.124), channel_id=1, source_target_pairs={{0,4},{4,0},{8,12},{12,8},{1,5},{5,1},{9,13},{13,9},{2,6},{6,2},{1... | collective-permute-start | bytes 4325384 | tf_op jit(solution)/shard_map/ppermute | solution.py:35
  74.2 28.2 %collective-permute-start.4 = (bf16[352,1536]{1,0:T(8,128)(2,1)}, bf16[352,1536]{1,0:T(8,128)(2,1)}, u32[]{:S(2)}, u32[]{:S(2)}) collective-permute-start(bf16[352,1536]{1,0:T(8,128)(2,1)} %collective-permute-done.refs_0_), channel_id=1, source_target_pairs={{0,4},{4,0},{8,12},{12,8},{1,5},{5,1},{9,13},{13,9},{2,6},{6,2},{1... | collective-permute-start | bytes 3244040 | tf_op jit(solution)/shard_map/ppermute | solution.py:35
  74.7 27.7 %collective-permute-start.3 = (bf16[352,1536]{1,0:T(8,128)(2,1)}, bf16[352,1536]{1,0:T(8,128)(2,1)S(1)}, u32[]{:S(2)}, u32[]{:S(2)}) collective-permute-start(bf16[352,1536]{1,0:T(8,128)(2,1)} %collective-permute-done.refs_0_), channel_id=1, source_target_pairs={{0,16},{16,0},{1,17},{17,1},{2,18},{18,2},{3,19},{19,3},{4,20},{20... | collective-permute-start | bytes 3244040 | tf_op jit(solution)/shard_map/ppermute | solution.py:35
  76.4 26.0 %collective-permute-start.2 = (bf16[352,1536]{1,0:T(8,128)(2,1)}, bf16[352,1536]{1,0:T(8,128)(2,1)}, u32[]{:S(2)}, u32[]{:S(2)}) collective-permute-start(bf16[352,1536]{1,0:T(8,128)(2,1)} %collective-permute-done.refs_0_), channel_id=1, source_target_pairs={{0,8},{4,12},{8,0},{12,4},{1,9},{5,13},{9,1},{13,5},{2,10},{6,14},... | collective-permute-start | bytes 3244040 | tf_op jit(solution)/shard_map/ppermute | solution.py:35
  102.4 16.3 %collective-permute-start.8 = (bf16[352,1536]{1,0:T(8,128)(2,1)S(1)}, bf16[352,1536]{1,0:T(8,128)(2,1)S(1)}, u32[]{:S(2)}, u32[]{:S(2)}) collective-permute-start(bf16[352,1536]{1,0:T(8,128)(2,1)S(1)} %collective-permute-done.3.refs_2_), channel_id=1, source_target_pairs={{0,4},{4,0},{8,12},{12,8},{1,5},{5,1},{9,13},{13,9},{2,6},{6,2},{1... | collective-permute-start | bytes 3244040 | tf_op jit(solution)/shard_map/ppermute | solution.py:35
  102.5 17.3 %collective-permute-start.9 = (bf16[352,1536]{1,0:T(8,128)(2,1)}, bf16[352,1536]{1,0:T(8,128)(2,1)S(1)}, u32[]{:S(2)}, u32[]{:S(2)}) collective-permute-start(bf16[352,1536]{1,0:T(8,128)(2,1)} %collective-permute-done.2.refs_4_), channel_id=1, source_target_pairs={{0,4},{4,0},{8,12},{12,8},{1,5},{5,1},{9,13},{13,9},{2,6},{6,2},{1... | collective-permute-start | bytes 3244040 | tf_op jit(solution)/shard_map/ppermute | solution.py:35
  104.3 14.2 %collective-permute-start.6 = (bf16[176,1536]{1,0:T(8,128)(2,1)S(1)}, bf16[176,1536]{1,0:T(8,128)(2,1)S(1)}, u32[]{:S(2)}, u32[]{:S(2)}) collective-permute-start(bf16[176,1536]{1,0:T(8,128)(2,1)S(1)} %slice.61), channel_id=1, source_target_pairs={{0,16},{16,0},{1,17},{17,1},{2,18},{18,2},{3,19},{19,3},{4,20},{20... | collective-permute-start | bytes 1622024 | tf_op jit(solution)/shard_map/ppermute | solution.py:35
  104.9 13.8 %collective-permute-start.7 = (bf16[176,1536]{1,0:T(8,128)(2,1)S(1)}, bf16[176,1536]{1,0:T(8,128)(2,1)S(1)}, u32[]{:S(2)}, u32[]{:S(2)}) collective-permute-start(bf16[176,1536]{1,0:T(8,128)(2,1)S(1)} %slice.62), channel_id=1, source_target_pairs={{0,8},{4,12},{8,0},{12,4},{1,9},{5,13},{9,1},{13,5},{2,10},{6,14},... | collective-permute-start | bytes 1622024 | tf_op jit(solution)/shard_map/ppermute | solution.py:35
  123.5 13.9 %collective-permute-start.12 = (bf16[512,1408]{1,0:T(8,128)(2,1)}, bf16[512,1408]{1,0:T(8,128)(2,1)}, u32[]{:S(2)}, u32[]{:S(2)}) collective-permute-start(bf16[512,1408]{1,0:T(8,128)(2,1)} %get-tuple-element.139), channel_id=1, source_target_pairs={{0,4},{4,0},{8,12},{12,8},{1,5},{5,1},{9,13},{13,9},{2,6},{6,2},{1... | collective-permute-start | bytes 4325384 | tf_op jit(solution)/shard_map/ppermute | solution.py:35
  123.7 38.7 %collective-permute-start.13 = (bf16[512,1408]{1,0:T(8,128)(2,1)}, bf16[512,1408]{1,0:T(8,128)(2,1)}, u32[]{:S(2)}, u32[]{:S(2)}) collective-permute-start(bf16[512,1408]{1,0:T(8,128)(2,1)} %add_convert_fusion), channel_id=1, source_target_pairs={{0,8},{4,12},{8,0},{12,4},{1,9},{5,13},{9,1},{13,5},{2,10},{6,14},... | collective-permute-start | bytes 4325384 | tf_op jit(solution)/shard_map/ppermute | solution.py:35
  146.1 34.7 %collective-permute-start.14 = (bf16[512,1408]{1,0:T(8,128)(2,1)}, bf16[512,1408]{1,0:T(8,128)(2,1)S(1)}, u32[]{:S(2)}, u32[]{:S(2)}) collective-permute-start(bf16[512,1408]{1,0:T(8,128)(2,1)} %branch_far.1), channel_id=1, source_target_pairs={{0,1},{1,0},{2,3},{3,2},{4,5},{5,4},{6,7},{7,6},{8,9},{9,8},{10,11... | collective-permute-start | bytes 4325384 | tf_op jit(solution)/shard_map/ppermute | solution.py:35
  185.4 33.2 %collective-permute-start.15 = (bf16[512,1408]{1,0:T(8,128)(2,1)S(1)}, bf16[512,1408]{1,0:T(8,128)(2,1)}, u32[]{:S(2)}, u32[]{:S(2)}) collective-permute-start(bf16[512,1408]{1,0:T(8,128)(2,1)S(1)} %multiply_convert_fusion.go), channel_id=1, source_target_pairs={{0,1},{1,0},{2,3},{3,2},{4,5},{5,4},{6,7},{7,6},{8,9},{9,8},{10,11... | collective-permute-start | bytes 4325384 | tf_op jit(solution)/shard_map/ppermute | solution.py:35
  227.4 13.2 %collective-permute-start.20 = (bf16[352,1536]{1,0:T(8,128)(2,1)S(1)}, bf16[352,1536]{1,0:T(8,128)(2,1)S(1)}, u32[]{:S(2)}, u32[]{:S(2)}) collective-permute-start(bf16[352,1536]{1,0:T(8,128)(2,1)S(1)} %get-tuple-element.175), channel_id=1, source_target_pairs={{0,4},{4,0},{8,12},{12,8},{1,5},{5,1},{9,13},{13,9},{2,6},{6,2},{1... | collective-permute-start | bytes 3244040 | tf_op jit(solution)/shard_map/ppermute | solution.py:35
  240.8 19.6 %collective-permute-start.22 = (bf16[352,1536]{1,0:T(8,128)(2,1)S(1)}, bf16[352,1536]{1,0:T(8,128)(2,1)S(1)}, u32[]{:S(2)}, u32[]{:S(2)}) collective-permute-start(bf16[352,1536]{1,0:T(8,128)(2,1)S(1)} %get-tuple-element.185), channel_id=1, source_target_pairs={{0,4},{4,0},{8,12},{12,8},{1,5},{5,1},{9,13},{13,9},{2,6},{6,2},{1... | collective-permute-start | bytes 3244040 | tf_op jit(solution)/shard_map/ppermute | solution.py:35
  241.0 19.4 %collective-permute-start.23 = (bf16[352,1536]{1,0:T(8,128)(2,1)S(1)}, bf16[352,1536]{1,0:T(8,128)(2,1)S(1)}, u32[]{:S(2)}, u32[]{:S(2)}) collective-permute-start(bf16[352,1536]{1,0:T(8,128)(2,1)S(1)} %get-tuple-element.187), channel_id=1, source_target_pairs={{0,4},{4,0},{8,12},{12,8},{1,5},{5,1},{9,13},{13,9},{2,6},{6,2},{1... | collective-permute-start | bytes 3244040 | tf_op jit(solution)/shard_map/ppermute | solution.py:35
  241.3 19.0 %collective-permute-start.21 = (bf16[240,1536]{1,0:T(8,128)(2,1)S(1)}, bf16[240,1536]{1,0:T(8,128)(2,1)S(1)}, u32[]{:S(2)}, u32[]{:S(2)}) collective-permute-start(bf16[240,1536]{1,0:T(8,128)(2,1)S(1)} %add_convert_fusion.6), channel_id=1, source_target_pairs={{0,8},{4,12},{8,0},{12,4},{1,9},{5,13},{9,1},{13,5},{2,10},{6,14},... | collective-permute-start | bytes 2211848 | tf_op jit(solution)/shard_map/ppermute | solution.py:35
  242.2 18.1 %collective-permute-start.24 = (bf16[112,1536]{1,0:T(8,128)(2,1)S(1)}, bf16[112,1536]{1,0:T(8,128)(2,1)S(1)}, u32[]{:S(2)}, u32[]{:S(2)}) collective-permute-start(bf16[112,1536]{1,0:T(8,128)(2,1)S(1)} %add_convert_fusion.8), channel_id=1, source_target_pairs={{0,2},{1,3},{2,0},{3,1},{4,6},{5,7},{6,4},{7,5},{8,10},{9,11},{10,... | collective-permute-start | bytes 1032200 | tf_op jit(solution)/shard_map/ppermute | solution.py:35
  260.3 14.1 %collective-permute-start.25 = (bf16[352,1536]{1,0:T(8,128)(2,1)S(1)}, bf16[352,1536]{1,0:T(8,128)(2,1)S(1)}, u32[]{:S(2)}, u32[]{:S(2)}) collective-permute-start(bf16[352,1536]{1,0:T(8,128)(2,1)S(1)} %get-tuple-element.188), channel_id=1, source_target_pairs={{0,4},{4,0},{8,12},{12,8},{1,5},{5,1},{9,13},{13,9},{2,6},{6,2},{1... | collective-permute-start | bytes 3244040 | tf_op jit(solution)/shard_map/ppermute | solution.py:35
  260.4 14.0 %collective-permute-start.26 = (bf16[352,1536]{1,0:T(8,128)(2,1)S(1)}, bf16[352,1536]{1,0:T(8,128)(2,1)S(1)}, u32[]{:S(2)}, u32[]{:S(2)}) collective-permute-start(bf16[352,1536]{1,0:T(8,128)(2,1)S(1)} %get-tuple-element.189), channel_id=1, source_target_pairs={{0,4},{4,0},{8,12},{12,8},{1,5},{5,1},{9,13},{13,9},{2,6},{6,2},{1... | collective-permute-start | bytes 3244040 | tf_op jit(solution)/shard_map/ppermute | solution.py:35
  262.7 11.7 %collective-permute-start.28 = (bf16[64,1536]{1,0:T(8,128)(2,1)S(1)}, bf16[64,1536]{1,0:T(8,128)(2,1)S(1)}, u32[]{:S(2)}, u32[]{:S(2)}) collective-permute-start(bf16[64,1536]{1,0:T(8,128)(2,1)S(1)} %slice.83), channel_id=1, source_target_pairs={{0,2},{1,3},{2,0},{3,1},{4,6},{5,7},{6,4},{7,5},{8,10},{9,11},{10,... | collective-permute-start | bytes 589832 | tf_op jit(solution)/shard_map/ppermute | solution.py:35
  274.7 26.8 %collective-permute-start.29 = (bf16[352,1536]{1,0:T(8,128)(2,1)S(1)}, bf16[352,1536]{1,0:T(8,128)(2,1)S(1)}, u32[]{:S(2)}, u32[]{:S(2)}) collective-permute-start(bf16[352,1536]{1,0:T(8,128)(2,1)S(1)} %add_convert_fusion.2), channel_id=1, source_target_pairs={{0,8},{4,12},{8,0},{12,4},{1,9},{5,13},{9,1},{13,5},{2,10},{6,14},... | collective-permute-start | bytes 3244040 | tf_op jit(solution)/shard_map/ppermute | solution.py:35
  276.0 24.3 %collective-permute-start.30 = (bf16[176,1536]{1,0:T(8,128)(2,1)S(1)}, bf16[176,1536]{1,0:T(8,128)(2,1)S(1)}, u32[]{:S(2)}, u32[]{:S(2)}) collective-permute-start(bf16[176,1536]{1,0:T(8,128)(2,1)S(1)} %slice.84), channel_id=1, source_target_pairs={{0,2},{1,3},{2,0},{3,1},{4,6},{5,7},{6,4},{7,5},{8,10},{9,11},{10,... | collective-permute-start | bytes 1622024 | tf_op jit(solution)/shard_map/ppermute | solution.py:35
  276.0 47.7 %collective-permute-start.33 = (bf16[352,1536]{1,0:T(8,128)(2,1)S(1)}, bf16[352,1536]{1,0:T(8,128)(2,1)S(1)}, u32[]{:S(2)}, u32[]{:S(2)}) collective-permute-start(bf16[352,1536]{1,0:T(8,128)(2,1)S(1)} %add_convert_fusion.3), channel_id=1, source_target_pairs={{0,8},{4,12},{8,0},{12,4},{1,9},{5,13},{9,1},{13,5},{2,10},{6,14},... | collective-permute-start | bytes 3244040 | tf_op jit(solution)/shard_map/ppermute | solution.py:35
  301.9 21.8 %collective-permute-start.31 = (bf16[352,1536]{1,0:T(8,128)(2,1)S(1)}, bf16[352,1536]{1,0:T(8,128)(2,1)S(1)}, u32[]{:S(2)}, u32[]{:S(2)}) collective-permute-start(bf16[352,1536]{1,0:T(8,128)(2,1)S(1)} %get-tuple-element.208), channel_id=1, source_target_pairs={{0,4},{4,0},{8,12},{12,8},{1,5},{5,1},{9,13},{13,9},{2,6},{6,2},{1... | collective-permute-start | bytes 3244040 | tf_op jit(solution)/shard_map/ppermute | solution.py:35
  302.0 21.7 %collective-permute-start.32 = (bf16[352,1536]{1,0:T(8,128)(2,1)S(1)}, bf16[352,1536]{1,0:T(8,128)(2,1)S(1)}, u32[]{:S(2)}, u32[]{:S(2)}) collective-permute-start(bf16[352,1536]{1,0:T(8,128)(2,1)S(1)} %get-tuple-element.210), channel_id=1, source_target_pairs={{0,4},{4,0},{8,12},{12,8},{1,5},{5,1},{9,13},{13,9},{2,6},{6,2},{1... | collective-permute-start | bytes 3244040 | tf_op jit(solution)/shard_map/ppermute | solution.py:35
  302.5 21.2 %collective-permute-start.34 = (bf16[112,1536]{1,0:T(8,128)(2,1)S(1)}, bf16[112,1536]{1,0:T(8,128)(2,1)S(1)}, u32[]{:S(2)}, u32[]{:S(2)}) collective-permute-start(bf16[112,1536]{1,0:T(8,128)(2,1)S(1)} %add_convert_fusion.7), channel_id=1, source_target_pairs={{0,2},{1,3},{2,0},{3,1},{4,6},{5,7},{6,4},{7,5},{8,10},{9,11},{10,... | collective-permute-start | bytes 1032200 | tf_op jit(solution)/shard_map/ppermute | solution.py:35
  302.5 21.2 %collective-permute-start.35 = (f32[8,128]{1,0:T(8,128)S(1)}, f32[8,128]{1,0:T(8,128)S(1)}, u32[]{:S(2)}, u32[]{:S(2)}) collective-permute-start(f32[8,128]{1,0:T(8,128)S(1)} %add.161), channel_id=1, source_target_pairs={{0,2},{1,3},{2,0},{3,1},{4,6},{5,7},{6,4},{7,5},{8,10},{9,11},{10,... | collective-permute-start | bytes 12296 | tf_op jit(solution)/shard_map/ppermute | solution.py:35
  324.0 32.1 %collective-permute-start.36 = (bf16[352,1536]{1,0:T(8,128)(2,1)S(1)}, bf16[352,1536]{1,0:T(8,128)(2,1)S(1)}, u32[]{:S(2)}, u32[]{:S(2)}) collective-permute-start(bf16[352,1536]{1,0:T(8,128)(2,1)S(1)} %add_convert_fusion.1), channel_id=1, source_target_pairs={{0,8},{4,12},{8,0},{12,4},{1,9},{5,13},{9,1},{13,5},{2,10},{6,14},... | collective-permute-start | bytes 3244040 | tf_op jit(solution)/shard_map/ppermute | solution.py:35
  325.2 30.9 %collective-permute-start.37 = (bf16[240,1536]{1,0:T(8,128)(2,1)S(1)}, bf16[240,1536]{1,0:T(8,128)(2,1)S(1)}, u32[]{:S(2)}, u32[]{:S(2)}) collective-permute-start(bf16[240,1536]{1,0:T(8,128)(2,1)S(1)} %add_convert_fusion.4), channel_id=1, source_target_pairs={{0,2},{1,3},{2,0},{3,1},{4,6},{5,7},{6,4},{7,5},{8,10},{9,11},{10,... | collective-permute-start | bytes 2211848 | tf_op jit(solution)/shard_map/ppermute | solution.py:35
  (36 other events, 356.0 us)
Sparse Core Ops, SparseCore 0:
  10.4 62.7 all-gather.1
